TPU v7x, 256 devices: a whole 4x4x8 slice. The times are simulated.
256 devices in a mesh: ctx: 16 (over x, z_lo, core), row: 4 (over y), col: 4 (over z_hi).
Axes of the slice: x: 4, y: 4, z: 8 (z_hi: 4, z_lo: 2; z = z_hi * 2 + z_lo), core: 2. Of those that a mesh axis runs over, the one named last changes fastest.
Arguments:
- activations: bfloat16 [16384, 4096], P('ctx', 'col'), may hold values from -640 to 640
- norm_gain: float32 [4096], P('col'), may hold values from 0.1 to 1.9
- w_query: bfloat16 [4096, 4096], P(('row', 'ctx'), 'col'), may hold values from -0.09375 to 0.09375
- w_key: bfloat16 [4096, 4096], P(('row', 'ctx'), 'col'), may hold values from -0.09375 to 0.09375
- w_value: bfloat16 [4096, 4096], P(('row', 'ctx'), 'col'), may hold values from -0.09375 to 0.09375
- short_taps: float32 [3, 3, 4096], P(None, None, ('row', 'col')), may hold values from -2.5 to 2.5
- long_taps: float32 [128, 4096], P(None, ('row', 'col')), may hold values from -0.5 to 0.5
- skip_gain: float32 [4096], P(('row', 'col')), may hold values from -4 to 4
- w_out: bfloat16 [4096, 4096], P(('col', 'ctx'), 'row'), may hold values from -0.09375 to 0.09375
Outputs:
- mixer_out: bfloat16 [16384, 4096], P(('ctx', 'row'), 'col')
All inputs are finite; a program needn't handle non-finite values.
Results may differ from a plain program's by a relative error of at most 0.03.
Values may be sent and summed in bfloat16 or wider, within the bound.
No kernel may reach another device: no remote copies, remote signals or barrier semaphores. Data moves between devices by JAX's collectives and lax.ppermute only.
A program may use at most 128 MiB of HBM per device.

v0:
```python
import jax
import jax.numpy as jnp
from jax import lax
from jax.sharding import PartitionSpec as P

D = 4096
SHORT_LEN = 3
FILTER_LEN = 128


epsilon = 1e-05


def tap_matrix(kernel):
    group_size = kernel.shape[0]
    width = 3 * FILTER_LEN
    padded = jnp.concatenate(
        [
            jnp.zeros((group_size, FILTER_LEN - 1), jnp.float32),
            kernel,
            jnp.zeros((group_size, FILTER_LEN + 1), jnp.float32),
        ],
        axis=1,
    )
    tiled = jnp.tile(padded, (1, FILTER_LEN + 1))
    rows = tiled[:, : FILTER_LEN * (width + 1)].reshape(group_size, FILTER_LEN, width + 1)
    return rows[:, :, : 2 * FILTER_LEN][:, :, ::-1]


def block_filter(gate_ext, tap_vals):
    channels, length = gate_ext.shape
    blocks = length // FILTER_LEN - 1
    group_size = min(channels, 32)

    def filter_group(operands):
        signal, kernel = operands
        matrix = tap_matrix(kernel)
        pieces = signal.reshape(group_size, blocks + 1, FILTER_LEN)
        joined = jnp.concatenate([pieces[:, :-1], pieces[:, 1:]], axis=2)
        result = jnp.einsum("cbi,coi->cbo", joined, matrix, precision=lax.Precision.HIGHEST)
        return result.reshape(group_size, blocks * FILTER_LEN)

    grouped = gate_ext.reshape(channels // group_size, group_size, length)
    kernels = jnp.transpose(tap_vals).reshape(channels // group_size, group_size, FILTER_LEN)
    return lax.map(filter_group, (grouped, kernels)).reshape(channels, blocks * FILTER_LEN)


def mix_channels(stacked_in, short_part, long_part_taps, skip_part):
    as_float = stacked_in.astype(jnp.float32)
    span_len = as_float.shape[2] - (SHORT_LEN - 1)
    filtered = short_part[:, 0, :, None] * as_float[:, :, SHORT_LEN - 1 : SHORT_LEN - 1 + span_len]
    for tap_idx in range(1, SHORT_LEN):
        first_pos = SHORT_LEN - 1 - tap_idx
        filtered = (
            filtered
            + short_part[:, tap_idx, :, None] * as_float[:, :, first_pos : first_pos + span_len]
        )
    query_vals = filtered[0, :, FILTER_LEN - 1 :]
    gate_vals = filtered[1] * filtered[2]
    gate_ext = jnp.concatenate([jnp.zeros((gate_vals.shape[0], 1), jnp.float32), gate_vals], axis=1)
    long_part = block_filter(gate_ext, long_part_taps)
    mixed_vals = query_vals * (long_part + skip_part[:, None] * gate_vals[:, FILTER_LEN - 1 :])
    return mixed_vals.astype(jnp.bfloat16)


def on_device(
    activations, norm_gain, w_query, w_key, w_value, short_taps, long_taps, skip_gain, w_out
):
    as_float = activations.astype(jnp.float32)
    squares = lax.psum(jnp.sum(as_float * as_float, axis=1), "col")
    normed = (as_float * lax.rsqrt(squares / D + epsilon)[:, None] * norm_gain).astype(jnp.bfloat16)
    stacked = jnp.stack([w_query, w_key, w_value])
    partial_value = jnp.einsum(
        "snd,td->snt",
        lax.all_gather(stacked, "ctx", axis=1, tiled=True),
        normed,
        preferred_element_type=jnp.float32,
    )
    qkv_vals = lax.psum_scatter(
        partial_value.astype(jnp.bfloat16), "col", scatter_dimension=1, tiled=True
    )
    prior_len = SHORT_LEN + FILTER_LEN - 2
    spread = lax.all_to_all(qkv_vals, "ctx", split_axis=1, concat_axis=2, tiled=True)
    channels = spread.shape[1]
    offset = lax.axis_index("ctx") * channels
    prior_zeros = jnp.zeros((3, channels, prior_len), jnp.bfloat16)
    mixed_chan = mix_channels(
        jnp.concatenate([prior_zeros, spread], axis=2),
        lax.dynamic_slice_in_dim(short_taps, offset, channels, 2),
        lax.dynamic_slice_in_dim(long_taps, offset, channels, 1),
        lax.dynamic_slice_in_dim(skip_gain, offset, channels, 0),
    )
    mixed_tok = lax.all_to_all(mixed_chan, "ctx", split_axis=1, concat_axis=0, tiled=True)
    block_rows = lax.all_gather(mixed_tok, "col", axis=0, tiled=True)
    out_part = lax.dot_general(
        block_rows,
        lax.all_gather(w_out, "ctx", axis=0, tiled=True),
        (((0,), (1,)), ((), ())),
        preferred_element_type=jnp.float32,
    )
    return lax.psum_scatter(out_part.astype(jnp.bfloat16), "row", scatter_dimension=0, tiled=True)


def solution(mesh):
    in_specs = (
        P("ctx", "col"),
        P("col"),
        P(("row", "ctx"), "col"),
        P(("row", "ctx"), "col"),
        P(("row", "ctx"), "col"),
        P(None, None, ("row", "col")),
        P(None, ("row", "col")),
        P(("row", "col")),
        P(("col", "ctx"), "row"),
    )
    out_specs = P(("ctx", "row"), "col")
    return jax.shard_map(
        on_device, mesh=mesh, in_specs=in_specs, out_specs=out_specs, check_vma=False
    )
```

profile of v0, /device:TPU:1, one launch (start us, length us, event | category | flops | bytes accessed | tf_op | source)
XLA Modules:
  0.0 351.2 jit_solution(16740740798677649481)
XLA Ops:
  6.5 0.0 copy-start
  6.5 2.0 pad_maximum_fusion
  8.5 0.0 all-gather.4.cloned.1.call-update
  8.5 0.0 reduce-scatter.3.cloned.1.call-start
  8.6 2.1 fusion
  10.7 13.8 %psum.7 = f32[1024]{0:T(1024)S(1)} all-reduce(f32[1024]{0:T(1024)S(1)} %fusion), channel_id=1, replica_groups=mesh['ctx'=16,'row'=4,'col'=4] {'col'}, use_global_device_ids=true, to_apply=%region_1.0 | all-reduce | flops 1024 | bytes 8192 | tf_op jit(solution)/shard_map/psum | solution.py:70
  24.4 33.9 %all-gather.4.cloned.1.call-done = bf16[3,1024,1024]{2,1,0:T(8,128)(2,1)} async-done(((bf16[3,64,1024]{2,1,0:T(8,128)(2,1)}), bf16[3,1024,1024]{2,1,0:T(8,128)(2,1)}) %all-gather.4.cloned.1.call-update) | async-done | bytes 6291472 | tf_op jit(solution)/shard_map/all_gather | solution.py:75
  58.3 12.0 %convolution_convert_fusion = bf16[3,1024,1024]{2,1,0:T(8,128)(2,1)} fusion(bf16[3,1024,1024]{2,1,0:T(8,128)(2,1)} %all-gather.4.cloned.1.call-done, bf16[1024,1024]{1,0:T(8,128)(2,1)S(1)} %copy-done.4, f32[1024]{0:T(1024)S(1)} %copy-done.5, f32[1024]{0:T(1024)S(1)} %add_rsqrt_fusion), kind=kOutput, calls=%fused_computation.5 | convolution fusion | flops 6449790976 | bytes 14688256 | tf_op jit(solution)/shard_map/snd,td->snt/dot_general | solution.py:73
  70.3 0.0 reduce-scatter.3.cloned.1.call-update
  70.3 119.0 %reduce-scatter.3.cloned.1.call-done = bf16[3,256,1024]{2,1,0:T(8,128)(2,1)} async-done(((bf16[3,1024,1024]{2,1,0:T(8,128)(2,1)}), bf16[3,256,1024]{2,1,0:T(8,128)(2,1)}) %reduce-scatter.3.cloned.1.call-update) | async-done | bytes 1572880 | tf_op jit(solution)/shard_map/reduce_scatter | solution.py:79
  189.3 4.1 %copy.14 = bf16[3,256,1024]{2,0,1:T(4,128)(2,1)} copy(bf16[3,256,1024]{2,1,0:T(8,128)(2,1)} %reduce-scatter.3.cloned.1.call-done) | data formatting | bytes 3145728 | tf_op jit(solution)/shard_map/reduce_scatter | solution.py:79
  193.4 5.2 %all-to-all-start = ((bf16[3,256,1024]{2,0,1:T(4,128)(2,1)}), bf16[3,256,1024]{2,0,1:T(4,128)(2,1)}, u32[]{:S(2)}, u32[]{:S(2)}) async-start(bf16[3,256,1024]{2,0,1:T(4,128)(2,1)} %copy.14), calls=%async_computation.1 | async-start | bytes 4194304 | tf_op jit(solution)/shard_map/all_to_all | solution.py:83
  198.6 0.0 all-gather.8.cloned.1.call-start
  198.7 0.7 all-gather.8.cloned.1.call-update
  199.3 0.2 all-gather.6.cloned.1.call-start
  199.6 0.9 constant_dynamic-slice_fusion.1
  200.5 0.1 dynamic-slice_bitcast_fusion
  200.6 0.1 copy.16
  200.6 0.1 pad.4.clone
  200.7 0.1 maximum_maximum_fusion
  200.8 0.2 tile.14
  201.0 0.6 copy.22
  201.6 0.2 slice.68
  201.9 4.6 %reshape.37 = f32[16,128,385]{2,1,0:T(8,128)} reshape(f32[16,49280]{1,0:T(8,128)S(1)} %slice.68) | data formatting | bytes 6307840 | tf_op jit(solution)/shard_map/while/body/eval_jaxpr/reshape | solution.py:26
  206.5 1.6 slice-done
  208.1 11.6 %rev.4 = f32[16,128,256]{2,1,0:T(8,128)} reverse(f32[16,128,256]{2,1,0:T(8,128)S(1)} %slice-done), dimensions={2} | reverse | bytes 4194304 | tf_op jit(solution)/shard_map/while/body/eval_jaxpr/rev | solution.py:27
  219.7 0.1 dynamic_slice.17
  219.8 10.3 %all-to-all-done = bf16[3,256,1024]{2,0,1:T(4,128)(2,1)} async-done(((bf16[3,256,1024]{2,0,1:T(4,128)(2,1)}), bf16[3,256,1024]{2,0,1:T(4,128)(2,1)}, u32[]{:S(2)}, u32[]{:S(2)}) %all-to-all-start) | async-done | bytes 1572896 | tf_op jit(solution)/shard_map/all_to_all | solution.py:83
  230.1 2.8 copy.30
  232.8 0.8 all_to_all.30
  233.6 0.5 pad_convert_fusion
  234.1 1.8 fusion.3
  235.9 0.1 fusion.13
  236.0 1.0 copy-done.1
  237.0 1.4 concatenate.15
  238.4 2.4 reshape.36
  240.8 1.9 fusion.17
  242.7 0.3 copy-done.3
  243.0 2.1 fusion.7
  245.1 0.7 fusion.15
  245.9 14.2 %all_to_all.37 = bf16[16,16,1024]{2,0,1:T(8,128)(2,1)} all-to-all(bf16[16,16,1024]{2,0,1:T(8,128)(2,1)S(1)} %bitcast.52), channel_id=1, replica_groups=mesh['ctx'=16,'row'=4,'col'=4] {'ctx'}, dimensions={1} | all-to-all | bytes 1048576 | tf_op jit(solution)/shard_map/all_to_all | solution.py:93
  260.1 0.0 all-gather.6.cloned.1.call-update
  260.1 0.3 reduce-scatter.5.cloned.1.call-start
  260.4 0.0 all-gather.8.cloned.1.call-done
  260.4 44.7 %all-gather.6.cloned.1.call-done = bf16[1024,1024]{1,0:T(8,128)(2,1)} async-done(((bf16[256,1024]{1,0:T(8,128)(2,1)}), bf16[1024,1024]{1,0:T(8,128)(2,1)}) %all-gather.6.cloned.1.call-update) | async-done | bytes 2097168 | tf_op jit(solution)/shard_map/all_gather | solution.py:94
  305.1 5.9 %convolution_convert_fusion.1 = bf16[1024,1024]{1,0:T(8,128)(2,1)} fusion(bf16[1024,1024]{1,0:T(8,128)(2,1)} %all-gather.6.cloned.1.call-done, bf16[1024,1024]{1,0:T(8,128)(2,1)} %all-gather.8.cloned.1.call-done), kind=kOutput, calls=%fused_computation.18 | convolution fusion | flops 2148532224 | bytes 6291456 | tf_op jit(solution)/shard_map/dot_general | solution.py:95
  311.0 0.0 reduce-scatter.5.cloned.1.call-update
  311.0 33.7 %reduce-scatter.5.cloned.1.call-done = bf16[256,1024]{1,0:T(8,128)(2,1)} async-done(((bf16[1024,1024]{1,0:T(8,128)(2,1)}), bf16[256,1024]{1,0:T(8,128)(2,1)}) %reduce-scatter.5.cloned.1.call-update) | async-done | bytes 524304 | tf_op jit(solution)/shard_map/reduce_scatter | solution.py:101
  (20 shorter events, 0.1 us)
Async XLA Ops:
  6.5 193.9 %copy-start = (f32[128,256]{1,0:T(8,128)S(1)}, f32[128,256]{1,0:T(8,128)}, u32[]{:S(2)}) copy-start(f32[128,256]{1,0:T(8,128)} %param.15) | copy-start | bytes 393220
  6.5 51.8 %copy-start.4 = (bf16[1024,1024]{1,0:T(8,128)(2,1)S(1)}, bf16[1024,1024]{1,0:T(8,128)(2,1)}, u32[]{:S(2)}) copy-start(bf16[1024,1024]{1,0:T(8,128)(2,1)} %param.9) | copy-start | bytes 6291460
  6.5 51.8 %copy-start.5 = (f32[1024]{0:T(1024)S(1)}, f32[1024]{0:T(1024)}, u32[]{:S(2)}) copy-start(f32[1024]{0:T(1024)} %param.10) | copy-start | bytes 12292
  6.5 51.8 %all-gather.4.cloned.1.call-start = ((), (), s32[]{:S(2)}) async-start(), calls=%async_computation.4 | async-start | bytes 6684672 | tf_op jit(solution)/shard_map/all_gather | solution.py:75
  8.5 180.8 %reduce-scatter.3.cloned.1.call-start = ((), (), s32[]{:S(2)}) async-start(), calls=%async_computation.5 | async-start | bytes 7864320 | tf_op jit(solution)/shard_map/reduce_scatter | solution.py:79
  193.4 36.6 %all-to-all-start = ((bf16[3,256,1024]{2,0,1:T(4,128)(2,1)}), bf16[3,256,1024]{2,0,1:T(4,128)(2,1)}, u32[]{:S(2)}, u32[]{:S(2)}) async-start(bf16[3,256,1024]{2,0,1:T(4,128)(2,1)} %copy.14), calls=%async_computation.1 | async-start | bytes 4194304 | tf_op jit(solution)/shard_map/all_to_all | solution.py:83
  198.6 61.8 %all-gather.8.cloned.1.call-start = ((), (), s32[]{:S(2)}) async-start(), calls=%async_computation.7 | async-start | bytes 2228224 | tf_op jit(solution)/shard_map/all_gather | solution.py:97
  199.3 105.7 %all-gather.6.cloned.1.call-start = ((), (), s32[]{:S(2)}) async-start(), calls=%async_computation.6 | async-start | bytes 2621440 | tf_op jit(solution)/shard_map/all_gather | solution.py:94
  206.5 1.6 slice-start
  208.1 11.6 %copy-start.6 = (f32[256]{0:T(256)S(1)}, f32[256]{0:T(256)}, u32[]{:S(2)}) copy-start(f32[256]{0:T(256)} %param.16) | copy-start | bytes 3076
  236.0 1.0 copy-start.1
  240.8 2.2 copy-start.3
  243.0 2.1 copy-start.2
  260.1 84.6 %reduce-scatter.5.cloned.1.call-start = ((), (), s32[]{:S(2)}) async-start(), calls=%async_computation.8 | async-start | bytes 2621440 | tf_op jit(solution)/shard_map/reduce_scatter | solution.py:101
Sparse Core Ops, SparseCore 0:
  9.2 49.1 all-gather.3
  70.4 118.8 reduce-scatter.2
  201.3 44.9 all-gather.7
  260.2 44.8 all-gather.5
  311.2 33.5 reduce-scatter.4
where the time goes:
time: 352 us; the launch traced here: 351 us
  waiting for transfers between devices  242 us (69%)
  local copies, waits for them, and re-layouts  34.7 us (10%)
  blocking collectives  27.9 us (8%)
  matrix products  20 us (6%)
  between operations  13.3 us (4%)
  other arithmetic  7.24 us (2%)
  starting transfers between devices  5.72 us (2%)
    reduce_scatter x1, waiting for transfers between devices, on_device(): lax.psum_scatter(partial_value.astype(jnp.bfloat16), 'col', scatter_dimen...  119 us
    all_gather x1, waiting for transfers between devices, on_device(): block_rows = lax.all_gather(mixed_tok, 'col', axis=0, tiled=True)  44.7 us
    all_gather x1, waiting for transfers between devices, on_device(): lax.all_gather(stacked, 'ctx', axis=1, tiled=True)  33.9 us
    reduce_scatter x1, waiting for transfers between devices, on_device(): lax.psum_scatter(out_part.astype(jnp.bfloat16), 'row', scatter_dimension=...  33.7 us
    all_to_all x1, blocking collectives, on_device(): lax.all_to_all(mixed_chan, 'ctx', split_axis=1, concat_axis=0, tiled=True)  14.2 us
    psum x1, blocking collectives, on_device(): squares = lax.psum(jnp.sum(as_float * as_float, axis=1), 'col')  13.8 us
    dot_general x1, matrix products, on_device(): jnp.einsum('snd,td->snt', lax.all_gather(stacked, 'ctx', axis=1, tiled=Tr...  12 us
    rev x1, local copies, waits for them, and re-layouts, tap_matrix(): return rows[:, :, :2 * FILTER_LEN][:, :, ::-1]  11.6 us
  transfers between devices with their start and end apart: 6, of which 5 were waited for; matrix products, arithmetic and copies ran while one was open for 10% of the time, Pallas kernels for 0%

commit v1 on v0

v1 whole, which is shorter than its diff:
```python
import jax
import jax.numpy as jnp
from jax import lax
from jax.experimental import pallas as pl
from jax.experimental.pallas import tpu as pltpu
from jax.sharding import PartitionSpec as P

D = 4096
SHORT_LEN = 3
FILTER_LEN = 128
HALO = 144
Q = 256
CH = 256
F = 1024
epsilon = 1e-05
bf16 = jnp.bfloat16
f32 = jnp.float32


def ring(n, step):
    return [(i, (i + step) % n) for i in range(n)]


def shift(x, axis, step):
    return lax.ppermute(x, axis, ring(4, step))


def gather_ring(x, axis):
    half = x.shape[0] // 2
    before = shift(x, axis, 1)
    after = shift(x, axis, -1)
    far_lo = shift(before[:half], axis, 1)
    far_hi = shift(after[half:], axis, -1)
    return before, after, far_lo, far_hi


def project_kernel(x_ref, gain_ref, w_ref, out_ref, normed_ref):
    @pl.when(pl.program_id(0) == 0)
    def _():
        rows = 32

        @pl.loop(0, Q // rows)
        def _(i):
            at = pl.ds(pl.multiple_of(i * rows, rows), rows)
            x = x_ref[at, :].astype(f32)
            squares = jnp.sum(x * x, axis=1, keepdims=True)
            normed_ref[at, :] = (x * lax.rsqrt(squares / D + epsilon) * gain_ref[...]).astype(bf16)

    out_ref[0] = lax.dot_general(
        normed_ref[...], w_ref[0], (((1,), (1,)), ((), ())), preferred_element_type=f32
    ).astype(bf16)


def project(x, gain, w):
    return pl.pallas_call(
        project_kernel,
        grid=(3,),
        in_specs=[
            pl.BlockSpec((Q, D), lambda i: (0, 0)),
            pl.BlockSpec((1, D), lambda i: (0, 0)),
            pl.BlockSpec((1, CH, D), lambda i: (i, 0, 0)),
        ],
        out_specs=pl.BlockSpec((1, Q, CH), lambda i: (i, 0, 0)),
        out_shape=jax.ShapeDtypeStruct((3, Q, CH), bf16),
        scratch_shapes=[pltpu.VMEM((Q, D), bf16)],
        compiler_params=pltpu.CompilerParams(vmem_limit_bytes=24 << 20),
        cost_estimate=pl.CostEstimate(
            flops=2 * Q * 3 * CH * D, bytes_accessed=2 * (Q * D + 3 * CH * D), transcendentals=0
        ),
        name="project",
    )(x, gain, w)


def mix_kernel(row_ref, p0, p1, p2, p3, halo_ref, taps_ref, out_ref, qkv, gate, shifted):
    row = row_ref[0]
    qkv[:, :HALO, :] = halo_ref[...].astype(f32)
    for s, piece in enumerate((p0, p1, p2, p3)):
        start = HALO + lax.rem(row + s, 4) * Q
        for proj in range(3):
            qkv[proj, pl.ds(pl.multiple_of(start, 16), Q), :] = piece[proj].astype(f32)

    step = 64
    for lanes in (pl.ds(0, 128), pl.ds(128, 128)):

        @pl.loop(0, 1152 // step)
        def _(i):
            base = pl.multiple_of(i * step, step) + (HALO - 128)
            total = []
            for proj in (1, 2):
                window = qkv[proj, pl.ds(pl.multiple_of(base - 8, 8), step + 8), lanes]
                acc = None
                for tap in range(SHORT_LEN):
                    term = taps_ref[pl.ds(3 * proj + tap, 1), lanes] * window[8 - tap : 8 - tap + step]
                    acc = term if acc is None else acc + term
                total.append(acc)
            gate[pl.ds(pl.multiple_of(i * step, step), step), lanes] = total[0] * total[1]

        @pl.loop(0, 1144 // 88)
        def _(i):
            base = pl.multiple_of(i * 88, 8)
            window = gate[pl.ds(base, 96), lanes]
            for r in range(8):
                shifted[r, pl.ds(base + 8, 88), lanes] = window[8 - r : 96 - r]

        @pl.loop(0, 8)
        def _(i):
            base = pl.multiple_of(i * 128, 128)
            acc = taps_ref[pl.ds(137, 1), lanes] * gate[pl.ds(base + 128, 128), lanes]
            for j in range(FILTER_LEN):
                acc = acc + taps_ref[pl.ds(9 + j, 1), lanes] * shifted[
                    j % 8, pl.ds(base + 128 - 8 * (j // 8), 128), lanes
                ]
            window = qkv[0, pl.ds(base + HALO - 8, 136), lanes]
            query = None
            for tap in range(SHORT_LEN):
                term = taps_ref[pl.ds(tap, 1), lanes] * window[8 - tap : 136 - tap]
                query = term if query is None else query + term
            place = lax.rem(i // 2 - row + 4, 4) * Q + lax.rem(i, 2) * 128
            out_ref[pl.ds(pl.multiple_of(place, 128), 128), lanes] = (query * acc).astype(bf16)


def mix(row, pieces, halo, taps):
    return pl.pallas_call(
        mix_kernel,
        in_specs=[pl.BlockSpec(memory_space=pltpu.SMEM)] + [pl.BlockSpec(memory_space=pltpu.VMEM)] * 6,
        out_specs=pl.BlockSpec(memory_space=pltpu.VMEM),
        out_shape=jax.ShapeDtypeStruct((4 * Q, CH), bf16),
        scratch_shapes=[
            pltpu.VMEM((3, HALO + 4 * Q, CH), f32),
            pltpu.VMEM((1152, CH), f32),
            pltpu.VMEM((8, 1152, CH), f32),
        ],
        compiler_params=pltpu.CompilerParams(vmem_limit_bytes=32 << 20),
        cost_estimate=pl.CostEstimate(
            flops=2 * 4 * Q * CH * FILTER_LEN * 20, bytes_accessed=4 << 20, transcendentals=0
        ),
        name="mix",
    )(row, *pieces, halo, taps)


def on_device(
    activations, norm_gain, w_query, w_key, w_value, short_taps, long_taps, skip_gain, w_out
):
    row = lax.axis_index("row")
    col = lax.axis_index("col")
    order = jnp.stack([col, (col + 3) % 4, (col + 1) % 4, (col + 2) % 4])

    mine = lax.dynamic_slice_in_dim(activations, row * Q, Q, 0)
    before, after, far_lo, far_hi = gather_ring(mine, "col")

    stacked = jnp.stack([w_query, w_key, w_value]).reshape(3, 4, 16, F)

    def group(i):
        return lax.dynamic_index_in_dim(stacked, i, 1, keepdims=False)

    w_rows = jnp.concatenate(
        [
            group(order[0]),
            shift(group(order[2]), "col", 1),
            shift(group(order[1]), "col", -1),
            shift(group(order[3]), "col", 2),
        ],
        axis=2,
    )
    w_all = lax.all_gather(w_rows, "ctx", axis=1, tiled=True)

    small = jnp.concatenate(
        [short_taps.reshape(9, CH), long_taps, skip_gain[None], norm_gain.reshape(4, CH)], axis=0
    )
    small_all = lax.all_gather(small, "col", axis=0, tiled=False)
    gain = jnp.take(small_all[:, 138:].reshape(4, F), order, axis=0).reshape(1, D)
    n = jnp.arange(CH)
    wanted = (n // 16) * 64 + col * 16 + n % 16
    pick = (jnp.arange(F)[:, None] == wanted[None, :]).astype(f32)
    taps = jnp.dot(
        jnp.transpose(small_all[:, :138], (1, 0, 2)).reshape(138, F), pick, precision=lax.Precision.HIGHEST
    )

    full = jnp.concatenate([mine, before, after, jnp.concatenate([far_lo, far_hi], 0)], axis=1)
    y_before, y_after, y_far_lo, y_far_hi = gather_ring(full, "row")
    y_far = jnp.concatenate([y_far_lo, y_far_hi], 0)
    pieces = [project(x, gain, w_all) for x in (full, y_after, y_far, y_before)]

    tails = jnp.stack([piece[:, Q - HALO :] for piece in pieces])
    tail = lax.dynamic_index_in_dim(tails, (3 - row) % 4, 0, keepdims=False)
    halo = lax.ppermute(tail, "ctx", [(i, i + 1) for i in range(15)])

    mixed = mix(row[None], pieces, halo, taps)

    m = jnp.arange(F)
    blocks = order[m // 256]
    wanted_out = ((m % 256) // 16) * 64 + blocks * 16 + m % 16
    pick_out = (jnp.arange(F)[:, None] == wanted_out[None, :]).astype(bf16)
    out_rows = jnp.dot(w_out, pick_out, preferred_element_type=f32).astype(bf16)
    out_all = lax.all_gather(out_rows, "ctx", axis=0, tiled=True)

    m_before, m_after, m_far_lo, m_far_hi = gather_ring(mixed, "col")
    mixed_all = jnp.concatenate(
        [mixed, m_before, m_after, jnp.concatenate([m_far_lo, m_far_hi], 0)], axis=1
    )
    part = lax.dot_general(
        mixed_all, out_all, (((1,), (1,)), ((), ())), preferred_element_type=f32
    ).astype(bf16)
    part = part.reshape(4, Q, F)
    got = [part[0], shift(part[1], "row", 1), shift(part[2], "row", 2), shift(part[3], "row", -1)]
    return sum(g.astype(f32) for g in got).astype(bf16)


def solution(mesh):
    in_specs = (
        P("ctx", "col"),
        P("col"),
        P(("row", "ctx"), "col"),
        P(("row", "ctx"), "col"),
        P(("row", "ctx"), "col"),
        P(None, None, ("row", "col")),
        P(None, ("row", "col")),
        P(("row", "col")),
        P(("col", "ctx"), "row"),
    )
    out_specs = P(("ctx", "row"), "col")
    return jax.shard_map(
        on_device, mesh=mesh, in_specs=in_specs, out_specs=out_specs, check_vma=False
    )
```

time: 352 us -> 291 us (0.83)
  the two profiles are of different devices: /device:TPU:1 before, /device:TPU:2 now
where the time goes in v1:
time: 291 us
  waiting for transfers between devices  150 us (52%)
  Pallas kernels  41.7 us (14%)
  starting transfers between devices  39.6 us (14%)
  blocking collectives  16.2 us (6%)
  other arithmetic  13.9 us (5%)
  between operations  13.8 us (5%)
  local copies, waits for them, and re-layouts  9.82 us (3%)
  matrix products  6.37 us (2%)
    ppermute x18, waiting for transfers between devices, shift(): return lax.ppermute(x, axis, ring(4, step))  132 us
    ppermute x18, starting transfers between devices, shift(): return lax.ppermute(x, axis, ring(4, step))  37.6 us
    pallas_call x1, Pallas kernels, mix(): pl.pallas_call(mix_kernel, in_specs=[pl.BlockSpec(memory_space=pltpu.SMEM...  22 us
    pallas_call x4, Pallas kernels, project(): pl.pallas_call(project_kernel, grid=(3,), in_specs=[pl.BlockSpec((Q, D),...  19.7 us
    ppermute x1, waiting for transfers between devices, on_device(): halo = lax.ppermute(tail, 'ctx', [(i, i + 1) for i in range(15)])  18 us
    all_gather x1, blocking collectives, on_device(): small_all = lax.all_gather(small, 'col', axis=0, tiled=False)  16.2 us
    concatenate x1, other arithmetic, on_device(): jnp.concatenate([mine, before, after, jnp.concatenate([far_lo, far_hi], 0...  7.21 us
  transfers between devices with their start and end apart: 21, of which 16 were waited for; matrix products, arithmetic and copies ran while one was open for 6% of the time, Pallas kernels for 14%

profile of v1, /device:TPU:2, one launch (start us, length us, event | category | flops | bytes accessed | tf_op | source)
XLA Modules:
  0.0 291.2 jit_solution(17685807245171382714)
XLA Ops:
  6.5 1.2 pad_maximum_fusion.1
  7.8 7.3 %collective-permute-start.6 = (bf16[3,16,1024]{2,1,0:T(8,128)(2,1)S(1)}, bf16[3,16,1024]{2,1,0:T(8,128)(2,1)S(1)}, u32[]{:S(2)}, u32[]{:S(2)}) collective-permute-start(bf16[3,16,1024]{2,1,0:T(8,128)(2,1)S(1)} %get-tuple-element.9), channel_id=1, source_target_pairs={{0,2},{1,3},{2,0},{3,1},{4,6},{5,7},{6,4},{7,5},{8,10},{9,11},{10,... | collective-permute-start | bytes 294920 | tf_op jit(solution)/shard_map/ppermute | solution.py:25
  15.1 2.9 %collective-permute-start.4 = (bf16[3,16,1024]{2,1,0:T(8,128)(2,1)S(1)}, bf16[3,16,1024]{2,1,0:T(8,128)(2,1)S(1)}, u32[]{:S(2)}, u32[]{:S(2)}) collective-permute-start(bf16[3,16,1024]{2,1,0:T(8,128)(2,1)S(1)} %get-tuple-element.11), channel_id=1, source_target_pairs={{0,1},{1,2},{2,3},{3,0},{4,5},{5,6},{6,7},{7,4},{8,9},{9,10},{10,1... | collective-permute-start | bytes 294920 | tf_op jit(solution)/shard_map/ppermute | solution.py:25
  18.0 6.7 %collective-permute-done.5 = bf16[3,16,1024]{2,1,0:T(8,128)(2,1)S(1)} collective-permute-done((bf16[3,16,1024]{2,1,0:T(8,128)(2,1)S(1)}, bf16[3,16,1024]{2,1,0:T(8,128)(2,1)S(1)}, u32[]{:S(2)}, u32[]{:S(2)}) %collective-permute-start.5) | collective-permute-done | bytes 98336 | tf_op jit(solution)/shard_map/ppermute | solution.py:25
  24.8 0.8 pad_maximum_fusion.2
  25.7 3.1 %collective-permute-start.1 = (bf16[256,1024]{1,0:T(8,128)(2,1)S(1)}, bf16[256,1024]{1,0:T(8,128)(2,1)S(1)}, u32[]{:S(2)}, u32[]{:S(2)}) collective-permute-start(bf16[256,1024]{1,0:T(8,128)(2,1)S(1)} %constant_dynamic-slice_fusion), channel_id=1, source_target_pairs={{0,3},{1,0},{2,1},{3,2},{4,7},{5,4},{6,5},{7,6},{8,11},{9,8},{10,9... | collective-permute-start | bytes 1572872 | tf_op jit(solution)/shard_map/ppermute | solution.py:25
  28.8 15.7 %collective-permute-done.1 = bf16[256,1024]{1,0:T(8,128)(2,1)S(1)} collective-permute-done((bf16[256,1024]{1,0:T(8,128)(2,1)S(1)}, bf16[256,1024]{1,0:T(8,128)(2,1)S(1)}, u32[]{:S(2)}, u32[]{:S(2)}) %collective-permute-start.1) | collective-permute-done | bytes 524320 | tf_op jit(solution)/shard_map/ppermute | solution.py:25
  44.5 3.7 %collective-permute-start.3 = (bf16[128,1024]{1,0:T(8,128)(2,1)S(1)}, bf16[128,1024]{1,0:T(8,128)(2,1)S(1)}, u32[]{:S(2)}, u32[]{:S(2)}) collective-permute-start(bf16[128,1024]{1,0:T(8,128)(2,1)S(1)} %slice.76), channel_id=1, source_target_pairs={{0,3},{1,0},{2,1},{3,2},{4,7},{5,4},{6,5},{7,6},{8,11},{9,8},{10,9... | collective-permute-start | bytes 786440 | tf_op jit(solution)/shard_map/ppermute | solution.py:25
  48.2 8.2 %collective-permute-done = bf16[256,1024]{1,0:T(8,128)(2,1)S(1)} collective-permute-done((bf16[256,1024]{1,0:T(8,128)(2,1)S(1)}, bf16[256,1024]{1,0:T(8,128)(2,1)S(1)}, u32[]{:S(2)}, u32[]{:S(2)}) %collective-permute-start) | collective-permute-done | bytes 524320 | tf_op jit(solution)/shard_map/ppermute | solution.py:25
  57.1 13.6 %collective-permute-done.2 = bf16[128,1024]{1,0:T(8,128)(2,1)S(1)} collective-permute-done((bf16[128,1024]{1,0:T(8,128)(2,1)S(1)}, bf16[128,1024]{1,0:T(8,128)(2,1)S(1)}, u32[]{:S(2)}, u32[]{:S(2)}) %collective-permute-start.2) | collective-permute-done | bytes 262176 | tf_op jit(solution)/shard_map/ppermute | solution.py:25
  70.7 7.2 %maximum_maximum_fusion.x_ref = bf16[256,4096]{1,0:T(8,128)(2,1)} fusion(bf16[128,1024]{1,0:T(8,128)(2,1)S(1)} %collective-permute-done.3, bf16[128,1024]{1,0:T(8,128)(2,1)S(1)} %collective-permute-done.2, bf16[256,1024]{1,0:T(8,128)(2,1)S(1)} %collective-permute-done.1, bf16[256,1024]{1,0:T(8,128)(2,1)S(1)} %collective-permute-done, ...), kind=kLoop, calls=%fused_computation.3 | loop fusion | flops 10485760 | bytes 4194304 | tf_op jit(solution)/shard_map/concatenate | solution.py:179
  77.9 1.6 collective-permute-start.8
  79.5 1.7 collective-permute-start.7
  81.2 1.5 fusion.16
  82.8 16.2 %all-gather.1 = f32[4,142,256]{2,1,0:T(8,128)S(1)} all-gather(f32[1,142,256]{2,1,0:T(8,128)S(1)} %maximum_bitcast_fusion), channel_id=2, replica_groups=mesh['ctx'=16,'row'=4,'col'=4] {'col'}, dimensions={0}, use_global_device_ids=true | all-gather | bytes 727040 | tf_op jit(solution)/shard_map/all_gather | solution.py:170
  99.0 22.4 %collective-permute-done.8.x_ref = bf16[256,4096]{1,0:T(8,128)(2,1)} collective-permute-done((bf16[256,4096]{1,0:T(8,128)(2,1)}, bf16[256,4096]{1,0:T(8,128)(2,1)}, u32[]{:S(2)}, u32[]{:S(2)}) %collective-permute-start.8) | collective-permute-done | bytes 2097184 | tf_op jit(solution)/shard_map/ppermute | solution.py:25
  121.4 2.3 slice.78
  123.8 1.5 collective-permute-start.9
  125.3 2.3 slice.79
  127.6 1.7 collective-permute-start.10
  129.9 0.6 gather_fusion
  130.9 9.2 %collective-permute-done.9 = bf16[128,4096]{1,0:T(8,128)(2,1)} collective-permute-done((bf16[128,4096]{1,0:T(8,128)(2,1)}, bf16[128,4096]{1,0:T(8,128)(2,1)}, u32[]{:S(2)}, u32[]{:S(2)}) %collective-permute-start.9) | collective-permute-done | bytes 1048608 | tf_op jit(solution)/shard_map/ppermute | solution.py:25
  140.1 2.6 collective-permute-done.10
  142.7 3.1 %pad_maximum_fusion.x_ref = bf16[256,4096]{1,0:T(8,128)(2,1)} fusion(bf16[128,4096]{1,0:T(8,128)(2,1)} %collective-permute-done.10, bf16[128,4096]{1,0:T(8,128)(2,1)} %collective-permute-done.9), kind=kLoop, calls=%fused_computation.4 | loop fusion | flops 4194304 | bytes 4194304 | tf_op jit(solution)/shard_map/concatenate | solution.py:181
  145.8 2.8 copy-done.1
  148.6 5.4 %project.4.p0 = bf16[3,256,256]{2,1,0:T(8,128)(2,1)S(1)} custom-call(bf16[256,4096]{1,0:T(8,128)(2,1)} %maximum_maximum_fusion.x_ref, f32[1,4096]{1,0:T(1,128)S(1)} %bitcast.59, bf16[3,256,4096]{2,1,0:T(8,128)(2,1)S(1)} %copy-done.1), custom_call_target="tpu_custom_call" | custom-call | flops 1610612736 | bytes 8388608 | tf_op jit(solution)/shard_map/project/pallas_call | solution.py:55
  154.0 5.2 %project.7.p3 = bf16[3,256,256]{2,1,0:T(8,128)(2,1)S(1)} custom-call(bf16[256,4096]{1,0:T(8,128)(2,1)} %collective-permute-done.8.x_ref, f32[1,4096]{1,0:T(1,128)S(1)} %bitcast.60, bf16[3,256,4096]{2,1,0:T(8,128)(2,1)S(1)} %copy-done.2), custom_call_target="tpu_custom_call" | custom-call | flops 1610612736 | bytes 8388608 | tf_op jit(solution)/shard_map/project/pallas_call | solution.py:55
  159.2 5.4 %project.5.p1 = bf16[3,256,256]{2,1,0:T(8,128)(2,1)S(1)} custom-call(bf16[256,4096]{1,0:T(8,128)(2,1)} %collective-permute-done.7.x_ref, f32[1,4096]{1,0:T(1,128)S(1)} %bitcast.61, bf16[3,256,4096]{2,1,0:T(8,128)(2,1)S(1)} %copy-done.2), custom_call_target="tpu_custom_call" | custom-call | flops 1610612736 | bytes 8388608 | tf_op jit(solution)/shard_map/project/pallas_call | solution.py:55
  164.6 3.7 %project.6.p2 = bf16[3,256,256]{2,1,0:T(8,128)(2,1)S(1)} custom-call(bf16[256,4096]{1,0:T(8,128)(2,1)S(1)} %copy-done.3, f32[1,4096]{1,0:T(1,128)S(1)} %bitcast.62, bf16[3,256,4096]{2,1,0:T(8,128)(2,1)S(1)} %copy-done.2), custom_call_target="tpu_custom_call" | custom-call | flops 1610612736 | bytes 8388608 | tf_op jit(solution)/shard_map/project/pallas_call | solution.py:55
  168.6 1.9 collective-permute-start.11
  171.1 18.0 %collective-permute-done.11.halo_ref = bf16[3,144,256]{2,1,0:T(8,128)(2,1)S(1)} collective-permute-done((bf16[3,144,256]{2,1,0:T(8,128)(2,1)S(1)}, bf16[3,144,256]{2,1,0:T(8,128)(2,1)S(1)}, u32[]{:S(2)}, u32[]{:S(2)}) %collective-permute-start.11) | collective-permute-done | bytes 221216 | tf_op jit(solution)/shard_map/ppermute | solution.py:186
  189.1 22.0 %mix.1 = bf16[1024,256]{1,0:T(8,128)(2,1)S(1)} custom-call(s32[1]{0:T(128)} %bitcast.row_ref, bf16[3,256,256]{2,1,0:T(8,128)(2,1)S(1)} %project.4.p0, bf16[3,256,256]{2,1,0:T(8,128)(2,1)S(1)} %project.5.p1, bf16[3,256,256]{2,1,0:T(8,128)(2,1)S(1)} %project.6.p2, bf16[3,256,256]{2,1,0:T(8,128)(2,1)S(1)} %project.7.p3, ...), custom_call_target="tpu_custom_call" | custom-call | flops 1342177280 | bytes 4194304 | tf_op jit(solution)/shard_map/mix/pallas_call | solution.py:123
  211.1 3.0 %collective-permute-start.13 = (bf16[1024,256]{1,0:T(8,128)(2,1)S(1)}, bf16[1024,256]{1,0:T(8,128)(2,1)S(1)}, u32[]{:S(2)}, u32[]{:S(2)}) collective-permute-start(bf16[1024,256]{1,0:T(8,128)(2,1)S(1)} %mix.1), channel_id=1, source_target_pairs={{0,3},{1,0},{2,1},{3,2},{4,7},{5,4},{6,5},{7,6},{8,11},{9,8},{10,9... | collective-permute-start | bytes 1572872 | tf_op jit(solution)/shard_map/ppermute | solution.py:25
  214.1 4.8 %collective-permute-start.12 = (bf16[1024,256]{1,0:T(8,128)(2,1)S(1)}, bf16[1024,256]{1,0:T(8,128)(2,1)S(1)}, u32[]{:S(2)}, u32[]{:S(2)}) collective-permute-start(bf16[1024,256]{1,0:T(8,128)(2,1)S(1)} %mix.1), channel_id=1, source_target_pairs={{0,1},{1,2},{2,3},{3,0},{4,5},{5,6},{6,7},{7,4},{8,9},{9,10},{10,1... | collective-permute-start | bytes 1572872 | tf_op jit(solution)/shard_map/ppermute | solution.py:25
  218.9 14.0 %collective-permute-done.13 = bf16[1024,256]{1,0:T(8,128)(2,1)S(1)} collective-permute-done((bf16[1024,256]{1,0:T(8,128)(2,1)S(1)}, bf16[1024,256]{1,0:T(8,128)(2,1)S(1)}, u32[]{:S(2)}, u32[]{:S(2)}) %collective-permute-start.13) | collective-permute-done | bytes 524320 | tf_op jit(solution)/shard_map/ppermute | solution.py:25
  232.9 1.0 collective-permute-start.15
  233.8 3.4 %collective-permute-done.12 = bf16[1024,256]{1,0:T(8,128)(2,1)S(1)} collective-permute-done((bf16[1024,256]{1,0:T(8,128)(2,1)S(1)}, bf16[1024,256]{1,0:T(8,128)(2,1)S(1)}, u32[]{:S(2)}, u32[]{:S(2)}) %collective-permute-start.12) | collective-permute-done | bytes 524320 | tf_op jit(solution)/shard_map/ppermute | solution.py:25
  237.3 0.8 copy-done.6
  238.0 4.8 %collective-permute-done.15 = bf16[512,256]{1,0:T(8,128)(2,1)S(1)} collective-permute-done((bf16[512,256]{1,0:T(8,128)(2,1)S(1)}, bf16[512,256]{1,0:T(8,128)(2,1)S(1)}, u32[]{:S(2)}, u32[]{:S(2)}) %collective-permute-start.15) | collective-permute-done | bytes 262176 | tf_op jit(solution)/shard_map/ppermute | solution.py:25
  242.8 8.4 %collective-permute-done.14 = bf16[512,256]{1,0:T(8,128)(2,1)} collective-permute-done((bf16[512,256]{1,0:T(8,128)(2,1)S(1)}, bf16[512,256]{1,0:T(8,128)(2,1)}, u32[]{:S(2)}, u32[]{:S(2)}) %collective-permute-start.14) | collective-permute-done | bytes 262176 | tf_op jit(solution)/shard_map/ppermute | solution.py:25
  251.2 4.4 %fusion.12 = bf16[1024,1024]{1,0:T(8,128)(2,1)S(1)} fusion(bf16[1024,1024]{1,0:T(8,128)(2,1)} %all-gather.7.cloned.1.call-done, bf16[512,256]{1,0:T(8,128)(2,1)S(1)} %collective-permute-done.15, bf16[512,256]{1,0:T(8,128)(2,1)} %collective-permute-done.14, bf16[1024,256]{1,0:T(8,128)(2,1)} %copy-done.5, bf16[1024,256]{1,0:T(8,128)(2,1)} %copy-done.6, ...), kind=kOutput, calls=%fused_computation.16 | convolution fusion | flops 2159017984 | bytes 6291456 | tf_op jit(solution)/shard_map/dot_general | solution.py:201
  255.7 1.1 collective-permute-start.16
  256.8 2.8 collective-permute-start.18
  259.6 1.4 collective-permute-start.17
  261.0 10.5 %collective-permute-done.16 = bf16[256,1024]{1,0:T(8,128)(2,1)S(1)} collective-permute-done((bf16[256,1024]{1,0:T(8,128)(2,1)S(1)}, bf16[256,1024]{1,0:T(8,128)(2,1)S(1)}, u32[]{:S(2)}, u32[]{:S(2)}) %collective-permute-start.16) | collective-permute-done | bytes 524320 | tf_op jit(solution)/shard_map/ppermute | solution.py:25
  271.5 9.9 %collective-permute-done.18 = bf16[256,1024]{1,0:T(8,128)(2,1)S(1)} collective-permute-done((bf16[256,1024]{1,0:T(8,128)(2,1)S(1)}, bf16[256,1024]{1,0:T(8,128)(2,1)S(1)}, u32[]{:S(2)}, u32[]{:S(2)}) %collective-permute-start.18) | collective-permute-done | bytes 524320 | tf_op jit(solution)/shard_map/ppermute | solution.py:25
  281.4 1.8 collective-permute-done.17
  283.2 1.1 add_convert_fusion
  (64 shorter events, 2.8 us)
Async XLA Ops:
  6.5 19.1 %copy-start = (bf16[1024,1024]{1,0:T(8,128)(2,1)S(1)}, bf16[1024,1024]{1,0:T(8,128)(2,1)}, u32[]{:S(2)}) copy-start(bf16[1024,1024]{1,0:T(8,128)(2,1)} %param.9) | copy-start | bytes 6291460
  6.5 139.2 %all-gather.5.cloned.1.call-start = ((), (), s32[]{:S(2)}) async-start(), calls=%async_computation | async-start | bytes 6684672 | tf_op jit(solution)/shard_map/all_gather | solution.py:165
  7.8 10.2 %collective-permute-start.6 = (bf16[3,16,1024]{2,1,0:T(8,128)(2,1)S(1)}, bf16[3,16,1024]{2,1,0:T(8,128)(2,1)S(1)}, u32[]{:S(2)}, u32[]{:S(2)}) collective-permute-start(bf16[3,16,1024]{2,1,0:T(8,128)(2,1)S(1)} %get-tuple-element.9), channel_id=1, source_target_pairs={{0,2},{1,3},{2,0},{3,1},{4,6},{5,7},{6,4},{7,5},{8,10},{9,11},{10,... | collective-permute-start | bytes 294920 | tf_op jit(solution)/shard_map/ppermute | solution.py:25
  15.1 9.7 %collective-permute-start.5 = (bf16[3,16,1024]{2,1,0:T(8,128)(2,1)S(1)}, bf16[3,16,1024]{2,1,0:T(8,128)(2,1)S(1)}, u32[]{:S(2)}, u32[]{:S(2)}) collective-permute-start(bf16[3,16,1024]{2,1,0:T(8,128)(2,1)S(1)} %get-tuple-element.10), channel_id=1, source_target_pairs={{0,3},{1,0},{2,1},{3,2},{4,7},{5,4},{6,5},{7,6},{8,11},{9,8},{10,9... | collective-permute-start | bytes 294920 | tf_op jit(solution)/shard_map/ppermute | solution.py:25
  15.1 9.7 %collective-permute-start.4 = (bf16[3,16,1024]{2,1,0:T(8,128)(2,1)S(1)}, bf16[3,16,1024]{2,1,0:T(8,128)(2,1)S(1)}, u32[]{:S(2)}, u32[]{:S(2)}) collective-permute-start(bf16[3,16,1024]{2,1,0:T(8,128)(2,1)S(1)} %get-tuple-element.11), channel_id=1, source_target_pairs={{0,1},{1,2},{2,3},{3,0},{4,5},{5,6},{6,7},{7,4},{8,9},{9,10},{10,1... | collective-permute-start | bytes 294920 | tf_op jit(solution)/shard_map/ppermute | solution.py:25
  25.6 212.5 %all-gather.7.cloned.1.call-start = ((), (), s32[]{:S(2)}) async-start(), calls=%async_computation.1 | async-start | bytes 2228224 | tf_op jit(solution)/shard_map/all_gather | solution.py:195
  25.7 18.8 %collective-permute-start.1 = (bf16[256,1024]{1,0:T(8,128)(2,1)S(1)}, bf16[256,1024]{1,0:T(8,128)(2,1)S(1)}, u32[]{:S(2)}, u32[]{:S(2)}) collective-permute-start(bf16[256,1024]{1,0:T(8,128)(2,1)S(1)} %constant_dynamic-slice_fusion), channel_id=1, source_target_pairs={{0,3},{1,0},{2,1},{3,2},{4,7},{5,4},{6,5},{7,6},{8,11},{9,8},{10,9... | collective-permute-start | bytes 1572872 | tf_op jit(solution)/shard_map/ppermute | solution.py:25
  28.8 27.6 %collective-permute-start = (bf16[256,1024]{1,0:T(8,128)(2,1)S(1)}, bf16[256,1024]{1,0:T(8,128)(2,1)S(1)}, u32[]{:S(2)}, u32[]{:S(2)}) collective-permute-start(bf16[256,1024]{1,0:T(8,128)(2,1)S(1)} %constant_dynamic-slice_fusion), channel_id=1, source_target_pairs={{0,1},{1,2},{2,3},{3,0},{4,5},{5,6},{6,7},{7,4},{8,9},{9,10},{10,1... | collective-permute-start | bytes 1572872 | tf_op jit(solution)/shard_map/ppermute | solution.py:25
  44.5 12.6 %collective-permute-start.3 = (bf16[128,1024]{1,0:T(8,128)(2,1)S(1)}, bf16[128,1024]{1,0:T(8,128)(2,1)S(1)}, u32[]{:S(2)}, u32[]{:S(2)}) collective-permute-start(bf16[128,1024]{1,0:T(8,128)(2,1)S(1)} %slice.76), channel_id=1, source_target_pairs={{0,3},{1,0},{2,1},{3,2},{4,7},{5,4},{6,5},{7,6},{8,11},{9,8},{10,9... | collective-permute-start | bytes 786440 | tf_op jit(solution)/shard_map/ppermute | solution.py:25
  56.5 24.7 %copy-start.10 = (bf16[64,1024]{1,0:T(8,128)(2,1)S(1)}, bf16[64,1024]{1,0:T(8,128)(2,1)}, u32[]{:S(2)}) copy-start(bf16[64,1024]{1,0:T(8,128)(2,1)} %param.17) | copy-start | bytes 393220
  56.5 26.2 %copy-start.8 = (f32[1024]{0:T(1024)S(1)}, f32[1024]{0:T(1024)}, u32[]{:S(2)}) copy-start(f32[1024]{0:T(1024)} %param.10) | copy-start | bytes 12292
  56.5 26.2 %copy-start.7 = (f32[3,3,256]{2,1,0:T(4,128)S(1)}, f32[3,3,256]{2,1,0:T(4,128)}, u32[]{:S(2)}) copy-start(f32[3,3,256]{2,1,0:T(4,128)} %param.14) | copy-start | bytes 27652
  56.5 26.2 %copy-start.4 = (f32[128,256]{1,0:T(8,128)S(1)}, f32[128,256]{1,0:T(8,128)}, u32[]{:S(2)}) copy-start(f32[128,256]{1,0:T(8,128)} %param.15) | copy-start | bytes 393220
  56.5 26.2 %copy-start.9 = (f32[256]{0:T(256)S(1)}, f32[256]{0:T(256)}, u32[]{:S(2)}) copy-start(f32[256]{0:T(256)} %param.16) | copy-start | bytes 3076
  56.5 14.2 %collective-permute-start.2 = (bf16[128,1024]{1,0:T(8,128)(2,1)S(1)}, bf16[128,1024]{1,0:T(8,128)(2,1)S(1)}, u32[]{:S(2)}, u32[]{:S(2)}) collective-permute-start(bf16[128,1024]{1,0:T(8,128)(2,1)S(1)} %slice.75), channel_id=1, source_target_pairs={{0,1},{1,2},{2,3},{3,0},{4,5},{5,6},{6,7},{7,4},{8,9},{9,10},{10,1... | collective-permute-start | bytes 786440 | tf_op jit(solution)/shard_map/ppermute | solution.py:25
  77.9 43.5 %collective-permute-start.8 = (bf16[256,4096]{1,0:T(8,128)(2,1)}, bf16[256,4096]{1,0:T(8,128)(2,1)}, u32[]{:S(2)}, u32[]{:S(2)}) collective-permute-start(bf16[256,4096]{1,0:T(8,128)(2,1)} %maximum_maximum_fusion.x_ref), channel_id=1, source_target_pairs={{0,4},{4,8},{8,12},{12,0},{1,5},{5,9},{9,13},{13,1},{2,6},{6,10},{... | collective-permute-start | bytes 6291464 | tf_op jit(solution)/shard_map/ppermute | solution.py:25
  79.5 45.8 %collective-permute-start.7 = (bf16[256,4096]{1,0:T(8,128)(2,1)}, bf16[256,4096]{1,0:T(8,128)(2,1)}, u32[]{:S(2)}, u32[]{:S(2)}) collective-permute-start(bf16[256,4096]{1,0:T(8,128)(2,1)} %maximum_maximum_fusion.x_ref), channel_id=1, source_target_pairs={{0,12},{4,0},{8,4},{12,8},{1,13},{5,1},{9,5},{13,9},{2,14},{6,2},{... | collective-permute-start | bytes 6291464 | tf_op jit(solution)/shard_map/ppermute | solution.py:25
  123.8 16.3 %collective-permute-start.9 = (bf16[128,4096]{1,0:T(8,128)(2,1)}, bf16[128,4096]{1,0:T(8,128)(2,1)}, u32[]{:S(2)}, u32[]{:S(2)}) collective-permute-start(bf16[128,4096]{1,0:T(8,128)(2,1)} %slice.78), channel_id=1, source_target_pairs={{0,4},{4,8},{8,12},{12,0},{1,5},{5,9},{9,13},{13,1},{2,6},{6,10},{... | collective-permute-start | bytes 3145736 | tf_op jit(solution)/shard_map/ppermute | solution.py:25
  127.6 15.1 %collective-permute-start.10 = (bf16[128,4096]{1,0:T(8,128)(2,1)}, bf16[128,4096]{1,0:T(8,128)(2,1)}, u32[]{:S(2)}, u32[]{:S(2)}) collective-permute-start(bf16[128,4096]{1,0:T(8,128)(2,1)} %slice.79), channel_id=1, source_target_pairs={{0,12},{4,0},{8,4},{12,8},{1,13},{5,1},{9,5},{13,9},{2,14},{6,2},{... | collective-permute-start | bytes 3145736 | tf_op jit(solution)/shard_map/ppermute | solution.py:25
  145.8 2.8 copy-start.1
  148.6 5.4 %copy-start.2 = (bf16[3,256,4096]{2,1,0:T(8,128)(2,1)S(1)}, bf16[3,256,4096]{2,1,0:T(8,128)(2,1)}, u32[]{:S(2)}) copy-start(bf16[3,256,4096]{2,1,0:T(8,128)(2,1)} %all-gather.5.cloned.1.call-done.w_ref) | copy-start | bytes 18874372
  159.2 5.4 %copy-start.3 = (bf16[256,4096]{1,0:T(8,128)(2,1)S(1)}, bf16[256,4096]{1,0:T(8,128)(2,1)}, u32[]{:S(2)}) copy-start(bf16[256,4096]{1,0:T(8,128)(2,1)} %pad_maximum_fusion.x_ref) | copy-start | bytes 6291460
  168.6 20.5 %collective-permute-start.11 = (bf16[3,144,256]{2,1,0:T(8,128)(2,1)S(1)}, bf16[3,144,256]{2,1,0:T(8,128)(2,1)S(1)}, u32[]{:S(2)}, u32[]{:S(2)}) collective-permute-start(bf16[3,144,256]{2,1,0:T(8,128)(2,1)S(1)} %fusion.22), channel_id=1, source_target_pairs={{0,16},{16,32},{32,48},{48,64},{64,80},{80,96},{96,112},{112,128},... | collective-permute-start | bytes 663560 | tf_op jit(solution)/shard_map/ppermute | solution.py:186
  211.1 21.8 %collective-permute-start.13 = (bf16[1024,256]{1,0:T(8,128)(2,1)S(1)}, bf16[1024,256]{1,0:T(8,128)(2,1)S(1)}, u32[]{:S(2)}, u32[]{:S(2)}) collective-permute-start(bf16[1024,256]{1,0:T(8,128)(2,1)S(1)} %mix.1), channel_id=1, source_target_pairs={{0,3},{1,0},{2,1},{3,2},{4,7},{5,4},{6,5},{7,6},{8,11},{9,8},{10,9... | collective-permute-start | bytes 1572872 | tf_op jit(solution)/shard_map/ppermute | solution.py:25
  214.1 23.2 %collective-permute-start.12 = (bf16[1024,256]{1,0:T(8,128)(2,1)S(1)}, bf16[1024,256]{1,0:T(8,128)(2,1)S(1)}, u32[]{:S(2)}, u32[]{:S(2)}) collective-permute-start(bf16[1024,256]{1,0:T(8,128)(2,1)S(1)} %mix.1), channel_id=1, source_target_pairs={{0,1},{1,2},{2,3},{3,0},{4,5},{5,6},{6,7},{7,4},{8,9},{9,10},{10,1... | collective-permute-start | bytes 1572872 | tf_op jit(solution)/shard_map/ppermute | solution.py:25
  232.9 4.4 %copy-start.5 = (bf16[1024,256]{1,0:T(8,128)(2,1)}, bf16[1024,256]{1,0:T(8,128)(2,1)S(1)}, u32[]{:S(2)}) copy-start(bf16[1024,256]{1,0:T(8,128)(2,1)S(1)} %collective-permute-done.13) | copy-start | bytes 1572868
  232.9 9.9 %collective-permute-start.15 = (bf16[512,256]{1,0:T(8,128)(2,1)S(1)}, bf16[512,256]{1,0:T(8,128)(2,1)S(1)}, u32[]{:S(2)}, u32[]{:S(2)}) collective-permute-start(bf16[512,256]{1,0:T(8,128)(2,1)S(1)} %slice.86), channel_id=1, source_target_pairs={{0,3},{1,0},{2,1},{3,2},{4,7},{5,4},{6,5},{7,6},{8,11},{9,8},{10,9... | collective-permute-start | bytes 786440 | tf_op jit(solution)/shard_map/ppermute | solution.py:25
  237.2 0.8 copy-start.6
  238.0 13.2 %collective-permute-start.14 = (bf16[512,256]{1,0:T(8,128)(2,1)S(1)}, bf16[512,256]{1,0:T(8,128)(2,1)}, u32[]{:S(2)}, u32[]{:S(2)}) collective-permute-start(bf16[512,256]{1,0:T(8,128)(2,1)S(1)} %slice.85), channel_id=1, source_target_pairs={{0,1},{1,2},{2,3},{3,0},{4,5},{5,6},{6,7},{7,4},{8,9},{9,10},{10,1... | collective-permute-start | bytes 786440 | tf_op jit(solution)/shard_map/ppermute | solution.py:25
  255.7 15.7 %collective-permute-start.16 = (bf16[256,1024]{1,0:T(8,128)(2,1)S(1)}, bf16[256,1024]{1,0:T(8,128)(2,1)S(1)}, u32[]{:S(2)}, u32[]{:S(2)}) collective-permute-start(bf16[256,1024]{1,0:T(8,128)(2,1)S(1)} %get-tuple-element.5), channel_id=1, source_target_pairs={{0,4},{4,8},{8,12},{12,0},{1,5},{5,9},{9,13},{13,1},{2,6},{6,10},{... | collective-permute-start | bytes 1572872 | tf_op jit(solution)/shard_map/ppermute | solution.py:25
  256.8 24.5 %collective-permute-start.18 = (bf16[256,1024]{1,0:T(8,128)(2,1)S(1)}, bf16[256,1024]{1,0:T(8,128)(2,1)S(1)}, u32[]{:S(2)}, u32[]{:S(2)}) collective-permute-start(bf16[256,1024]{1,0:T(8,128)(2,1)S(1)} %get-tuple-element.6), channel_id=1, source_target_pairs={{0,12},{4,0},{8,4},{12,8},{1,13},{5,1},{9,5},{13,9},{2,14},{6,2},{... | collective-permute-start | bytes 1572872 | tf_op jit(solution)/shard_map/ppermute | solution.py:25
  259.6 23.6 %collective-permute-start.17 = (bf16[256,1024]{1,0:T(8,128)(2,1)S(1)}, bf16[256,1024]{1,0:T(8,128)(2,1)S(1)}, u32[]{:S(2)}, u32[]{:S(2)}) collective-permute-start(bf16[256,1024]{1,0:T(8,128)(2,1)S(1)} %get-tuple-element.7), channel_id=1, source_target_pairs={{0,8},{4,12},{8,0},{12,4},{1,9},{5,13},{9,1},{13,5},{2,10},{6,14},... | collective-permute-start | bytes 1572872 | tf_op jit(solution)/shard_map/ppermute | solution.py:25
Sparse Core Ops, SparseCore 0:
  25.7 69.0 all-gather.4
  96.6 39.3 all-gather.6

commit v2 on v1

v2 whole, which is shorter than its diff:
```python
import functools

import jax
import jax.numpy as jnp
from jax import lax
from jax.experimental import pallas as pl
from jax.experimental.pallas import tpu as pltpu
from jax.sharding import PartitionSpec as P

D = 4096
SHORT_LEN = 3
FILTER_LEN = 128
HALO = 144
Q = 256
CH = 256
F = 1024
epsilon = 1e-05
bf16 = jnp.bfloat16
f32 = jnp.float32


def ring(n, step):
    return [(i, (i + step) % n) for i in range(n)]


def shift(x, axis, step):
    return lax.ppermute(x, axis, ring(4, step))


def project_kernel(count, *refs):
    pieces, w_hbm, out_ref, x, w, scale_ref, x_sems, w_sems = refs[: 4 * count], *refs[4 * count :]
    x_copies = [pltpu.make_async_copy(piece, x.at[i], x_sems.at[i]) for i, piece in enumerate(pieces)]
    w_copies = [pltpu.make_async_copy(w_hbm.at[i], w.at[i], w_sems.at[i]) for i in range(16)]
    for copy in x_copies + w_copies:
        copy.start()
    rows = 64
    for s in range(count):
        for copy in x_copies[4 * s : 4 * s + 4]:
            copy.wait()

    @pl.loop(0, count * (Q // rows))
    def _(i):
        s = i // (Q // rows)
        at = pl.ds(pl.multiple_of(lax.rem(i, Q // rows) * rows, rows), rows)
        squares = None
        for b in range(4):
            values = x[4 * s + b, at, :].astype(f32)
            part = jnp.sum(values * values, axis=1, keepdims=True)
            squares = part if squares is None else squares + part
        scale_ref[s, at, :] = jnp.broadcast_to(lax.rsqrt(squares / D + epsilon), (rows, 128))

    for copy in w_copies:
        copy.wait()

    @pl.loop(0, 3 * count)
    def _(i):
        p, s = i // count, lax.rem(i, count)
        total = None
        for b in range(4):
            part = lax.dot_general(
                x[4 * s + b],
                w[:, p, :, F * b : F * b + F].reshape(CH, F),
                (((1,), (1,)), ((), ())),
                preferred_element_type=f32,
            )
            total = part if total is None else total + part
        scale = scale_ref[s]
        for lanes in (slice(0, 128), slice(128, 256)):
            out_ref[p, pl.ds(pl.multiple_of(s * Q, Q), Q), lanes] = (total[:, lanes] * scale).astype(bf16)


def project(pieces, w):
    count = len(pieces) // 4
    anywhere = pl.BlockSpec(memory_space=pl.ANY)
    return pl.pallas_call(
        functools.partial(project_kernel, count),
        in_specs=[anywhere] * (4 * count + 1),
        out_specs=pl.BlockSpec(memory_space=pltpu.VMEM),
        out_shape=jax.ShapeDtypeStruct((3, count * Q, CH), bf16),
        scratch_shapes=[
            pltpu.VMEM((4 * count, Q, F), bf16),
            pltpu.VMEM((16, 3, 16, D), bf16),
            pltpu.VMEM((count, Q, 128), f32),
            pltpu.SemaphoreType.DMA((4 * count,)),
            pltpu.SemaphoreType.DMA((16,)),
        ],
        compiler_params=pltpu.CompilerParams(vmem_limit_bytes=56 << 20),
        cost_estimate=pl.CostEstimate(
            flops=2 * count * Q * 3 * CH * D,
            bytes_accessed=2 * (count * Q * D + 3 * CH * D),
            transcendentals=0,
        ),
        name="project",
    )(*pieces, w)


HALF = 512


def mix_kernel(first, row_ref, near_ref, far_ref, halo_ref, taps_ref, out_ref, qkv, gate, shifted):
    row = row_ref[0]
    if first:
        qkv[:, :HALO, :] = halo_ref[...].astype(f32)
    for s, (ref, at) in enumerate(((near_ref, 0), (near_ref, Q), (far_ref, 0), (near_ref, 2 * Q))):
        start = pl.multiple_of(lax.rem(row + s, 4) * Q + HALO, 16)
        for proj in range(3):
            qkv[proj, pl.ds(start, Q), :] = ref[proj, at : at + Q, :].astype(f32)
    offset = 0 if first else HALF

    step = 64

    @pl.loop(0, 2)
    def _(lane_block):
        lanes = pl.ds(pl.multiple_of(lane_block * 128, 128), 128)

        @pl.loop(0, (HALF + 128) // step)
        def _(i):
            base = pl.multiple_of(i * step, step) + (HALO - 128 + offset)
            total = []
            for proj in (1, 2):
                window = qkv[proj, pl.ds(pl.multiple_of(base - 8, 8), step + 8), lanes]
                acc = None
                for tap in range(SHORT_LEN):
                    term = taps_ref[pl.ds(3 * proj + tap, 1), lanes] * window[8 - tap : 8 - tap + step]
                    acc = term if acc is None else acc + term
                total.append(acc)
            gate[pl.ds(pl.multiple_of(i * step, step) + 8, step), lanes] = total[0] * total[1]

        @pl.loop(0, (HALF + 128) // 64)
        def _(i):
            base = pl.multiple_of(i * 64, 64)
            window = gate[pl.ds(base, 72), lanes]
            for r in range(8):
                shifted[r, pl.ds(base, 64), lanes] = window[8 - r : 72 - r]

        @pl.loop(0, HALF // 128)
        def _(i):
            base = pl.multiple_of(i * 128, 128)
            acc = taps_ref[pl.ds(137, 1), lanes] * gate[pl.ds(base + 136, 128), lanes]
            for r in range(8):
                window = shifted[r, pl.ds(base + 8, 248), lanes]
                for m in range(16):
                    acc = acc + taps_ref[pl.ds(9 + 8 * m + r, 1), lanes] * window[120 - 8 * m : 248 - 8 * m]
            window = qkv[0, pl.ds(base + (HALO - 8 + offset), 136), lanes]
            query = None
            for tap in range(SHORT_LEN):
                term = taps_ref[pl.ds(tap, 1), lanes] * window[8 - tap : 136 - tap]
                query = term if query is None else query + term
            out_ref[pl.ds(base, 128), lanes] = (query * acc).astype(bf16)


def mix(first, row, near, far, halo, taps):
    return pl.pallas_call(
        functools.partial(mix_kernel, first),
        in_specs=[pl.BlockSpec(memory_space=pltpu.SMEM)] + [pl.BlockSpec(memory_space=pltpu.VMEM)] * 4,
        out_specs=pl.BlockSpec(memory_space=pltpu.VMEM),
        out_shape=jax.ShapeDtypeStruct((HALF, CH), bf16),
        scratch_shapes=[
            pltpu.VMEM((3, HALO + 4 * Q, CH), f32),
            pltpu.VMEM((HALF + 136, CH), f32),
            pltpu.VMEM((8, HALF + 128, CH), f32),
        ],
        compiler_params=pltpu.CompilerParams(vmem_limit_bytes=24 << 20),
        cost_estimate=pl.CostEstimate(
            flops=9_000_000_000, bytes_accessed=2 << 20, transcendentals=0
        ),
        name="mix",
    )(row, near, far, halo, taps)


def shard_of(n):
    return n // 4 * 4 + n % 2 * 2 + n // 2 % 2


def after(x, *others):
    return lax.optimization_barrier((x, others))[0]


def gather_col(x):
    half = x.shape[0] // 2
    before = shift(x, "col", 1)
    behind = shift(x, "col", -1)
    far = [shift(before[:half], "col", 1), shift(behind[half:], "col", -1)]
    return [x, before, behind, jnp.concatenate(far, 0)]


HF = F // 2


def on_device(
    activations, norm_gain, w_query, w_key, w_value, short_taps, long_taps, skip_gain, w_out
):
    row = lax.axis_index("row")
    col = lax.axis_index("col")
    order = jnp.stack([col, (col + 3) % 4, (col + 1) % 4, (col + 2) % 4])

    stacked = (jnp.stack([w_query, w_key, w_value]).astype(f32) * norm_gain).astype(bf16).reshape(3, 4, 16, F)

    def group(i):
        return lax.dynamic_index_in_dim(stacked, i, 1, keepdims=False).reshape(48, F)

    own = lax.dynamic_slice_in_dim(activations, row * Q, Q, 0)

    def payload(x, w):
        return jnp.concatenate([x, w[:, :HF], w[:, HF:]], axis=0)

    own_from_before = shift(own, "row", 1)
    own_from_after = shift(own, "row", -1)
    up = shift(payload(own[:, :HF], group(order[2])), "col", 1)
    down = shift(payload(own[:, HF:], group(order[1])), "col", -1)
    w_far = shift(group(order[3]), "col", 2)
    w_up = (up[Q : Q + 48], up[Q + 48 :])
    w_down = (down[Q : Q + 48], down[Q + 48 :])
    w_rows = jnp.concatenate(
        [group(order[0]), w_up[0], w_down[1], w_down[0], w_up[1], w_far], axis=1
    )
    w_rows = after(w_rows, own_from_before, own_from_after)
    low_z = (lax.axis_index("ctx") // 2) % 2 == 0
    w_other = lax.ppermute(w_rows, "ctx", [(i, i ^ 2) for i in range(16)])

    mixed_up = jnp.concatenate([up[:Q], down[:Q]], axis=1)
    up_from_before = shift(mixed_up, "row", 1)
    up_from_after = shift(mixed_up, "row", -1)

    w_pair = jnp.concatenate([jnp.where(low_z, w_rows, w_other), jnp.where(low_z, w_other, w_rows)], axis=0)
    rest_up = shift(own[:, HF:], "col", 1)
    rest_down = shift(own[:, :HF], "col", -1)
    far_own = shift(own_from_before, "row", 1)
    w_pair = after(w_pair, up_from_before, up_from_after, rest_up, rest_down, far_own)
    groups = [[4 * x + 2 * z + core for x in range(4) for core in range(2)] for z in range(2)]
    w_all = lax.all_gather(w_pair, "ctx", axis=0, tiled=True, axis_index_groups=groups).reshape(16, 3, 16, D)

    far_up = shift(up[:Q], "col", 1)
    far_down = shift(down[:Q], "col", -1)
    own = [
        own,
        mixed_up,
        jnp.concatenate([rest_down, rest_up], axis=1),
        jnp.concatenate([far_up, far_down], axis=1),
    ]
    from_before = [own_from_before, up_from_before] + [shift(x, "row", 1) for x in own[2:]]
    from_after = [own_from_after, up_from_after] + [shift(x, "row", -1) for x in own[2:]]
    far = [far_own, shift(up_from_before, "row", 1)] + [shift(x, "row", -1) for x in from_after[2:]]
    near_out = project(own + from_after + from_before, w_all)
    far_out = project([after(far[0], near_out)] + far[1:], w_all)

    small = jnp.concatenate(
        [short_taps.reshape(9, CH), long_taps, skip_gain[None], jnp.zeros((6, CH), f32)], axis=0
    )
    small = after(small, far_up, far_down)
    v = jnp.arange(512)
    wanted = shard_of(v % 128 // 16) * 64 + order[v // 128] * 16 + v % 16
    pick = ((jnp.arange(CH)[:, None] == wanted[None, :]) & (v % 128 < 64)[None, :]).astype(f32)
    small = jnp.dot(small, pick, precision=lax.Precision.HIGHEST)
    small = jnp.concatenate(
        [
            small[:, :128],
            shift(small[:, 256:384], "col", 1),
            shift(small[:, 128:256], "col", -1),
            shift(small[:, 384:], "col", 2),
        ],
        axis=1,
    )
    place = ((order[v // 128] * 64 + v % 128)[:, None] == jnp.arange(CH)[None, :]) & (v % 128 < 64)[:, None]
    taps = jnp.dot(small, place.astype(f32), precision=lax.Precision.HIGHEST)

    m = jnp.arange(F)
    blocks = order[m // 256]
    wanted_out = shard_of((m % 256) // 16) * 64 + blocks * 16 + m % 16
    pick_out = (jnp.arange(F)[:, None] == wanted_out[None, :]).astype(bf16)
    out_rows = jnp.dot(w_out, pick_out, preferred_element_type=f32).astype(bf16)
    out_all = lax.all_gather(out_rows, "ctx", axis=0, tiled=True)

    tails = [near_out[:, Q - HALO : Q], near_out[:, 2 * Q - HALO : 2 * Q], far_out[:, Q - HALO :], near_out[:, 3 * Q - HALO :]]
    tail = lax.dynamic_index_in_dim(jnp.stack(tails), (3 - row) % 4, 0, keepdims=False)
    halo = lax.ppermute(tail, "ctx", [(i, i + 1) for i in range(15)])

    late = mix(False, row[None], near_out, far_out, tail, taps)
    early = mix(True, row[None], near_out, far_out, halo, taps)
    mixed = jnp.concatenate([early, late], axis=0).reshape(4, Q, CH)

    def quarter(s):
        return lax.dynamic_index_in_dim(mixed, (row + s) % 4, 0, keepdims=False)

    first = gather_col(jnp.concatenate([quarter(2), quarter(1)], axis=0))
    second = gather_col(after(jnp.concatenate([quarter(3), quarter(0)], axis=0), first[1], first[2]))

    def outputs(gathered):
        return lax.dot_general(
            jnp.concatenate(gathered, axis=1), out_all, (((1,), (1,)), ((), ())), preferred_element_type=f32
        ).astype(bf16)

    part = outputs(first)
    got = [shift(part[:Q], "row", 2), shift(part[Q:], "row", 1)]
    part = outputs(second)
    got += [shift(part[:Q], "row", -1), part[Q:]]
    return sum(g.astype(f32) for g in got).astype(bf16)


def solution(mesh):
    in_specs = (
        P("ctx", "col"),
        P("col"),
        P(("row", "ctx"), "col"),
        P(("row", "ctx"), "col"),
        P(("row", "ctx"), "col"),
        P(None, None, ("row", "col")),
        P(None, ("row", "col")),
        P(("row", "col")),
        P(("col", "ctx"), "row"),
    )
    out_specs = P(("ctx", "row"), "col")
    return jax.shard_map(
        on_device, mesh=mesh, in_specs=in_specs, out_specs=out_specs, check_vma=False
    )
```

time: 291 us -> 232 us (0.80)
  the two profiles are of different devices: /device:TPU:2 before, /device:TPU:1 now
where the time goes in v2:
time: 232 us
  waiting for transfers between devices  97.2 us (42%)
  starting transfers between devices  64 us (28%)
  Pallas kernels  37.8 us (16%)
  between operations  13.9 us (6%)
  local copies, waits for them, and re-layouts  7.39 us (3%)
  matrix products  6.41 us (3%)
  other arithmetic  4.74 us (2%)
    ppermute x33, waiting for transfers between devices, shift(): return lax.ppermute(x, axis, ring(4, step))  82.9 us
    ppermute x33, starting transfers between devices, shift(): return lax.ppermute(x, axis, ring(4, step))  53.3 us
    pallas_call x2, Pallas kernels, project(): pl.pallas_call(functools.partial(project_kernel, count), in_specs=[anywhe...  22 us
    pallas_call x2, Pallas kernels, mix(): pl.pallas_call(functools.partial(mix_kernel, first), in_specs=[pl.BlockSp...  15.8 us
    ppermute x1, waiting for transfers between devices, on_device(): w_other = lax.ppermute(w_rows, 'ctx', [(i, i ^ 2) for i in range(16)])  8.47 us
    ppermute x1, starting transfers between devices, on_device(): halo = lax.ppermute(tail, 'ctx', [(i, i + 1) for i in range(15)])  5.91 us
    all_gather x1, waiting for transfers between devices, on_device(): lax.all_gather(w_pair, 'ctx', axis=0, tiled=True, axis_index_groups=groups)  5.79 us
    ppermute x1, starting transfers between devices, on_device(): w_other = lax.ppermute(w_rows, 'ctx', [(i, i ^ 2) for i in range(16)])  4.73 us
  transfers between devices with their start and end apart: 37, of which 21 were waited for; matrix products, arithmetic and copies ran while one was open for 6% of the time, Pallas kernels for 16%

profile of v2, /device:TPU:1, one launch (start us, length us, event | category | flops | bytes accessed | tf_op | source)
XLA Modules:
  0.0 231.5 jit_solution(17171899612006324548)
XLA Ops:
  8.9 3.9 %collective-permute-start = (bf16[352,512]{1,0:T(8,128)(2,1)S(1)}, bf16[352,512]{1,0:T(8,128)(2,1)S(1)}, u32[]{:S(2)}, u32[]{:S(2)}) collective-permute-start(bf16[352,512]{1,0:T(8,128)(2,1)S(1)} %pad_maximum_fusion.3), channel_id=1, source_target_pairs={{0,1},{1,2},{2,3},{3,0},{4,5},{5,6},{6,7},{7,4},{8,9},{9,10},{10,1... | collective-permute-start | bytes 1081352 | tf_op jit(solution)/shard_map/ppermute | solution.py:27
  12.8 3.1 %collective-permute-start.1 = (bf16[352,512]{1,0:T(8,128)(2,1)S(1)}, bf16[352,512]{1,0:T(8,128)(2,1)S(1)}, u32[]{:S(2)}, u32[]{:S(2)}) collective-permute-start(bf16[352,512]{1,0:T(8,128)(2,1)S(1)} %pad_maximum_fusion.4), channel_id=1, source_target_pairs={{0,3},{1,0},{2,1},{3,2},{4,7},{5,4},{6,5},{7,6},{8,11},{9,8},{10,9... | collective-permute-start | bytes 1081352 | tf_op jit(solution)/shard_map/ppermute | solution.py:27
  17.0 1.4 collective-permute-start.10
  18.4 1.5 collective-permute-start.6
  19.9 4.4 %collective-permute-start.14 = (bf16[48,1024]{1,0:T(8,128)(2,1)S(1)}, bf16[48,1024]{1,0:T(8,128)(2,1)S(1)}, u32[]{:S(2)}, u32[]{:S(2)}) collective-permute-start(bf16[48,1024]{1,0:T(8,128)(2,1)S(1)} %bitcast.53), channel_id=1, source_target_pairs={{0,2},{1,3},{2,0},{3,1},{4,6},{5,7},{6,4},{7,5},{8,10},{9,11},{10,... | collective-permute-start | bytes 294920 | tf_op jit(solution)/shard_map/ppermute | solution.py:27
  24.4 2.2 collective-permute-done
  26.6 9.3 %collective-permute-done.1 = bf16[352,512]{1,0:T(8,128)(2,1)S(1)} collective-permute-done((bf16[352,512]{1,0:T(8,128)(2,1)S(1)}, bf16[352,512]{1,0:T(8,128)(2,1)S(1)}, u32[]{:S(2)}, u32[]{:S(2)}) %collective-permute-start.1) | collective-permute-done | bytes 360480 | tf_op jit(solution)/shard_map/ppermute | solution.py:27
  36.0 4.7 %collective-permute-start.15 = (bf16[48,4096]{1,0:T(8,128)(2,1)S(1)}, bf16[48,4096]{1,0:T(8,128)(2,1)S(1)}, u32[]{:S(2)}, u32[]{:S(2)}) collective-permute-start(bf16[48,4096]{1,0:T(8,128)(2,1)S(1)} %constant_dynamic-update-slice_fusion.4), channel_id=1, source_target_pairs={{0,32},{16,48},{32,0},{48,16},{64,96},{80,112},{96,64},{112,80},{1... | collective-permute-start | bytes 1179656 | tf_op jit(solution)/shard_map/ppermute | solution.py:219
  40.7 2.4 %collective-permute-start.3 = (bf16[256,512]{1,0:T(8,128)(2,1)S(1)}, bf16[256,512]{1,0:T(8,128)(2,1)}, u32[]{:S(2)}, u32[]{:S(2)}) collective-permute-start(bf16[256,512]{1,0:T(8,128)(2,1)S(1)} %get-tuple-element.16), channel_id=1, source_target_pairs={{0,1},{1,2},{2,3},{3,0},{4,5},{5,6},{6,7},{7,4},{8,9},{9,10},{10,1... | collective-permute-start | bytes 786440 | tf_op jit(solution)/shard_map/ppermute | solution.py:27
  43.2 1.4 collective-permute-start.11
  44.6 1.5 collective-permute-start.7
  46.1 8.5 %collective-permute-done.15 = bf16[48,4096]{1,0:T(8,128)(2,1)S(1)} collective-permute-done((bf16[48,4096]{1,0:T(8,128)(2,1)S(1)}, bf16[48,4096]{1,0:T(8,128)(2,1)S(1)}, u32[]{:S(2)}, u32[]{:S(2)}) %collective-permute-start.15) | collective-permute-done | bytes 393248 | tf_op jit(solution)/shard_map/ppermute | solution.py:219
  56.9 3.6 %collective-permute-done.3 = bf16[256,512]{1,0:T(8,128)(2,1)} collective-permute-done((bf16[256,512]{1,0:T(8,128)(2,1)S(1)}, bf16[256,512]{1,0:T(8,128)(2,1)}, u32[]{:S(2)}, u32[]{:S(2)}) %collective-permute-start.3) | collective-permute-done | bytes 262176 | tf_op jit(solution)/shard_map/ppermute | solution.py:27
  60.5 5.7 %collective-permute-done.16.refs_0_ = bf16[256,1024]{1,0:T(8,128)(2,1)S(1)} collective-permute-done((bf16[256,1024]{1,0:T(8,128)(2,1)}, bf16[256,1024]{1,0:T(8,128)(2,1)S(1)}, u32[]{:S(2)}, u32[]{:S(2)}) %collective-permute-start.16) | collective-permute-done | bytes 524320 | tf_op jit(solution)/shard_map/ppermute | solution.py:27
  67.6 3.6 %collective-permute-start.5 = (bf16[256,512]{1,0:T(8,128)(2,1)S(1)}, bf16[256,512]{1,0:T(8,128)(2,1)S(1)}, u32[]{:S(2)}, u32[]{:S(2)}) collective-permute-start(bf16[256,512]{1,0:T(8,128)(2,1)S(1)} %slice.131), channel_id=1, source_target_pairs={{0,3},{1,0},{2,1},{3,2},{4,7},{5,4},{6,5},{7,6},{8,11},{9,8},{10,9... | collective-permute-start | bytes 786440 | tf_op jit(solution)/shard_map/ppermute | solution.py:27
  73.1 1.5 collective-permute-start.8
  75.8 5.7 %collective-permute-done.5 = bf16[256,512]{1,0:T(8,128)(2,1)S(1)} collective-permute-done((bf16[256,512]{1,0:T(8,128)(2,1)S(1)}, bf16[256,512]{1,0:T(8,128)(2,1)S(1)}, u32[]{:S(2)}, u32[]{:S(2)}) %collective-permute-start.5) | collective-permute-done | bytes 262176 | tf_op jit(solution)/shard_map/ppermute | solution.py:27
  82.8 1.5 collective-permute-start.9
  84.6 3.0 %collective-permute-done.21 = f32[144,128]{1,0:T(8,128)S(1)} collective-permute-done((f32[144,128]{1,0:T(8,128)S(1)}, f32[144,128]{1,0:T(8,128)S(1)}, u32[]{:S(2)}, u32[]{:S(2)}) %collective-permute-start.21) | collective-permute-done | bytes 73760 | tf_op jit(solution)/shard_map/ppermute | solution.py:27
  88.4 1.4 fusion.3
  89.8 2.2 collective-permute-done.22
  92.6 2.3 collective-permute-start.18
  94.9 4.3 %collective-permute-done.23 = f32[144,128]{1,0:T(8,128)S(1)} collective-permute-done((f32[144,128]{1,0:T(8,128)S(1)}, f32[144,128]{1,0:T(8,128)S(1)}, u32[]{:S(2)}, u32[]{:S(2)}) %collective-permute-start.23) | collective-permute-done | bytes 73760 | tf_op jit(solution)/shard_map/ppermute | solution.py:27
  99.2 2.7 %collective-permute-start.19 = (bf16[256,1024]{1,0:T(8,128)(2,1)}, bf16[256,1024]{1,0:T(8,128)(2,1)S(1)}, u32[]{:S(2)}, u32[]{:S(2)}) collective-permute-start(bf16[256,1024]{1,0:T(8,128)(2,1)} %collective-permute-done.9.refs_7_), channel_id=1, source_target_pairs={{0,12},{4,0},{8,4},{12,8},{1,13},{5,1},{9,5},{13,9},{2,14},{6,2},{... | collective-permute-start | bytes 1572872 | tf_op jit(solution)/shard_map/ppermute | solution.py:27
  102.3 2.5 %collective-permute-done.13.refs_11_ = bf16[256,1024]{1,0:T(8,128)(2,1)} collective-permute-done((bf16[256,1024]{1,0:T(8,128)(2,1)S(1)}, bf16[256,1024]{1,0:T(8,128)(2,1)}, u32[]{:S(2)}, u32[]{:S(2)}) %collective-permute-start.13) | collective-permute-done | bytes 524320 | tf_op jit(solution)/shard_map/ppermute | solution.py:27
  104.9 5.8 %all-gather.3.cloned.1.call-done = bf16[768,4096]{1,0:T(8,128)(2,1)} async-done(((bf16[96,4096]{1,0:T(8,128)(2,1)}), bf16[768,4096]{1,0:T(8,128)(2,1)}) %all-gather.3.cloned.1.call-update) | async-done | bytes 6291472 | tf_op jit(solution)/shard_map/all_gather | solution.py:231
  110.7 14.7 %project.2.near_ref = bf16[3,768,256]{2,1,0:T(8,128)(2,1)} custom-call(bf16[256,1024]{1,0:T(8,128)(2,1)} %copy-done.8, bf16[256,1024]{1,0:T(8,128)(2,1)} %copy-done.7, bf16[256,1024]{1,0:T(8,128)(2,1)} %copy-done.9, bf16[256,1024]{1,0:T(8,128)(2,1)} %copy-done.10, bf16[256,1024]{1,0:T(8,128)(2,1)} %copy-done.14, ...), custom_call_target="tpu_custom_call" | custom-call | flops 4831838208 | bytes 12582912 | tf_op jit(solution)/shard_map/project/pallas_call | solution.py:75
  127.1 7.3 %project.3.far_ref = bf16[3,256,256]{2,1,0:T(8,128)(2,1)} custom-call(bf16[256,1024]{1,0:T(8,128)(2,1)} %copy-done.3, bf16[256,1024]{1,0:T(8,128)(2,1)} %copy-done.5, bf16[256,1024]{1,0:T(8,128)(2,1)} %copy-done.4, bf16[256,1024]{1,0:T(8,128)(2,1)} %copy-done.6, bf16[16,3,16,4096]{3,2,1,0:T(8,128)(2,1)} %bitcast.45), custom_call_target="tpu_custom_call" | custom-call | flops 1610612736 | bytes 8388608 | tf_op jit(solution)/shard_map/project/pallas_call | solution.py:75
  135.7 5.9 %collective-permute-start.20 = (bf16[3,144,256]{2,1,0:T(8,128)(2,1)S(1)}, bf16[3,144,256]{2,1,0:T(8,128)(2,1)S(1)}, u32[]{:S(2)}, u32[]{:S(2)}) collective-permute-start(bf16[3,144,256]{2,1,0:T(8,128)(2,1)S(1)} %fusion.44.halo_ref), channel_id=1, source_target_pairs={{0,16},{16,32},{32,48},{48,64},{64,80},{80,96},{96,112},{112,128},... | collective-permute-start | bytes 663560 | tf_op jit(solution)/shard_map/ppermute | solution.py:276
  141.6 7.9 %mix.3 = bf16[512,256]{1,0:T(8,128)(2,1)S(1)} custom-call(s32[1]{0:T(128)} %bitcast.row_ref, bf16[3,768,256]{2,1,0:T(8,128)(2,1)S(1)} %copy-done.2, bf16[3,256,256]{2,1,0:T(8,128)(2,1)S(1)} %copy-done.1, bf16[3,144,256]{2,1,0:T(8,128)(2,1)S(1)} %fusion.44.halo_ref, f32[144,256]{1,0:T(8,128)S(1)} %fusion.28.taps_ref), custom_call_target="tpu_custom_call" | custom-call | flops 8999999488 | bytes 2097152 | tf_op jit(solution)/shard_map/mix/pallas_call | solution.py:153
  149.6 7.9 %mix.2 = bf16[512,256]{1,0:T(8,128)(2,1)S(1)} custom-call(s32[1]{0:T(128)} %bitcast.row_ref, bf16[3,768,256]{2,1,0:T(8,128)(2,1)S(1)} %copy-done.2, bf16[3,256,256]{2,1,0:T(8,128)(2,1)S(1)} %copy-done.1, bf16[3,144,256]{2,1,0:T(8,128)(2,1)S(1)} %collective-permute-done.20.halo_ref, f32[144,256]{1,0:T(8,128)S(1)} %fusion.28.taps_ref), custom_call_target="tpu_custom_call" | custom-call | flops 8999999488 | bytes 2097152 | tf_op jit(solution)/shard_map/mix/pallas_call | solution.py:153
  157.6 2.1 collective-permute-start.24
  159.6 1.6 collective-permute-start.25
  161.2 8.1 %collective-permute-done.24 = bf16[512,256]{1,0:T(8,128)(2,1)S(1)} collective-permute-done((bf16[512,256]{1,0:T(8,128)(2,1)S(1)}, bf16[512,256]{1,0:T(8,128)(2,1)S(1)}, u32[]{:S(2)}, u32[]{:S(2)}) %collective-permute-start.24) | collective-permute-done | bytes 262176 | tf_op jit(solution)/shard_map/ppermute | solution.py:27
  169.3 2.8 %collective-permute-start.26 = (bf16[256,256]{1,0:T(8,128)(2,1)S(1)}, bf16[256,256]{1,0:T(8,128)(2,1)S(1)}, u32[]{:S(2)}, u32[]{:S(2)}) collective-permute-start(bf16[256,256]{1,0:T(8,128)(2,1)S(1)} %slice.144), channel_id=1, source_target_pairs={{0,1},{1,2},{2,3},{3,0},{4,5},{5,6},{6,7},{7,4},{8,9},{9,10},{10,1... | collective-permute-start | bytes 393224 | tf_op jit(solution)/shard_map/ppermute | solution.py:27
  172.2 2.0 collective-permute-done.25
  174.2 1.9 collective-permute-start.27
  176.0 1.3 collective-permute-start.30
  177.3 2.3 %collective-permute-start.31 = (bf16[512,256]{1,0:T(8,128)(2,1)S(1)}, bf16[512,256]{1,0:T(8,128)(2,1)S(1)}, u32[]{:S(2)}, u32[]{:S(2)}) collective-permute-start(bf16[512,256]{1,0:T(8,128)(2,1)S(1)} %pad_maximum_fusion.6), channel_id=1, source_target_pairs={{0,3},{1,0},{2,1},{3,2},{4,7},{5,4},{6,5},{7,6},{8,11},{9,8},{10,9... | collective-permute-start | bytes 786440 | tf_op jit(solution)/shard_map/ppermute | solution.py:27
  179.7 3.4 %collective-permute-done.27 = bf16[256,256]{1,0:T(8,128)(2,1)S(1)} collective-permute-done((bf16[256,256]{1,0:T(8,128)(2,1)S(1)}, bf16[256,256]{1,0:T(8,128)(2,1)S(1)}, u32[]{:S(2)}, u32[]{:S(2)}) %collective-permute-start.27) | collective-permute-done | bytes 131104 | tf_op jit(solution)/shard_map/ppermute | solution.py:27
  183.1 2.9 %convolution_convert_fusion.1 = bf16[512,1024]{1,0:T(8,128)(2,1)S(1)} fusion(bf16[1024,1024]{1,0:T(8,128)(2,1)} %all-gather.5.cloned.1.call-done, bf16[256,256]{1,0:T(8,128)(2,1)S(1)} %collective-permute-done.27, bf16[256,256]{1,0:T(8,128)(2,1)S(1)} %collective-permute-done.26, bf16[512,256]{1,0:T(8,128)(2,1)S(1)} %collective-permute-done.25, ...), kind=kOutput, calls=%fused_computation.4 | convolution fusion | flops 1080557568 | bytes 4194304 | tf_op jit(solution)/shard_map/dot_general | solution.py:289
  186.0 7.4 %collective-permute-done.30 = bf16[512,256]{1,0:T(8,128)(2,1)S(1)} collective-permute-done((bf16[512,256]{1,0:T(8,128)(2,1)S(1)}, bf16[512,256]{1,0:T(8,128)(2,1)S(1)}, u32[]{:S(2)}, u32[]{:S(2)}) %collective-permute-start.30) | collective-permute-done | bytes 262176 | tf_op jit(solution)/shard_map/ppermute | solution.py:27
  194.6 2.6 %collective-permute-start.33 = (bf16[256,256]{1,0:T(8,128)(2,1)S(1)}, bf16[256,256]{1,0:T(8,128)(2,1)S(1)}, u32[]{:S(2)}, u32[]{:S(2)}) collective-permute-start(bf16[256,256]{1,0:T(8,128)(2,1)S(1)} %slice.149), channel_id=1, source_target_pairs={{0,3},{1,0},{2,1},{3,2},{4,7},{5,4},{6,5},{7,6},{8,11},{9,8},{10,9... | collective-permute-start | bytes 393224 | tf_op jit(solution)/shard_map/ppermute | solution.py:27
  197.7 2.7 %collective-permute-done.32 = bf16[256,256]{1,0:T(8,128)(2,1)S(1)} collective-permute-done((bf16[256,256]{1,0:T(8,128)(2,1)S(1)}, bf16[256,256]{1,0:T(8,128)(2,1)S(1)}, u32[]{:S(2)}, u32[]{:S(2)}) %collective-permute-start.32) | collective-permute-done | bytes 131104 | tf_op jit(solution)/shard_map/ppermute | solution.py:27
  200.3 1.9 collective-permute-done.33
  203.6 2.8 %collective-permute-start.34 = (bf16[256,1024]{1,0:T(8,128)(2,1)S(1)}, bf16[256,1024]{1,0:T(8,128)(2,1)S(1)}, u32[]{:S(2)}, u32[]{:S(2)}) collective-permute-start(bf16[256,1024]{1,0:T(8,128)(2,1)S(1)} %slice.150), channel_id=1, source_target_pairs={{0,12},{4,0},{8,4},{12,8},{1,13},{5,1},{9,5},{13,9},{2,14},{6,2},{... | collective-permute-start | bytes 1572872 | tf_op jit(solution)/shard_map/ppermute | solution.py:27
  206.4 4.2 %collective-permute-done.28 = bf16[256,1024]{1,0:T(8,128)(2,1)S(1)} collective-permute-done((bf16[256,1024]{1,0:T(8,128)(2,1)S(1)}, bf16[256,1024]{1,0:T(8,128)(2,1)S(1)}, u32[]{:S(2)}, u32[]{:S(2)}) %collective-permute-start.28) | collective-permute-done | bytes 524320 | tf_op jit(solution)/shard_map/ppermute | solution.py:27
  210.6 12.9 %collective-permute-done.29 = bf16[256,1024]{1,0:T(8,128)(2,1)S(1)} collective-permute-done((bf16[256,1024]{1,0:T(8,128)(2,1)S(1)}, bf16[256,1024]{1,0:T(8,128)(2,1)S(1)}, u32[]{:S(2)}, u32[]{:S(2)}) %collective-permute-start.29) | collective-permute-done | bytes 524320 | tf_op jit(solution)/shard_map/ppermute | solution.py:27
  (115 shorter events, 20.9 us)
Async XLA Ops:
  6.5 81.8 %copy-start = (bf16[64,1024]{1,0:T(8,128)(2,1)S(1)}, bf16[64,1024]{1,0:T(8,128)(2,1)}, u32[]{:S(2)}) copy-start(bf16[64,1024]{1,0:T(8,128)(2,1)} %param.17) | copy-start | bytes 393220
  6.5 104.1 %all-gather.3.cloned.1.call-start = ((), (), s32[]{:S(2)}) async-start(), calls=%async_computation | async-start | bytes 7077888 | tf_op jit(solution)/shard_map/all_gather | solution.py:231
  8.9 17.8 %collective-permute-start = (bf16[352,512]{1,0:T(8,128)(2,1)S(1)}, bf16[352,512]{1,0:T(8,128)(2,1)S(1)}, u32[]{:S(2)}, u32[]{:S(2)}) collective-permute-start(bf16[352,512]{1,0:T(8,128)(2,1)S(1)} %pad_maximum_fusion.3), channel_id=1, source_target_pairs={{0,1},{1,2},{2,3},{3,0},{4,5},{5,6},{6,7},{7,4},{8,9},{9,10},{10,1... | collective-permute-start | bytes 1081352 | tf_op jit(solution)/shard_map/ppermute | solution.py:27
  12.8 23.1 %collective-permute-start.1 = (bf16[352,512]{1,0:T(8,128)(2,1)S(1)}, bf16[352,512]{1,0:T(8,128)(2,1)S(1)}, u32[]{:S(2)}, u32[]{:S(2)}) collective-permute-start(bf16[352,512]{1,0:T(8,128)(2,1)S(1)} %pad_maximum_fusion.4), channel_id=1, source_target_pairs={{0,3},{1,0},{2,1},{3,2},{4,7},{5,4},{6,5},{7,6},{8,11},{9,8},{10,9... | collective-permute-start | bytes 1081352 | tf_op jit(solution)/shard_map/ppermute | solution.py:27
  17.0 38.9 %copy-start.8 = (bf16[256,1024]{1,0:T(8,128)(2,1)}, bf16[256,1024]{1,0:T(8,128)(2,1)S(1)}, u32[]{:S(2)}) copy-start(bf16[256,1024]{1,0:T(8,128)(2,1)S(1)} %constant_dynamic-slice_fusion.5.refs_0_) | copy-start | bytes 1572868
  17.0 18.9 %collective-permute-start.10 = (bf16[256,1024]{1,0:T(8,128)(2,1)S(1)}, bf16[256,1024]{1,0:T(8,128)(2,1)}, u32[]{:S(2)}, u32[]{:S(2)}) collective-permute-start(bf16[256,1024]{1,0:T(8,128)(2,1)S(1)} %constant_dynamic-slice_fusion.5.refs_0_), channel_id=1, source_target_pairs={{0,4},{4,8},{8,12},{12,0},{1,5},{5,9},{9,13},{13,1},{2,6},{6,10},{... | collective-permute-start | bytes 1572872 | tf_op jit(solution)/shard_map/ppermute | solution.py:27
  18.4 17.6 %collective-permute-start.6 = (bf16[256,1024]{1,0:T(8,128)(2,1)S(1)}, bf16[256,1024]{1,0:T(8,128)(2,1)S(1)}, u32[]{:S(2)}, u32[]{:S(2)}) collective-permute-start(bf16[256,1024]{1,0:T(8,128)(2,1)S(1)} %constant_dynamic-slice_fusion.5.refs_0_), channel_id=1, source_target_pairs={{0,12},{4,0},{8,4},{12,8},{1,13},{5,1},{9,5},{13,9},{2,14},{6,2},{... | collective-permute-start | bytes 1572872 | tf_op jit(solution)/shard_map/ppermute | solution.py:27
  19.9 16.0 %collective-permute-start.14 = (bf16[48,1024]{1,0:T(8,128)(2,1)S(1)}, bf16[48,1024]{1,0:T(8,128)(2,1)S(1)}, u32[]{:S(2)}, u32[]{:S(2)}) collective-permute-start(bf16[48,1024]{1,0:T(8,128)(2,1)S(1)} %bitcast.53), channel_id=1, source_target_pairs={{0,2},{1,3},{2,0},{3,1},{4,6},{5,7},{6,4},{7,5},{8,10},{9,11},{10,... | collective-permute-start | bytes 294920 | tf_op jit(solution)/shard_map/ppermute | solution.py:27
  36.0 18.6 %collective-permute-start.15 = (bf16[48,4096]{1,0:T(8,128)(2,1)S(1)}, bf16[48,4096]{1,0:T(8,128)(2,1)S(1)}, u32[]{:S(2)}, u32[]{:S(2)}) collective-permute-start(bf16[48,4096]{1,0:T(8,128)(2,1)S(1)} %constant_dynamic-update-slice_fusion.4), channel_id=1, source_target_pairs={{0,32},{16,48},{32,0},{48,16},{64,96},{80,112},{96,64},{112,80},{1... | collective-permute-start | bytes 1179656 | tf_op jit(solution)/shard_map/ppermute | solution.py:219
  40.7 16.2 %collective-permute-start.2 = (bf16[256,512]{1,0:T(8,128)(2,1)S(1)}, bf16[256,512]{1,0:T(8,128)(2,1)}, u32[]{:S(2)}, u32[]{:S(2)}) collective-permute-start(bf16[256,512]{1,0:T(8,128)(2,1)S(1)} %get-tuple-element.15), channel_id=1, source_target_pairs={{0,3},{1,0},{2,1},{3,2},{4,7},{5,4},{6,5},{7,6},{8,11},{9,8},{10,9... | collective-permute-start | bytes 786440 | tf_op jit(solution)/shard_map/ppermute | solution.py:27
  40.7 19.8 %collective-permute-start.3 = (bf16[256,512]{1,0:T(8,128)(2,1)S(1)}, bf16[256,512]{1,0:T(8,128)(2,1)}, u32[]{:S(2)}, u32[]{:S(2)}) collective-permute-start(bf16[256,512]{1,0:T(8,128)(2,1)S(1)} %get-tuple-element.16), channel_id=1, source_target_pairs={{0,1},{1,2},{2,3},{3,0},{4,5},{5,6},{6,7},{7,4},{8,9},{9,10},{10,1... | collective-permute-start | bytes 786440 | tf_op jit(solution)/shard_map/ppermute | solution.py:27
  43.2 24.3 %copy-start.7 = (bf16[256,1024]{1,0:T(8,128)(2,1)}, bf16[256,1024]{1,0:T(8,128)(2,1)S(1)}, u32[]{:S(2)}) copy-start(bf16[256,1024]{1,0:T(8,128)(2,1)S(1)} %pad_maximum_fusion.1.refs_1_) | copy-start | bytes 1572868
  43.2 23.1 %copy-start.11 = (f32[3,3,256]{2,1,0:T(4,128)S(1)}, f32[3,3,256]{2,1,0:T(4,128)}, u32[]{:S(2)}) copy-start(f32[3,3,256]{2,1,0:T(4,128)} %param.14) | copy-start | bytes 27652
  43.2 23.2 %copy-start.12 = (f32[256]{0:T(256)S(1)}, f32[256]{0:T(256)}, u32[]{:S(2)}) copy-start(f32[256]{0:T(256)} %param.16) | copy-start | bytes 3076
  43.2 17.2 %collective-permute-start.11 = (bf16[256,1024]{1,0:T(8,128)(2,1)S(1)}, bf16[256,1024]{1,0:T(8,128)(2,1)}, u32[]{:S(2)}, u32[]{:S(2)}) collective-permute-start(bf16[256,1024]{1,0:T(8,128)(2,1)S(1)} %pad_maximum_fusion.1.refs_1_), channel_id=1, source_target_pairs={{0,4},{4,8},{8,12},{12,0},{1,5},{5,9},{9,13},{13,1},{2,6},{6,10},{... | collective-permute-start | bytes 1572872 | tf_op jit(solution)/shard_map/ppermute | solution.py:27
  44.6 15.9 %collective-permute-start.7 = (bf16[256,1024]{1,0:T(8,128)(2,1)S(1)}, bf16[256,1024]{1,0:T(8,128)(2,1)}, u32[]{:S(2)}, u32[]{:S(2)}) collective-permute-start(bf16[256,1024]{1,0:T(8,128)(2,1)S(1)} %pad_maximum_fusion.1.refs_1_), channel_id=1, source_target_pairs={{0,12},{4,0},{8,4},{12,8},{1,13},{5,1},{9,5},{13,9},{2,14},{6,2},{... | collective-permute-start | bytes 1572872 | tf_op jit(solution)/shard_map/ppermute | solution.py:27
  54.6 11.6 %collective-permute-start.16 = (bf16[256,1024]{1,0:T(8,128)(2,1)}, bf16[256,1024]{1,0:T(8,128)(2,1)S(1)}, u32[]{:S(2)}, u32[]{:S(2)}) collective-permute-start(bf16[256,1024]{1,0:T(8,128)(2,1)} %collective-permute-done.10.refs_8_), channel_id=1, source_target_pairs={{0,4},{4,8},{8,12},{12,0},{1,5},{5,9},{9,13},{13,1},{2,6},{6,10},{... | collective-permute-start | bytes 1572872 | tf_op jit(solution)/shard_map/ppermute | solution.py:27
  66.2 16.6 %copy-start.3 = (bf16[256,1024]{1,0:T(8,128)(2,1)}, bf16[256,1024]{1,0:T(8,128)(2,1)S(1)}, u32[]{:S(2)}) copy-start(bf16[256,1024]{1,0:T(8,128)(2,1)S(1)} %collective-permute-done.16.refs_0_) | copy-start | bytes 1572868
  66.3 113.4 %all-gather.5.cloned.1.call-start = ((), (), s32[]{:S(2)}) async-start(), calls=%async_computation.1 | async-start | bytes 2228224 | tf_op jit(solution)/shard_map/all_gather | solution.py:272
  67.5 8.3 %collective-permute-start.4 = (bf16[256,512]{1,0:T(8,128)(2,1)S(1)}, bf16[256,512]{1,0:T(8,128)(2,1)S(1)}, u32[]{:S(2)}, u32[]{:S(2)}) collective-permute-start(bf16[256,512]{1,0:T(8,128)(2,1)S(1)} %slice.128), channel_id=1, source_target_pairs={{0,1},{1,2},{2,3},{3,0},{4,5},{5,6},{6,7},{7,4},{8,9},{9,10},{10,1... | collective-permute-start | bytes 786440 | tf_op jit(solution)/shard_map/ppermute | solution.py:27
  67.6 14.0 %collective-permute-start.5 = (bf16[256,512]{1,0:T(8,128)(2,1)S(1)}, bf16[256,512]{1,0:T(8,128)(2,1)S(1)}, u32[]{:S(2)}, u32[]{:S(2)}) collective-permute-start(bf16[256,512]{1,0:T(8,128)(2,1)S(1)} %slice.131), channel_id=1, source_target_pairs={{0,3},{1,0},{2,1},{3,2},{4,7},{5,4},{6,5},{7,6},{8,11},{9,8},{10,9... | collective-permute-start | bytes 786440 | tf_op jit(solution)/shard_map/ppermute | solution.py:27
  73.1 29.2 %copy-start.9 = (bf16[256,1024]{1,0:T(8,128)(2,1)}, bf16[256,1024]{1,0:T(8,128)(2,1)S(1)}, u32[]{:S(2)}) copy-start(bf16[256,1024]{1,0:T(8,128)(2,1)S(1)} %constant_dynamic-update-slice_fusion.refs_2_) | copy-start | bytes 1572868
  73.1 19.5 %collective-permute-start.8 = (bf16[256,1024]{1,0:T(8,128)(2,1)S(1)}, bf16[256,1024]{1,0:T(8,128)(2,1)}, u32[]{:S(2)}, u32[]{:S(2)}) collective-permute-start(bf16[256,1024]{1,0:T(8,128)(2,1)S(1)} %constant_dynamic-update-slice_fusion.refs_2_), channel_id=1, source_target_pairs={{0,12},{4,0},{8,4},{12,8},{1,13},{5,1},{9,5},{13,9},{2,14},{6,2},{... | collective-permute-start | bytes 1572872 | tf_op jit(solution)/shard_map/ppermute | solution.py:27
  82.0 5.6 %collective-permute-start.21 = (f32[144,128]{1,0:T(8,128)S(1)}, f32[144,128]{1,0:T(8,128)S(1)}, u32[]{:S(2)}, u32[]{:S(2)}) collective-permute-start(f32[144,128]{1,0:T(8,128)S(1)} %get-tuple-element.35), channel_id=1, source_target_pairs={{0,1},{1,2},{2,3},{3,0},{4,5},{5,6},{6,7},{7,4},{8,9},{9,10},{10,1... | collective-permute-start | bytes 221192 | tf_op jit(solution)/shard_map/ppermute | solution.py:27
  82.8 27.9 %copy-start.10 = (bf16[256,1024]{1,0:T(8,128)(2,1)}, bf16[256,1024]{1,0:T(8,128)(2,1)S(1)}, u32[]{:S(2)}) copy-start(bf16[256,1024]{1,0:T(8,128)(2,1)S(1)} %constant_dynamic-update-slice_fusion.2.refs_3_) | copy-start | bytes 1572868
  82.8 16.4 %collective-permute-start.9 = (bf16[256,1024]{1,0:T(8,128)(2,1)S(1)}, bf16[256,1024]{1,0:T(8,128)(2,1)}, u32[]{:S(2)}, u32[]{:S(2)}) collective-permute-start(bf16[256,1024]{1,0:T(8,128)(2,1)S(1)} %constant_dynamic-update-slice_fusion.2.refs_3_), channel_id=1, source_target_pairs={{0,12},{4,0},{8,4},{12,8},{1,13},{5,1},{9,5},{13,9},{2,14},{6,2},{... | collective-permute-start | bytes 1572872 | tf_op jit(solution)/shard_map/ppermute | solution.py:27
  84.3 18.0 %collective-permute-start.12 = (bf16[256,1024]{1,0:T(8,128)(2,1)S(1)}, bf16[256,1024]{1,0:T(8,128)(2,1)}, u32[]{:S(2)}, u32[]{:S(2)}) collective-permute-start(bf16[256,1024]{1,0:T(8,128)(2,1)S(1)} %constant_dynamic-update-slice_fusion.refs_2_), channel_id=1, source_target_pairs={{0,4},{4,8},{8,12},{12,0},{1,5},{5,9},{9,13},{13,1},{2,6},{6,10},{... | collective-permute-start | bytes 1572872 | tf_op jit(solution)/shard_map/ppermute | solution.py:27
  84.5 20.4 %collective-permute-start.13 = (bf16[256,1024]{1,0:T(8,128)(2,1)S(1)}, bf16[256,1024]{1,0:T(8,128)(2,1)}, u32[]{:S(2)}, u32[]{:S(2)}) collective-permute-start(bf16[256,1024]{1,0:T(8,128)(2,1)S(1)} %constant_dynamic-update-slice_fusion.2.refs_3_), channel_id=1, source_target_pairs={{0,4},{4,8},{8,12},{12,0},{1,5},{5,9},{9,13},{13,1},{2,6},{6,10},{... | collective-permute-start | bytes 1572872 | tf_op jit(solution)/shard_map/ppermute | solution.py:27
  87.6 4.5 %collective-permute-start.22 = (f32[144,128]{1,0:T(8,128)S(1)}, f32[144,128]{1,0:T(8,128)S(1)}, u32[]{:S(2)}, u32[]{:S(2)}) collective-permute-start(f32[144,128]{1,0:T(8,128)S(1)} %get-tuple-element.34), channel_id=1, source_target_pairs={{0,3},{1,0},{2,1},{3,2},{4,7},{5,4},{6,5},{7,6},{8,11},{9,8},{10,9... | collective-permute-start | bytes 221192 | tf_op jit(solution)/shard_map/ppermute | solution.py:27
  92.1 7.1 %collective-permute-start.23 = (f32[144,128]{1,0:T(8,128)S(1)}, f32[144,128]{1,0:T(8,128)S(1)}, u32[]{:S(2)}, u32[]{:S(2)}) collective-permute-start(f32[144,128]{1,0:T(8,128)S(1)} %get-tuple-element.33), channel_id=1, source_target_pairs={{0,2},{1,3},{2,0},{3,1},{4,6},{5,7},{6,4},{7,5},{8,10},{9,11},{10,... | collective-permute-start | bytes 221192 | tf_op jit(solution)/shard_map/ppermute | solution.py:27
  92.6 32.8 %collective-permute-start.18 = (bf16[256,1024]{1,0:T(8,128)(2,1)}, bf16[256,1024]{1,0:T(8,128)(2,1)S(1)}, u32[]{:S(2)}, u32[]{:S(2)}) collective-permute-start(bf16[256,1024]{1,0:T(8,128)(2,1)} %collective-permute-done.8.refs_6_), channel_id=1, source_target_pairs={{0,12},{4,0},{8,4},{12,8},{1,13},{5,1},{9,5},{13,9},{2,14},{6,2},{... | collective-permute-start | bytes 1572872 | tf_op jit(solution)/shard_map/ppermute | solution.py:27
  99.2 26.2 %collective-permute-start.17 = (bf16[256,1024]{1,0:T(8,128)(2,1)}, bf16[256,1024]{1,0:T(8,128)(2,1)S(1)}, u32[]{:S(2)}, u32[]{:S(2)}) collective-permute-start(bf16[256,1024]{1,0:T(8,128)(2,1)} %collective-permute-done.11.refs_9_), channel_id=1, source_target_pairs={{0,4},{4,8},{8,12},{12,0},{1,5},{5,9},{9,13},{13,1},{2,6},{6,10},{... | collective-permute-start | bytes 1572872 | tf_op jit(solution)/shard_map/ppermute | solution.py:27
  99.2 26.2 %collective-permute-start.19 = (bf16[256,1024]{1,0:T(8,128)(2,1)}, bf16[256,1024]{1,0:T(8,128)(2,1)S(1)}, u32[]{:S(2)}, u32[]{:S(2)}) collective-permute-start(bf16[256,1024]{1,0:T(8,128)(2,1)} %collective-permute-done.9.refs_7_), channel_id=1, source_target_pairs={{0,12},{4,0},{8,4},{12,8},{1,13},{5,1},{9,5},{13,9},{2,14},{6,2},{... | collective-permute-start | bytes 1572872 | tf_op jit(solution)/shard_map/ppermute | solution.py:27
  125.4 10.1 %copy-start.2 = (bf16[3,768,256]{2,1,0:T(8,128)(2,1)S(1)}, bf16[3,768,256]{2,1,0:T(8,128)(2,1)}, u32[]{:S(2)}) copy-start(bf16[3,768,256]{2,1,0:T(8,128)(2,1)} %project.2.near_ref) | copy-start | bytes 3538948
  134.4 7.2 %copy-start.1 = (bf16[3,256,256]{2,1,0:T(8,128)(2,1)S(1)}, bf16[3,256,256]{2,1,0:T(8,128)(2,1)}, u32[]{:S(2)}) copy-start(bf16[3,256,256]{2,1,0:T(8,128)(2,1)} %project.3.far_ref) | copy-start | bytes 1179652
  135.7 13.8 %collective-permute-start.20 = (bf16[3,144,256]{2,1,0:T(8,128)(2,1)S(1)}, bf16[3,144,256]{2,1,0:T(8,128)(2,1)S(1)}, u32[]{:S(2)}, u32[]{:S(2)}) collective-permute-start(bf16[3,144,256]{2,1,0:T(8,128)(2,1)S(1)} %fusion.44.halo_ref), channel_id=1, source_target_pairs={{0,16},{16,32},{32,48},{48,64},{64,80},{80,96},{96,112},{112,128},... | collective-permute-start | bytes 663560 | tf_op jit(solution)/shard_map/ppermute | solution.py:276
  157.6 11.7 %collective-permute-start.24 = (bf16[512,256]{1,0:T(8,128)(2,1)S(1)}, bf16[512,256]{1,0:T(8,128)(2,1)S(1)}, u32[]{:S(2)}, u32[]{:S(2)}) collective-permute-start(bf16[512,256]{1,0:T(8,128)(2,1)S(1)} %pad_maximum_fusion.5), channel_id=1, source_target_pairs={{0,1},{1,2},{2,3},{3,0},{4,5},{5,6},{6,7},{7,4},{8,9},{9,10},{10,1... | collective-permute-start | bytes 786440 | tf_op jit(solution)/shard_map/ppermute | solution.py:27
  159.6 14.5 %collective-permute-start.25 = (bf16[512,256]{1,0:T(8,128)(2,1)S(1)}, bf16[512,256]{1,0:T(8,128)(2,1)S(1)}, u32[]{:S(2)}, u32[]{:S(2)}) collective-permute-start(bf16[512,256]{1,0:T(8,128)(2,1)S(1)} %pad_maximum_fusion.5), channel_id=1, source_target_pairs={{0,3},{1,0},{2,1},{3,2},{4,7},{5,4},{6,5},{7,6},{8,11},{9,8},{10,9... | collective-permute-start | bytes 786440 | tf_op jit(solution)/shard_map/ppermute | solution.py:27
  169.3 10.4 %collective-permute-start.26 = (bf16[256,256]{1,0:T(8,128)(2,1)S(1)}, bf16[256,256]{1,0:T(8,128)(2,1)S(1)}, u32[]{:S(2)}, u32[]{:S(2)}) collective-permute-start(bf16[256,256]{1,0:T(8,128)(2,1)S(1)} %slice.144), channel_id=1, source_target_pairs={{0,1},{1,2},{2,3},{3,0},{4,5},{5,6},{6,7},{7,4},{8,9},{9,10},{10,1... | collective-permute-start | bytes 393224 | tf_op jit(solution)/shard_map/ppermute | solution.py:27
  174.2 8.9 %collective-permute-start.27 = (bf16[256,256]{1,0:T(8,128)(2,1)S(1)}, bf16[256,256]{1,0:T(8,128)(2,1)S(1)}, u32[]{:S(2)}, u32[]{:S(2)}) collective-permute-start(bf16[256,256]{1,0:T(8,128)(2,1)S(1)} %slice.145), channel_id=1, source_target_pairs={{0,3},{1,0},{2,1},{3,2},{4,7},{5,4},{6,5},{7,6},{8,11},{9,8},{10,9... | collective-permute-start | bytes 393224 | tf_op jit(solution)/shard_map/ppermute | solution.py:27
  176.0 17.4 %collective-permute-start.30 = (bf16[512,256]{1,0:T(8,128)(2,1)S(1)}, bf16[512,256]{1,0:T(8,128)(2,1)S(1)}, u32[]{:S(2)}, u32[]{:S(2)}) collective-permute-start(bf16[512,256]{1,0:T(8,128)(2,1)S(1)} %pad_maximum_fusion.6), channel_id=1, source_target_pairs={{0,1},{1,2},{2,3},{3,0},{4,5},{5,6},{6,7},{7,4},{8,9},{9,10},{10,1... | collective-permute-start | bytes 786440 | tf_op jit(solution)/shard_map/ppermute | solution.py:27
  177.3 17.2 %collective-permute-start.31 = (bf16[512,256]{1,0:T(8,128)(2,1)S(1)}, bf16[512,256]{1,0:T(8,128)(2,1)S(1)}, u32[]{:S(2)}, u32[]{:S(2)}) collective-permute-start(bf16[512,256]{1,0:T(8,128)(2,1)S(1)} %pad_maximum_fusion.6), channel_id=1, source_target_pairs={{0,3},{1,0},{2,1},{3,2},{4,7},{5,4},{6,5},{7,6},{8,11},{9,8},{10,9... | collective-permute-start | bytes 786440 | tf_op jit(solution)/shard_map/ppermute | solution.py:27
  186.0 16.3 %copy-start.13 = (bf16[1024,1024]{1,0:T(8,128)(2,1)S(1)}, bf16[1024,1024]{1,0:T(8,128)(2,1)}, u32[]{:S(2)}) copy-start(bf16[1024,1024]{1,0:T(8,128)(2,1)} %all-gather.5.cloned.1.call-done) | copy-start | bytes 6291460
  193.4 6.9 %collective-permute-start.32 = (bf16[256,256]{1,0:T(8,128)(2,1)S(1)}, bf16[256,256]{1,0:T(8,128)(2,1)S(1)}, u32[]{:S(2)}, u32[]{:S(2)}) collective-permute-start(bf16[256,256]{1,0:T(8,128)(2,1)S(1)} %slice.148), channel_id=1, source_target_pairs={{0,1},{1,2},{2,3},{3,0},{4,5},{5,6},{6,7},{7,4},{8,9},{9,10},{10,1... | collective-permute-start | bytes 393224 | tf_op jit(solution)/shard_map/ppermute | solution.py:27
  194.6 7.6 %collective-permute-start.33 = (bf16[256,256]{1,0:T(8,128)(2,1)S(1)}, bf16[256,256]{1,0:T(8,128)(2,1)S(1)}, u32[]{:S(2)}, u32[]{:S(2)}) collective-permute-start(bf16[256,256]{1,0:T(8,128)(2,1)S(1)} %slice.149), channel_id=1, source_target_pairs={{0,3},{1,0},{2,1},{3,2},{4,7},{5,4},{6,5},{7,6},{8,11},{9,8},{10,9... | collective-permute-start | bytes 393224 | tf_op jit(solution)/shard_map/ppermute | solution.py:27
  197.2 13.3 %collective-permute-start.28 = (bf16[256,1024]{1,0:T(8,128)(2,1)S(1)}, bf16[256,1024]{1,0:T(8,128)(2,1)S(1)}, u32[]{:S(2)}, u32[]{:S(2)}) collective-permute-start(bf16[256,1024]{1,0:T(8,128)(2,1)S(1)} %get-tuple-element.20), channel_id=1, source_target_pairs={{0,8},{4,12},{8,0},{12,4},{1,9},{5,13},{9,1},{13,5},{2,10},{6,14},... | collective-permute-start | bytes 1572872 | tf_op jit(solution)/shard_map/ppermute | solution.py:27
  197.3 26.2 %collective-permute-start.29 = (bf16[256,1024]{1,0:T(8,128)(2,1)S(1)}, bf16[256,1024]{1,0:T(8,128)(2,1)S(1)}, u32[]{:S(2)}, u32[]{:S(2)}) collective-permute-start(bf16[256,1024]{1,0:T(8,128)(2,1)S(1)} %get-tuple-element.21), channel_id=1, source_target_pairs={{0,4},{4,8},{8,12},{12,0},{1,5},{5,9},{9,13},{13,1},{2,6},{6,10},{... | collective-permute-start | bytes 1572872 | tf_op jit(solution)/shard_map/ppermute | solution.py:27
  203.6 19.9 %collective-permute-start.34 = (bf16[256,1024]{1,0:T(8,128)(2,1)S(1)}, bf16[256,1024]{1,0:T(8,128)(2,1)S(1)}, u32[]{:S(2)}, u32[]{:S(2)}) collective-permute-start(bf16[256,1024]{1,0:T(8,128)(2,1)S(1)} %slice.150), channel_id=1, source_target_pairs={{0,12},{4,0},{8,4},{12,8},{1,13},{5,1},{9,5},{13,9},{2,14},{6,2},{... | collective-permute-start | bytes 1572872 | tf_op jit(solution)/shard_map/ppermute | solution.py:27
  (4 other events, 7.3 us)
Sparse Core Ops, SparseCore 0:
  66.4 44.2 all-gather.2
  112.5 37.0 all-gather.4

commit v3 on v2

--- a/solution.py
+++ b/solution.py
@@ -27,71 +27,74 @@
     return lax.ppermute(x, axis, ring(4, step))
 
 
-def project_kernel(count, *refs):
-    pieces, w_hbm, out_ref, x, w, scale_ref, x_sems, w_sems = refs[: 4 * count], *refs[4 * count :]
-    x_copies = [pltpu.make_async_copy(piece, x.at[i], x_sems.at[i]) for i, piece in enumerate(pieces)]
-    w_copies = [pltpu.make_async_copy(w_hbm.at[i], w.at[i], w_sems.at[i]) for i in range(16)]
-    for copy in x_copies + w_copies:
+TOKENS = 4 * Q
+
+
+def project_kernel(quarters, row_ref, act_hbm, *refs):
+    count = len(quarters)
+    pieces, w_hbm, out_ref, x, w, scale_ref, x_sems, w_sems = refs[: 3 * count], *refs[3 * count :]
+    row = row_ref[0]
+    x_copies = []
+    for s, quarter in enumerate(quarters):
+        own = pl.ds(pl.multiple_of(lax.rem(row + quarter, 4) * Q, Q), Q)
+        for b, source in enumerate([act_hbm.at[own, :], *pieces[3 * s : 3 * s + 3]]):
+            x_copies.append(
+                pltpu.make_async_copy(source, x.at[pl.ds(Q * s, Q), pl.ds(F * b, F)], x_sems.at[4 * s + b])
+            )
+
+    def w_copies(p):
+        return [
+            pltpu.make_async_copy(w_hbm.at[i, p], w.at[p, pl.ds(16 * i, 16), :], w_sems.at[p, i]) for i in range(16)
+        ]
+
+    for copy in x_copies + w_copies(0) + w_copies(1) + w_copies(2):
         copy.start()
     rows = 64
     for s in range(count):
         for copy in x_copies[4 * s : 4 * s + 4]:
             copy.wait()
 
-    @pl.loop(0, count * (Q // rows))
-    def _(i):
-        s = i // (Q // rows)
-        at = pl.ds(pl.multiple_of(lax.rem(i, Q // rows) * rows, rows), rows)
-        squares = None
-        for b in range(4):
-            values = x[4 * s + b, at, :].astype(f32)
-            part = jnp.sum(values * values, axis=1, keepdims=True)
-            squares = part if squares is None else squares + part
-        scale_ref[s, at, :] = jnp.broadcast_to(lax.rsqrt(squares / D + epsilon), (rows, 128))
-
-    for copy in w_copies:
-        copy.wait()
-
-    @pl.loop(0, 3 * count)
-    def _(i):
-        p, s = i // count, lax.rem(i, count)
-        total = None
-        for b in range(4):
-            part = lax.dot_general(
-                x[4 * s + b],
-                w[:, p, :, F * b : F * b + F].reshape(CH, F),
-                (((1,), (1,)), ((), ())),
-                preferred_element_type=f32,
-            )
-            total = part if total is None else total + part
-        scale = scale_ref[s]
+        @pl.loop(Q * s // rows, Q * (s + 1) // rows)
+        def _(i):
+            at = pl.ds(pl.multiple_of(i * rows, rows), rows)
+            squares = None
+            for b in range(4):
+                values = x[at, F * b : F * b + F].astype(f32)
+                part = jnp.sum(values * values, axis=1, keepdims=True)
+                squares = part if squares is None else squares + part
+            scale_ref[at, :] = jnp.broadcast_to(lax.rsqrt(squares / D + epsilon), (rows, 128))
+
+    @pl.loop(0, 3)
+    def _(p):
+        for copy in w_copies(p):
+            copy.wait()
+        total = lax.dot_general(x[...], w[p], (((1,), (1,)), ((), ())), preferred_element_type=f32)
+        scale = scale_ref[...]
         for lanes in (slice(0, 128), slice(128, 256)):
-            out_ref[p, pl.ds(pl.multiple_of(s * Q, Q), Q), lanes] = (total[:, lanes] * scale).astype(bf16)
-
-
-def project(pieces, w):
-    count = len(pieces) // 4
+            out_ref[p, :, lanes] = (total[:, lanes] * scale).astype(bf16)
+
+
+def project(row, quarters, activations, pieces, w):
+    count = len(quarters)
     anywhere = pl.BlockSpec(memory_space=pl.ANY)
     return pl.pallas_call(
-        functools.partial(project_kernel, count),
-        in_specs=[anywhere] * (4 * count + 1),
+        functools.partial(project_kernel, quarters),
+        in_specs=[pl.BlockSpec(memory_space=pltpu.SMEM)] + [anywhere] * (3 * count + 2),
         out_specs=pl.BlockSpec(memory_space=pltpu.VMEM),
         out_shape=jax.ShapeDtypeStruct((3, count * Q, CH), bf16),
         scratch_shapes=[
-            pltpu.VMEM((4 * count, Q, F), bf16),
-            pltpu.VMEM((16, 3, 16, D), bf16),
-            pltpu.VMEM((count, Q, 128), f32),
+            pltpu.VMEM((count * Q, D), bf16),
+            pltpu.VMEM((3, CH, D), bf16),
+            pltpu.VMEM((count * Q, 128), f32),
             pltpu.SemaphoreType.DMA((4 * count,)),
-            pltpu.SemaphoreType.DMA((16,)),
+            pltpu.SemaphoreType.DMA((3, 16)),
         ],
         compiler_params=pltpu.CompilerParams(vmem_limit_bytes=56 << 20),
         cost_estimate=pl.CostEstimate(
-            flops=2 * count * Q * 3 * CH * D,
-            bytes_accessed=2 * (count * Q * D + 3 * CH * D),
-            transcendentals=0,
+            flops=4_000_000_000 * count, bytes_accessed=2 * (count * Q * D + 3 * CH * D), transcendentals=0
         ),
         name="project",
-    )(*pieces, w)
+    )(row, activations, *pieces, w)
 
 
 HALF = 512
@@ -204,70 +207,66 @@
     def payload(x, w):
         return jnp.concatenate([x, w[:, :HF], w[:, HF:]], axis=0)
 
-    own_from_before = shift(own, "row", 1)
-    own_from_after = shift(own, "row", -1)
     up = shift(payload(own[:, :HF], group(order[2])), "col", 1)
     down = shift(payload(own[:, HF:], group(order[1])), "col", -1)
     w_far = shift(group(order[3]), "col", 2)
-    w_up = (up[Q : Q + 48], up[Q + 48 :])
-    w_down = (down[Q : Q + 48], down[Q + 48 :])
     w_rows = jnp.concatenate(
-        [group(order[0]), w_up[0], w_down[1], w_down[0], w_up[1], w_far], axis=1
+        [group(order[0]), up[Q : Q + 48], down[Q + 48 :], down[Q : Q + 48], up[Q + 48 :], w_far], axis=1
     )
-    w_rows = after(w_rows, own_from_before, own_from_after)
+    up, down = up[:Q], down[:Q]
     low_z = (lax.axis_index("ctx") // 2) % 2 == 0
     w_other = lax.ppermute(w_rows, "ctx", [(i, i ^ 2) for i in range(16)])
-
-    mixed_up = jnp.concatenate([up[:Q], down[:Q]], axis=1)
+    w_pair = jnp.concatenate([jnp.where(low_z, w_rows, w_other), jnp.where(low_z, w_other, w_rows)], axis=0)
+    mixed_up = jnp.concatenate([up, down], axis=1)
     up_from_before = shift(mixed_up, "row", 1)
     up_from_after = shift(mixed_up, "row", -1)
-
-    w_pair = jnp.concatenate([jnp.where(low_z, w_rows, w_other), jnp.where(low_z, w_other, w_rows)], axis=0)
-    rest_up = shift(own[:, HF:], "col", 1)
-    rest_down = shift(own[:, :HF], "col", -1)
-    far_own = shift(own_from_before, "row", 1)
-    w_pair = after(w_pair, up_from_before, up_from_after, rest_up, rest_down, far_own)
+    rest = after(own, up, down)
+    rest_up = shift(rest[:, HF:], "col", 1)
+    rest_down = shift(rest[:, :HF], "col", -1)
+    w_pair = after(w_pair, up_from_before, up_from_after, rest_up, rest_down)
     groups = [[4 * x + 2 * z + core for x in range(4) for core in range(2)] for z in range(2)]
     w_all = lax.all_gather(w_pair, "ctx", axis=0, tiled=True, axis_index_groups=groups).reshape(16, 3, 16, D)
 
-    far_up = shift(up[:Q], "col", 1)
-    far_down = shift(down[:Q], "col", -1)
-    own = [
-        own,
-        mixed_up,
-        jnp.concatenate([rest_down, rest_up], axis=1),
-        jnp.concatenate([far_up, far_down], axis=1),
-    ]
-    from_before = [own_from_before, up_from_before] + [shift(x, "row", 1) for x in own[2:]]
-    from_after = [own_from_after, up_from_after] + [shift(x, "row", -1) for x in own[2:]]
-    far = [far_own, shift(up_from_before, "row", 1)] + [shift(x, "row", -1) for x in from_after[2:]]
-    near_out = project(own + from_after + from_before, w_all)
-    far_out = project([after(far[0], near_out)] + far[1:], w_all)
-
+    mixed_rest = jnp.concatenate([rest_down, rest_up], axis=1)
+    up, down = after((up, down), rest_up, rest_down)
+    far_up = shift(up, "col", 1)
+    far_down = shift(down, "col", -1)
+    from_before = [up_from_before, shift(mixed_rest, "row", 1)]
+    from_after = [up_from_after, shift(mixed_rest, "row", -1)]
+    mixed_far = after(jnp.concatenate([far_up, far_down], axis=1), from_before[1], from_after[1])
+    from_before.append(shift(mixed_far, "row", 1))
+    from_after.append(shift(mixed_far, "row", -1))
+    own = [mixed_up, mixed_rest, mixed_far]
+    far = [shift(from_before[0], "row", 1), shift(from_after[1], "row", -1)]
+    far += [shift(from_before[2][:, :HF], "row", 1), shift(from_after[2][:, HF:], "row", -1)]
+    near_out = project(row[None], (0, 1, 3), activations, own + from_after + from_before, w_all)
     small = jnp.concatenate(
         [short_taps.reshape(9, CH), long_taps, skip_gain[None], jnp.zeros((6, CH), f32)], axis=0
     )
-    small = after(small, far_up, far_down)
+    small = after(small, mixed_far)
     v = jnp.arange(512)
     wanted = shard_of(v % 128 // 16) * 64 + order[v // 128] * 16 + v % 16
     pick = ((jnp.arange(CH)[:, None] == wanted[None, :]) & (v % 128 < 64)[None, :]).astype(f32)
     small = jnp.dot(small, pick, precision=lax.Precision.HIGHEST)
-    small = jnp.concatenate(
-        [
-            small[:, :128],
-            shift(small[:, 256:384], "col", 1),
-            shift(small[:, 128:256], "col", -1),
-            shift(small[:, 384:], "col", 2),
-        ],
-        axis=1,
-    )
+    small = [
+        small[:, :128],
+        shift(small[:, 256:384], "col", 1),
+        shift(small[:, 128:256], "col", -1),
+        shift(small[:, 384:], "col", 2),
+    ]
+    far = after(far, near_out)
+    far = far[:2] + [jnp.concatenate(far[2:], axis=1)]
+    far_out = project(row[None], (2,), activations, far, w_all)
+
+    small = after(small, near_out)
     place = ((order[v // 128] * 64 + v % 128)[:, None] == jnp.arange(CH)[None, :]) & (v % 128 < 64)[:, None]
-    taps = jnp.dot(small, place.astype(f32), precision=lax.Precision.HIGHEST)
+    taps = jnp.dot(jnp.concatenate(small, axis=1), place.astype(f32), precision=lax.Precision.HIGHEST)
 
     m = jnp.arange(F)
     blocks = order[m // 256]
     wanted_out = shard_of((m % 256) // 16) * 64 + blocks * 16 + m % 16
     pick_out = (jnp.arange(F)[:, None] == wanted_out[None, :]).astype(bf16)
+    w_out = after(w_out, from_before[2])
     out_rows = jnp.dot(w_out, pick_out, preferred_element_type=f32).astype(bf16)
     out_all = lax.all_gather(out_rows, "ctx", axis=0, tiled=True)
 
@@ -282,19 +281,31 @@
     def quarter(s):
         return lax.dynamic_index_in_dim(mixed, (row + s) % 4, 0, keepdims=False)
 
-    first = gather_col(jnp.concatenate([quarter(2), quarter(1)], axis=0))
-    second = gather_col(after(jnp.concatenate([quarter(3), quarter(0)], axis=0), first[1], first[2]))
+    mid = Q // 2
+    opposite, above, below = quarter(2), quarter(1), quarter(3)
+    first = gather_col(jnp.concatenate([opposite, above[:mid], below[mid:]], axis=0))
+    second = jnp.concatenate([above[mid:], below[:mid], quarter(0)], axis=0)
+    second = gather_col(after(second, first[1], first[2]))
 
     def outputs(gathered):
         return lax.dot_general(
             jnp.concatenate(gathered, axis=1), out_all, (((1,), (1,)), ((), ())), preferred_element_type=f32
         ).astype(bf16)
 
+    def add(a, b):
+        return (a.astype(f32) + b.astype(f32)).astype(bf16)
+
     part = outputs(first)
-    got = [shift(part[:Q], "row", 2), shift(part[Q:], "row", 1)]
+    opposite_lo = shift(part[:mid], "row", 1)
+    opposite_hi = shift(part[mid:Q], "row", -1)
+    up_lo = shift(add(part[Q : Q + mid], opposite_lo), "row", 1)
+    down_hi = shift(add(part[Q + mid :], opposite_hi), "row", -1)
     part = outputs(second)
-    got += [shift(part[:Q], "row", -1), part[Q:]]
-    return sum(g.astype(f32) for g in got).astype(bf16)
+    up_hi = shift(part[:mid], "row", 1)
+    down_lo = shift(part[mid:Q], "row", -1)
+    up = jnp.concatenate([up_lo, up_hi], axis=0)
+    down = jnp.concatenate([down_lo, down_hi], axis=0)
+    return (part[Q:].astype(f32) + up.astype(f32) + down.astype(f32)).astype(bf16)
 
 
 def solution(mesh):

time: 232 us -> 226 us (0.974); the launches traced: 232 us -> 222 us
  waiting for transfers between devices: 97.2 us -> 70.2 us
  starting transfers between devices: 64 us -> 85.5 us
  local copies, waits for them, and re-layouts: 7.39 us -> 4.42 us
    ppermute x33 -> x34, starting transfers between devices: 53.3 us -> 77.2 us  [shift(): return lax.ppermute(x, axis, ring(4, step))]
    ppermute x33 -> x34, waiting for transfers between devices: 82.9 us -> 60.4 us  [shift(): return lax.ppermute(x, axis, ring(4, step))]
    ppermute x1, waiting for transfers between devices: 8.47 us -> 4.32 us  [on_device(): w_other = lax.ppermute(w_rows, 'ctx', [(i, i ^ 2) for i in range(16)])]
    ppermute x1, starting transfers between devices: 5.91 us -> 3.5 us  [on_device(): halo = lax.ppermute(tail, 'ctx', [(i, i + 1) for i in range(15)])]
  transfers between devices with their start and end apart: 37 -> 38, of which waited for: 21 -> 17; matrix products, arithmetic and copies ran while one was open for 6% -> 5% of each run, Pallas kernels for 16% -> 16%
where the time goes in v3:
time: 226 us; the launch traced here: 222 us
  starting transfers between devices  85.5 us (38%)
  waiting for transfers between devices  70.2 us (31%)
  Pallas kernels  36.1 us (16%)
  between operations  14.3 us (6%)
  matrix products  6.5 us (3%)
  other arithmetic  4.84 us (2%)
  local copies, waits for them, and re-layouts  4.42 us (2%)
    ppermute x34, starting transfers between devices, shift(): return lax.ppermute(x, axis, ring(4, step))  77.2 us
    ppermute x34, waiting for transfers between devices, shift(): return lax.ppermute(x, axis, ring(4, step))  60.4 us
    pallas_call x2, Pallas kernels, project(): pl.pallas_call(functools.partial(project_kernel, quarters), in_specs=[pl....  20.3 us
    pallas_call x2, Pallas kernels, mix(): pl.pallas_call(functools.partial(mix_kernel, first), in_specs=[pl.BlockSp...  15.8 us
    all_gather x1, waiting for transfers between devices, on_device(): lax.all_gather(w_pair, 'ctx', axis=0, tiled=True, axis_index_groups=groups)  5.44 us
    ppermute x1, starting transfers between devices, on_device(): w_other = lax.ppermute(w_rows, 'ctx', [(i, i ^ 2) for i in range(16)])  4.73 us
  transfers between devices with their start and end apart: 38, of which 17 were waited for; matrix products, arithmetic and copies ran while one was open for 5% of the time, Pallas kernels for 16%

profile of v3, /device:TPU:1, one launch (start us, length us, event | category | flops | bytes accessed | tf_op | source)
XLA Modules:
  0.0 221.9 jit_solution(17532980128443377178)
XLA Ops:
  8.9 3.9 %collective-permute-start = (bf16[352,512]{1,0:T(8,128)(2,1)S(1)}, bf16[352,512]{1,0:T(8,128)(2,1)S(1)}, u32[]{:S(2)}, u32[]{:S(2)}) collective-permute-start(bf16[352,512]{1,0:T(8,128)(2,1)S(1)} %pad_maximum_fusion.5), channel_id=1, source_target_pairs={{0,1},{1,2},{2,3},{3,0},{4,5},{5,6},{6,7},{7,4},{8,9},{9,10},{10,1... | collective-permute-start | bytes 1081352 | tf_op jit(solution)/shard_map/ppermute | solution.py:27
  12.8 3.1 %collective-permute-start.1 = (bf16[352,512]{1,0:T(8,128)(2,1)S(1)}, bf16[352,512]{1,0:T(8,128)(2,1)S(1)}, u32[]{:S(2)}, u32[]{:S(2)}) collective-permute-start(bf16[352,512]{1,0:T(8,128)(2,1)S(1)} %pad_maximum_fusion.6), channel_id=1, source_target_pairs={{0,3},{1,0},{2,1},{3,2},{4,7},{5,4},{6,5},{7,6},{8,11},{9,8},{10,9... | collective-permute-start | bytes 1081352 | tf_op jit(solution)/shard_map/ppermute | solution.py:27
  15.9 4.4 %collective-permute-start.12 = (bf16[48,1024]{1,0:T(8,128)(2,1)S(1)}, bf16[48,1024]{1,0:T(8,128)(2,1)S(1)}, u32[]{:S(2)}, u32[]{:S(2)}) collective-permute-start(bf16[48,1024]{1,0:T(8,128)(2,1)S(1)} %bitcast.54), channel_id=1, source_target_pairs={{0,2},{1,3},{2,0},{3,1},{4,6},{5,7},{6,4},{7,5},{8,10},{9,11},{10,... | collective-permute-start | bytes 294920 | tf_op jit(solution)/shard_map/ppermute | solution.py:27
  20.4 6.2 %collective-permute-done = bf16[352,512]{1,0:T(8,128)(2,1)S(1)} collective-permute-done((bf16[352,512]{1,0:T(8,128)(2,1)S(1)}, bf16[352,512]{1,0:T(8,128)(2,1)S(1)}, u32[]{:S(2)}, u32[]{:S(2)}) %collective-permute-start) | collective-permute-done | bytes 360480 | tf_op jit(solution)/shard_map/ppermute | solution.py:27
  26.6 9.3 %collective-permute-done.1 = bf16[352,512]{1,0:T(8,128)(2,1)S(1)} collective-permute-done((bf16[352,512]{1,0:T(8,128)(2,1)S(1)}, bf16[352,512]{1,0:T(8,128)(2,1)S(1)}, u32[]{:S(2)}, u32[]{:S(2)}) %collective-permute-start.1) | collective-permute-done | bytes 360480 | tf_op jit(solution)/shard_map/ppermute | solution.py:27
  36.0 4.7 %collective-permute-start.13 = (bf16[48,4096]{1,0:T(8,128)(2,1)S(1)}, bf16[48,4096]{1,0:T(8,128)(2,1)S(1)}, u32[]{:S(2)}, u32[]{:S(2)}) collective-permute-start(bf16[48,4096]{1,0:T(8,128)(2,1)S(1)} %constant_dynamic-update-slice_fusion.2), channel_id=1, source_target_pairs={{0,32},{16,48},{32,0},{48,16},{64,96},{80,112},{96,64},{112,80},{1... | collective-permute-start | bytes 1179656 | tf_op jit(solution)/shard_map/ppermute | solution.py:218
  41.9 1.4 collective-permute-start.10
  43.3 1.5 collective-permute-start.8
  45.0 2.4 %collective-permute-start.3 = (bf16[256,512]{1,0:T(8,128)(2,1)S(1)}, bf16[256,512]{1,0:T(8,128)(2,1)S(1)}, u32[]{:S(2)}, u32[]{:S(2)}) collective-permute-start(bf16[256,512]{1,0:T(8,128)(2,1)S(1)} %get-tuple-element.57), channel_id=1, source_target_pairs={{0,1},{1,2},{2,3},{3,0},{4,5},{5,6},{6,7},{7,4},{8,9},{9,10},{10,1... | collective-permute-start | bytes 786440 | tf_op jit(solution)/shard_map/ppermute | solution.py:27
  47.3 4.3 %collective-permute-done.13 = bf16[48,4096]{1,0:T(8,128)(2,1)S(1)} collective-permute-done((bf16[48,4096]{1,0:T(8,128)(2,1)S(1)}, bf16[48,4096]{1,0:T(8,128)(2,1)S(1)}, u32[]{:S(2)}, u32[]{:S(2)}) %collective-permute-start.13) | collective-permute-done | bytes 393248 | tf_op jit(solution)/shard_map/ppermute | solution.py:218
  52.7 7.9 %collective-permute-done.3 = bf16[256,512]{1,0:T(8,128)(2,1)S(1)} collective-permute-done((bf16[256,512]{1,0:T(8,128)(2,1)S(1)}, bf16[256,512]{1,0:T(8,128)(2,1)S(1)}, u32[]{:S(2)}, u32[]{:S(2)}) %collective-permute-start.3) | collective-permute-done | bytes 262176 | tf_op jit(solution)/shard_map/ppermute | solution.py:27
  62.0 1.6 collective-permute-start.7
  63.6 1.7 collective-permute-start.4
  65.3 1.8 collective-permute-start.5
  67.3 7.0 %collective-permute-done.4 = bf16[256,512]{1,0:T(8,128)(2,1)S(1)} collective-permute-done((bf16[256,512]{1,0:T(8,128)(2,1)S(1)}, bf16[256,512]{1,0:T(8,128)(2,1)S(1)}, u32[]{:S(2)}, u32[]{:S(2)}) %collective-permute-start.4) | collective-permute-done | bytes 262176 | tf_op jit(solution)/shard_map/ppermute | solution.py:27
  74.3 1.8 collective-permute-done.5
  77.2 2.7 %collective-permute-start.9 = (bf16[256,1024]{1,0:T(8,128)(2,1)S(1)}, bf16[256,1024]{1,0:T(8,128)(2,1)S(1)}, u32[]{:S(2)}, u32[]{:S(2)}) collective-permute-start(bf16[256,1024]{1,0:T(8,128)(2,1)S(1)} %pad_maximum_fusion.2.refs_2_), channel_id=1, source_target_pairs={{0,12},{4,0},{8,4},{12,8},{1,13},{5,1},{9,5},{13,9},{2,14},{6,2},{... | collective-permute-start | bytes 1572872 | tf_op jit(solution)/shard_map/ppermute | solution.py:27
  80.3 1.3 collective-permute-start.19
  81.6 3.1 %collective-permute-start.20 = (f32[144,128]{1,0:T(8,128)S(1)}, f32[144,128]{1,0:T(8,128)S(1)}, u32[]{:S(2)}, u32[]{:S(2)}) collective-permute-start(f32[144,128]{1,0:T(8,128)S(1)} %get-tuple-element.63), channel_id=1, source_target_pairs={{0,3},{1,0},{2,1},{3,2},{4,7},{5,4},{6,5},{7,6},{8,11},{9,8},{10,9... | collective-permute-start | bytes 221192 | tf_op jit(solution)/shard_map/ppermute | solution.py:27
  84.8 1.7 collective-permute-done.11.refs_8_
  86.5 7.3 %collective-permute-start.21 = (f32[144,128]{1,0:T(8,128)S(1)}, f32[144,128]{1,0:T(8,128)S(1)}, u32[]{:S(2)}, u32[]{:S(2)}) collective-permute-start(f32[144,128]{1,0:T(8,128)S(1)} %get-tuple-element.62), channel_id=1, source_target_pairs={{0,2},{1,3},{2,0},{3,1},{4,6},{5,7},{6,4},{7,5},{8,10},{9,11},{10,... | collective-permute-start | bytes 221192 | tf_op jit(solution)/shard_map/ppermute | solution.py:27
  93.8 1.5 fusion.2
  95.6 1.5 collective-permute-start.16
  98.4 5.4 %all-gather.3.cloned.1.call-done = bf16[768,4096]{1,0:T(8,128)(2,1)} async-done(((bf16[96,4096]{1,0:T(8,128)(2,1)}), bf16[768,4096]{1,0:T(8,128)(2,1)}) %all-gather.3.cloned.1.call-update) | async-done | bytes 6291472 | tf_op jit(solution)/shard_map/all_gather | solution.py:228
  103.8 12.5 %project.2.near_ref = bf16[3,768,256]{2,1,0:T(8,128)(2,1)} custom-call(s32[1]{0:T(128)} %bitcast.row_ref, bf16[1024,1024]{1,0:T(8,128)(2,1)} %act_hbm.3, bf16[256,1024]{1,0:T(8,128)(2,1)} %copy-done.3, bf16[256,1024]{1,0:T(8,128)(2,1)} %copy-done.8, bf16[256,1024]{1,0:T(8,128)(2,1)} %copy-done.4, bf16[256,1024]{1,0:T(8,128)(2,1)} %collective-permute-done.8.refs_3_, ...), custom_call_target="tpu_custom_call" | custom-call | flops 12000000000 | bytes 12582912 | tf_op jit(solution)/shard_map/project/pallas_call | solution.py:80
  117.2 7.8 %project.3.far_ref = bf16[3,256,256]{2,1,0:T(8,128)(2,1)} custom-call(s32[1]{0:T(128)} %bitcast.row_ref, bf16[1024,1024]{1,0:T(8,128)(2,1)} %act_hbm.3, bf16[256,1024]{1,0:T(8,128)(2,1)} %collective-permute-done.14.refs_0_, bf16[256,1024]{1,0:T(8,128)(2,1)} %collective-permute-done.15.refs_1_, bf16[256,1024]{1,0:T(8,128)(2,1)} %pad_maximum_fusion.3.refs_2_, ...), custom_call_target="tpu_custom_call" | custom-call | flops 4000000000 | bytes 8388608 | tf_op jit(solution)/shard_map/project/pallas_call | solution.py:80
  126.3 3.5 %collective-permute-start.18 = (bf16[3,144,256]{2,1,0:T(8,128)(2,1)S(1)}, bf16[3,144,256]{2,1,0:T(8,128)(2,1)S(1)}, u32[]{:S(2)}, u32[]{:S(2)}) collective-permute-start(bf16[3,144,256]{2,1,0:T(8,128)(2,1)S(1)} %fusion.45.halo_ref), channel_id=1, source_target_pairs={{0,16},{16,32},{32,48},{48,64},{64,80},{80,96},{96,112},{112,128},... | collective-permute-start | bytes 663560 | tf_op jit(solution)/shard_map/ppermute | solution.py:275
  130.3 7.9 %mix.3 = bf16[512,256]{1,0:T(8,128)(2,1)S(1)} custom-call(s32[1]{0:T(128)} %bitcast.row_ref, bf16[3,768,256]{2,1,0:T(8,128)(2,1)S(1)} %copy-done.1, bf16[3,256,256]{2,1,0:T(8,128)(2,1)S(1)} %copy-done.2, bf16[3,144,256]{2,1,0:T(8,128)(2,1)S(1)} %fusion.45.halo_ref, f32[144,256]{1,0:T(8,128)S(1)} %fusion.29.taps_ref), custom_call_target="tpu_custom_call" | custom-call | flops 8999999488 | bytes 2097152 | tf_op jit(solution)/shard_map/mix/pallas_call | solution.py:156
  138.2 7.9 %mix.2 = bf16[512,256]{1,0:T(8,128)(2,1)S(1)} custom-call(s32[1]{0:T(128)} %bitcast.row_ref, bf16[3,768,256]{2,1,0:T(8,128)(2,1)S(1)} %copy-done.1, bf16[3,256,256]{2,1,0:T(8,128)(2,1)S(1)} %copy-done.2, bf16[3,144,256]{2,1,0:T(8,128)(2,1)S(1)} %collective-permute-done.18.halo_ref, f32[144,256]{1,0:T(8,128)S(1)} %fusion.29.taps_ref), custom_call_target="tpu_custom_call" | custom-call | flops 8999999488 | bytes 2097152 | tf_op jit(solution)/shard_map/mix/pallas_call | solution.py:156
  146.3 11.1 %collective-permute-start.22 = (bf16[512,256]{1,0:T(8,128)(2,1)S(1)}, bf16[512,256]{1,0:T(8,128)(2,1)S(1)}, u32[]{:S(2)}, u32[]{:S(2)}) collective-permute-start(bf16[512,256]{1,0:T(8,128)(2,1)S(1)} %pad_maximum_fusion.8), channel_id=1, source_target_pairs={{0,1},{1,2},{2,3},{3,0},{4,5},{5,6},{6,7},{7,4},{8,9},{9,10},{10,1... | collective-permute-start | bytes 786440 | tf_op jit(solution)/shard_map/ppermute | solution.py:27
  157.3 1.5 collective-permute-start.23
  158.9 6.7 %collective-permute-done.22 = bf16[512,256]{1,0:T(8,128)(2,1)S(1)} collective-permute-done((bf16[512,256]{1,0:T(8,128)(2,1)S(1)}, bf16[512,256]{1,0:T(8,128)(2,1)S(1)}, u32[]{:S(2)}, u32[]{:S(2)}) %collective-permute-start.22) | collective-permute-done | bytes 262176 | tf_op jit(solution)/shard_map/ppermute | solution.py:27
  165.6 5.5 %collective-permute-start.28 = (bf16[256,256]{1,0:T(8,128)(2,1)S(1)}, bf16[256,256]{1,0:T(8,128)(2,1)S(1)}, u32[]{:S(2)}, u32[]{:S(2)}) collective-permute-start(bf16[256,256]{1,0:T(8,128)(2,1)S(1)} %slice.205), channel_id=1, source_target_pairs={{0,1},{1,2},{2,3},{3,0},{4,5},{5,6},{6,7},{7,4},{8,9},{9,10},{10,1... | collective-permute-start | bytes 393224 | tf_op jit(solution)/shard_map/ppermute | solution.py:27
  171.9 2.5 %collective-permute-start.29 = (bf16[256,256]{1,0:T(8,128)(2,1)S(1)}, bf16[256,256]{1,0:T(8,128)(2,1)S(1)}, u32[]{:S(2)}, u32[]{:S(2)}) collective-permute-start(bf16[256,256]{1,0:T(8,128)(2,1)S(1)} %slice.206), channel_id=1, source_target_pairs={{0,3},{1,0},{2,1},{3,2},{4,7},{5,4},{6,5},{7,6},{8,11},{9,8},{10,9... | collective-permute-start | bytes 393224 | tf_op jit(solution)/shard_map/ppermute | solution.py:27
  174.5 1.3 collective-permute-start.24
  175.8 2.3 %collective-permute-start.25 = (bf16[512,256]{1,0:T(8,128)(2,1)S(1)}, bf16[512,256]{1,0:T(8,128)(2,1)S(1)}, u32[]{:S(2)}, u32[]{:S(2)}) collective-permute-start(bf16[512,256]{1,0:T(8,128)(2,1)S(1)} %pad_maximum_fusion.7), channel_id=1, source_target_pairs={{0,3},{1,0},{2,1},{3,2},{4,7},{5,4},{6,5},{7,6},{8,11},{9,8},{10,9... | collective-permute-start | bytes 786440 | tf_op jit(solution)/shard_map/ppermute | solution.py:27
  178.1 7.3 %collective-permute-done.29 = bf16[256,256]{1,0:T(8,128)(2,1)S(1)} collective-permute-done((bf16[256,256]{1,0:T(8,128)(2,1)S(1)}, bf16[256,256]{1,0:T(8,128)(2,1)S(1)}, u32[]{:S(2)}, u32[]{:S(2)}) %collective-permute-start.29) | collective-permute-done | bytes 131104 | tf_op jit(solution)/shard_map/ppermute | solution.py:27
  185.4 2.9 %convolution_convert_fusion = bf16[512,1024]{1,0:T(8,128)(2,1)S(1)} fusion(bf16[1024,1024]{1,0:T(8,128)(2,1)} %all-gather.5.cloned.1.call-done, bf16[256,256]{1,0:T(8,128)(2,1)S(1)} %collective-permute-done.29, bf16[256,256]{1,0:T(8,128)(2,1)S(1)} %collective-permute-done.28, bf16[512,256]{1,0:T(8,128)(2,1)S(1)} %collective-permute-done.23, ...), kind=kOutput, calls=%fused_computation.3 | convolution fusion | flops 1081606144 | bytes 4194304 | tf_op jit(solution)/shard_map/dot_general | solution.py:291
  188.3 1.4 collective-permute-start.30
  189.7 1.4 collective-permute-start.34
  192.3 1.3 collective-permute-done.25
  193.6 2.0 collective-permute-start.27
  197.4 2.3 %collective-permute-start.35 = (bf16[128,1024]{1,0:T(8,128)(2,1)S(1)}, bf16[128,1024]{1,0:T(8,128)(2,1)S(1)}, u32[]{:S(2)}, u32[]{:S(2)}) collective-permute-start(bf16[128,1024]{1,0:T(8,128)(2,1)S(1)} %get-tuple-element.44), channel_id=1, source_target_pairs={{0,12},{4,0},{8,4},{12,8},{1,13},{5,1},{9,5},{13,9},{2,14},{6,2},{... | collective-permute-start | bytes 786440 | tf_op jit(solution)/shard_map/ppermute | solution.py:27
  199.6 2.6 %collective-permute-done.27 = bf16[256,256]{1,0:T(8,128)(2,1)S(1)} collective-permute-done((bf16[256,256]{1,0:T(8,128)(2,1)S(1)}, bf16[256,256]{1,0:T(8,128)(2,1)S(1)}, u32[]{:S(2)}, u32[]{:S(2)}) %collective-permute-start.27) | collective-permute-done | bytes 131104 | tf_op jit(solution)/shard_map/ppermute | solution.py:27
  202.3 1.3 convolution_convert_fusion.1
  203.6 2.6 %collective-permute-start.32 = (bf16[128,1024]{1,0:T(8,128)(2,1)S(1)}, bf16[128,1024]{1,0:T(8,128)(2,1)S(1)}, u32[]{:S(2)}, u32[]{:S(2)}) collective-permute-start(bf16[128,1024]{1,0:T(8,128)(2,1)S(1)} %get-tuple-element.43), channel_id=1, source_target_pairs={{0,4},{4,8},{8,12},{12,0},{1,5},{5,9},{9,13},{13,1},{2,6},{6,10},{... | collective-permute-start | bytes 786440 | tf_op jit(solution)/shard_map/ppermute | solution.py:27
  206.2 1.6 collective-permute-start.33
  207.8 6.0 %collective-permute-done.32 = bf16[128,1024]{1,0:T(8,128)(2,1)S(1)} collective-permute-done((bf16[128,1024]{1,0:T(8,128)(2,1)S(1)}, bf16[128,1024]{1,0:T(8,128)(2,1)S(1)}, u32[]{:S(2)}, u32[]{:S(2)}) %collective-permute-start.32) | collective-permute-done | bytes 262176 | tf_op jit(solution)/shard_map/ppermute | solution.py:27
  (118 shorter events, 16.6 us)
Async XLA Ops:
  6.5 87.3 %copy-start = (bf16[64,1024]{1,0:T(8,128)(2,1)S(1)}, bf16[64,1024]{1,0:T(8,128)(2,1)}, u32[]{:S(2)}) copy-start(bf16[64,1024]{1,0:T(8,128)(2,1)} %param.17) | copy-start | bytes 393220
  6.5 97.3 %all-gather.3.cloned.1.call-start = ((), (), s32[]{:S(2)}) async-start(), calls=%async_computation | async-start | bytes 7077888 | tf_op jit(solution)/shard_map/all_gather | solution.py:228
  8.9 17.8 %collective-permute-start = (bf16[352,512]{1,0:T(8,128)(2,1)S(1)}, bf16[352,512]{1,0:T(8,128)(2,1)S(1)}, u32[]{:S(2)}, u32[]{:S(2)}) collective-permute-start(bf16[352,512]{1,0:T(8,128)(2,1)S(1)} %pad_maximum_fusion.5), channel_id=1, source_target_pairs={{0,1},{1,2},{2,3},{3,0},{4,5},{5,6},{6,7},{7,4},{8,9},{9,10},{10,1... | collective-permute-start | bytes 1081352 | tf_op jit(solution)/shard_map/ppermute | solution.py:27
  12.8 23.1 %collective-permute-start.1 = (bf16[352,512]{1,0:T(8,128)(2,1)S(1)}, bf16[352,512]{1,0:T(8,128)(2,1)S(1)}, u32[]{:S(2)}, u32[]{:S(2)}) collective-permute-start(bf16[352,512]{1,0:T(8,128)(2,1)S(1)} %pad_maximum_fusion.6), channel_id=1, source_target_pairs={{0,3},{1,0},{2,1},{3,2},{4,7},{5,4},{6,5},{7,6},{8,11},{9,8},{10,9... | collective-permute-start | bytes 1081352 | tf_op jit(solution)/shard_map/ppermute | solution.py:27
  15.9 20.0 %collective-permute-start.12 = (bf16[48,1024]{1,0:T(8,128)(2,1)S(1)}, bf16[48,1024]{1,0:T(8,128)(2,1)S(1)}, u32[]{:S(2)}, u32[]{:S(2)}) collective-permute-start(bf16[48,1024]{1,0:T(8,128)(2,1)S(1)} %bitcast.54), channel_id=1, source_target_pairs={{0,2},{1,3},{2,0},{3,1},{4,6},{5,7},{6,4},{7,5},{8,10},{9,11},{10,... | collective-permute-start | bytes 294920 | tf_op jit(solution)/shard_map/ppermute | solution.py:27
  36.0 15.7 %collective-permute-start.13 = (bf16[48,4096]{1,0:T(8,128)(2,1)S(1)}, bf16[48,4096]{1,0:T(8,128)(2,1)S(1)}, u32[]{:S(2)}, u32[]{:S(2)}) collective-permute-start(bf16[48,4096]{1,0:T(8,128)(2,1)S(1)} %constant_dynamic-update-slice_fusion.2), channel_id=1, source_target_pairs={{0,32},{16,48},{32,0},{48,16},{64,96},{80,112},{96,64},{112,80},{1... | collective-permute-start | bytes 1179656 | tf_op jit(solution)/shard_map/ppermute | solution.py:218
  41.9 10.7 %copy-start.3 = (bf16[256,1024]{1,0:T(8,128)(2,1)}, bf16[256,1024]{1,0:T(8,128)(2,1)S(1)}, u32[]{:S(2)}) copy-start(bf16[256,1024]{1,0:T(8,128)(2,1)S(1)} %pad_maximum_fusion.1.refs_0_) | copy-start | bytes 1572868
  41.9 18.6 %collective-permute-start.10 = (bf16[256,1024]{1,0:T(8,128)(2,1)S(1)}, bf16[256,1024]{1,0:T(8,128)(2,1)}, u32[]{:S(2)}, u32[]{:S(2)}) collective-permute-start(bf16[256,1024]{1,0:T(8,128)(2,1)S(1)} %pad_maximum_fusion.1.refs_0_), channel_id=1, source_target_pairs={{0,4},{4,8},{8,12},{12,0},{1,5},{5,9},{9,13},{13,1},{2,6},{6,10},{... | collective-permute-start | bytes 1572872 | tf_op jit(solution)/shard_map/ppermute | solution.py:27
  43.3 17.3 %collective-permute-start.8 = (bf16[256,1024]{1,0:T(8,128)(2,1)S(1)}, bf16[256,1024]{1,0:T(8,128)(2,1)}, u32[]{:S(2)}, u32[]{:S(2)}) collective-permute-start(bf16[256,1024]{1,0:T(8,128)(2,1)S(1)} %pad_maximum_fusion.1.refs_0_), channel_id=1, source_target_pairs={{0,12},{4,0},{8,4},{12,8},{1,13},{5,1},{9,5},{13,9},{2,14},{6,2},{... | collective-permute-start | bytes 1572872 | tf_op jit(solution)/shard_map/ppermute | solution.py:27
  44.9 7.8 %collective-permute-start.2 = (bf16[256,512]{1,0:T(8,128)(2,1)S(1)}, bf16[256,512]{1,0:T(8,128)(2,1)S(1)}, u32[]{:S(2)}, u32[]{:S(2)}) collective-permute-start(bf16[256,512]{1,0:T(8,128)(2,1)S(1)} %get-tuple-element.56), channel_id=1, source_target_pairs={{0,3},{1,0},{2,1},{3,2},{4,7},{5,4},{6,5},{7,6},{8,11},{9,8},{10,9... | collective-permute-start | bytes 786440 | tf_op jit(solution)/shard_map/ppermute | solution.py:27
  45.0 15.6 %collective-permute-start.3 = (bf16[256,512]{1,0:T(8,128)(2,1)S(1)}, bf16[256,512]{1,0:T(8,128)(2,1)S(1)}, u32[]{:S(2)}, u32[]{:S(2)}) collective-permute-start(bf16[256,512]{1,0:T(8,128)(2,1)S(1)} %get-tuple-element.57), channel_id=1, source_target_pairs={{0,1},{1,2},{2,3},{3,0},{4,5},{5,6},{6,7},{7,4},{8,9},{9,10},{10,1... | collective-permute-start | bytes 786440 | tf_op jit(solution)/shard_map/ppermute | solution.py:27
  51.7 15.5 %copy-start.9 = (f32[3,3,256]{2,1,0:T(4,128)S(1)}, f32[3,3,256]{2,1,0:T(4,128)}, u32[]{:S(2)}) copy-start(f32[3,3,256]{2,1,0:T(4,128)} %param.14) | copy-start | bytes 27652
  51.7 15.5 %copy-start.5 = (f32[128,256]{1,0:T(8,128)S(1)}, f32[128,256]{1,0:T(8,128)}, u32[]{:S(2)}) copy-start(f32[128,256]{1,0:T(8,128)} %param.15) | copy-start | bytes 393220
  51.7 15.5 %copy-start.10 = (f32[256]{0:T(256)S(1)}, f32[256]{0:T(256)}, u32[]{:S(2)}) copy-start(f32[256]{0:T(256)} %param.16) | copy-start | bytes 3076
  60.6 117.5 %all-gather.5.cloned.1.call-start = ((), (), s32[]{:S(2)}) async-start(), calls=%async_computation.1 | async-start | bytes 2228224 | tf_op jit(solution)/shard_map/all_gather | solution.py:271
  60.8 34.6 %copy-start.8 = (bf16[256,1024]{1,0:T(8,128)(2,1)}, bf16[256,1024]{1,0:T(8,128)(2,1)S(1)}, u32[]{:S(2)}) copy-start(bf16[256,1024]{1,0:T(8,128)(2,1)S(1)} %constant_dynamic-update-slice_fusion.refs_1_) | copy-start | bytes 1572868
  60.8 15.4 %collective-permute-start.6 = (bf16[256,1024]{1,0:T(8,128)(2,1)S(1)}, bf16[256,1024]{1,0:T(8,128)(2,1)S(1)}, u32[]{:S(2)}, u32[]{:S(2)}) collective-permute-start(bf16[256,1024]{1,0:T(8,128)(2,1)S(1)} %constant_dynamic-update-slice_fusion.refs_1_), channel_id=1, source_target_pairs={{0,4},{4,8},{8,12},{12,0},{1,5},{5,9},{9,13},{13,1},{2,6},{6,10},{... | collective-permute-start | bytes 1572872 | tf_op jit(solution)/shard_map/ppermute | solution.py:27
  62.0 14.2 %collective-permute-start.7 = (bf16[256,1024]{1,0:T(8,128)(2,1)S(1)}, bf16[256,1024]{1,0:T(8,128)(2,1)}, u32[]{:S(2)}, u32[]{:S(2)}) collective-permute-start(bf16[256,1024]{1,0:T(8,128)(2,1)S(1)} %constant_dynamic-update-slice_fusion.refs_1_), channel_id=1, source_target_pairs={{0,12},{4,0},{8,4},{12,8},{1,13},{5,1},{9,5},{13,9},{2,14},{6,2},{... | collective-permute-start | bytes 1572872 | tf_op jit(solution)/shard_map/ppermute | solution.py:27
  63.6 10.8 %collective-permute-start.4 = (bf16[256,512]{1,0:T(8,128)(2,1)S(1)}, bf16[256,512]{1,0:T(8,128)(2,1)S(1)}, u32[]{:S(2)}, u32[]{:S(2)}) collective-permute-start(bf16[256,512]{1,0:T(8,128)(2,1)S(1)} %slice.184), channel_id=1, source_target_pairs={{0,1},{1,2},{2,3},{3,0},{4,5},{5,6},{6,7},{7,4},{8,9},{9,10},{10,1... | collective-permute-start | bytes 786440 | tf_op jit(solution)/shard_map/ppermute | solution.py:27
  65.3 10.8 %collective-permute-start.5 = (bf16[256,512]{1,0:T(8,128)(2,1)S(1)}, bf16[256,512]{1,0:T(8,128)(2,1)S(1)}, u32[]{:S(2)}, u32[]{:S(2)}) collective-permute-start(bf16[256,512]{1,0:T(8,128)(2,1)S(1)} %slice.187), channel_id=1, source_target_pairs={{0,3},{1,0},{2,1},{3,2},{4,7},{5,4},{6,5},{7,6},{8,11},{9,8},{10,9... | collective-permute-start | bytes 786440 | tf_op jit(solution)/shard_map/ppermute | solution.py:27
  76.2 27.7 %copy-start.4 = (bf16[256,1024]{1,0:T(8,128)(2,1)}, bf16[256,1024]{1,0:T(8,128)(2,1)S(1)}, u32[]{:S(2)}) copy-start(bf16[256,1024]{1,0:T(8,128)(2,1)S(1)} %pad_maximum_fusion.2.refs_2_) | copy-start | bytes 1572868
  76.2 10.3 %collective-permute-start.11 = (bf16[256,1024]{1,0:T(8,128)(2,1)S(1)}, bf16[256,1024]{1,0:T(8,128)(2,1)S(1)}, u32[]{:S(2)}, u32[]{:S(2)}) collective-permute-start(bf16[256,1024]{1,0:T(8,128)(2,1)S(1)} %pad_maximum_fusion.2.refs_2_), channel_id=1, source_target_pairs={{0,4},{4,8},{8,12},{12,0},{1,5},{5,9},{9,13},{13,1},{2,6},{6,10},{... | collective-permute-start | bytes 1572872 | tf_op jit(solution)/shard_map/ppermute | solution.py:27
  77.0 39.3 %collective-permute-start.14 = (bf16[256,1024]{1,0:T(8,128)(2,1)}, bf16[256,1024]{1,0:T(8,128)(2,1)}, u32[]{:S(2)}, u32[]{:S(2)}) collective-permute-start(bf16[256,1024]{1,0:T(8,128)(2,1)} %collective-permute-done.10.refs_6_), channel_id=1, source_target_pairs={{0,4},{4,8},{8,12},{12,0},{1,5},{5,9},{9,13},{13,1},{2,6},{6,10},{... | collective-permute-start | bytes 1572872 | tf_op jit(solution)/shard_map/ppermute | solution.py:27
  77.2 18.2 %collective-permute-start.9 = (bf16[256,1024]{1,0:T(8,128)(2,1)S(1)}, bf16[256,1024]{1,0:T(8,128)(2,1)S(1)}, u32[]{:S(2)}, u32[]{:S(2)}) collective-permute-start(bf16[256,1024]{1,0:T(8,128)(2,1)S(1)} %pad_maximum_fusion.2.refs_2_), channel_id=1, source_target_pairs={{0,12},{4,0},{8,4},{12,8},{1,13},{5,1},{9,5},{13,9},{2,14},{6,2},{... | collective-permute-start | bytes 1572872 | tf_op jit(solution)/shard_map/ppermute | solution.py:27
  80.3 15.3 %collective-permute-start.19 = (f32[144,128]{1,0:T(8,128)S(1)}, f32[144,128]{1,0:T(8,128)S(1)}, u32[]{:S(2)}, u32[]{:S(2)}) collective-permute-start(f32[144,128]{1,0:T(8,128)S(1)} %get-tuple-element.64), channel_id=1, source_target_pairs={{0,1},{1,2},{2,3},{3,0},{4,5},{5,6},{6,7},{7,4},{8,9},{9,10},{10,1... | collective-permute-start | bytes 221192 | tf_op jit(solution)/shard_map/ppermute | solution.py:27
  81.6 15.5 %collective-permute-start.20 = (f32[144,128]{1,0:T(8,128)S(1)}, f32[144,128]{1,0:T(8,128)S(1)}, u32[]{:S(2)}, u32[]{:S(2)}) collective-permute-start(f32[144,128]{1,0:T(8,128)S(1)} %get-tuple-element.63), channel_id=1, source_target_pairs={{0,3},{1,0},{2,1},{3,2},{4,7},{5,4},{6,5},{7,6},{8,11},{9,8},{10,9... | collective-permute-start | bytes 221192 | tf_op jit(solution)/shard_map/ppermute | solution.py:27
  86.5 17.3 %copy-start.6 = (bf16[256,1024]{1,0:T(8,128)(2,1)}, bf16[256,1024]{1,0:T(8,128)(2,1)S(1)}, u32[]{:S(2)}) copy-start(bf16[256,1024]{1,0:T(8,128)(2,1)S(1)} %collective-permute-done.11.refs_8_) | copy-start | bytes 1572868
  86.5 29.8 %collective-permute-start.21 = (f32[144,128]{1,0:T(8,128)S(1)}, f32[144,128]{1,0:T(8,128)S(1)}, u32[]{:S(2)}, u32[]{:S(2)}) collective-permute-start(f32[144,128]{1,0:T(8,128)S(1)} %get-tuple-element.62), channel_id=1, source_target_pairs={{0,2},{1,3},{2,0},{3,1},{4,6},{5,7},{6,4},{7,5},{8,10},{9,11},{10,... | collective-permute-start | bytes 221192 | tf_op jit(solution)/shard_map/ppermute | solution.py:27
  95.5 20.9 %collective-permute-start.15 = (bf16[256,1024]{1,0:T(8,128)(2,1)}, bf16[256,1024]{1,0:T(8,128)(2,1)}, u32[]{:S(2)}, u32[]{:S(2)}) collective-permute-start(bf16[256,1024]{1,0:T(8,128)(2,1)} %collective-permute-done.7.refs_4_), channel_id=1, source_target_pairs={{0,12},{4,0},{8,4},{12,8},{1,13},{5,1},{9,5},{13,9},{2,14},{6,2},{... | collective-permute-start | bytes 1572872 | tf_op jit(solution)/shard_map/ppermute | solution.py:27
  95.6 20.7 %collective-permute-start.16 = (bf16[256,512]{1,0:T(8,128)(2,1)S(1)}, bf16[256,512]{1,0:T(8,128)(2,1)S(1)}, u32[]{:S(2)}, u32[]{:S(2)}) collective-permute-start(bf16[256,512]{1,0:T(8,128)(2,1)S(1)} %slice.192), channel_id=1, source_target_pairs={{0,4},{4,8},{8,12},{12,0},{1,5},{5,9},{9,13},{13,1},{2,6},{6,10},{... | collective-permute-start | bytes 786440 | tf_op jit(solution)/shard_map/ppermute | solution.py:27
  97.1 19.2 %collective-permute-start.17 = (bf16[256,512]{1,0:T(8,128)(2,1)S(1)}, bf16[256,512]{1,0:T(8,128)(2,1)S(1)}, u32[]{:S(2)}, u32[]{:S(2)}) collective-permute-start(bf16[256,512]{1,0:T(8,128)(2,1)S(1)} %slice.193), channel_id=1, source_target_pairs={{0,12},{4,0},{8,4},{12,8},{1,13},{5,1},{9,5},{13,9},{2,14},{6,2},{... | collective-permute-start | bytes 786440 | tf_op jit(solution)/shard_map/ppermute | solution.py:27
  117.2 8.8 %copy-start.1 = (bf16[3,768,256]{2,1,0:T(8,128)(2,1)S(1)}, bf16[3,768,256]{2,1,0:T(8,128)(2,1)}, u32[]{:S(2)}) copy-start(bf16[3,768,256]{2,1,0:T(8,128)(2,1)} %project.2.near_ref) | copy-start | bytes 3538948
  126.3 11.9 %collective-permute-start.18 = (bf16[3,144,256]{2,1,0:T(8,128)(2,1)S(1)}, bf16[3,144,256]{2,1,0:T(8,128)(2,1)S(1)}, u32[]{:S(2)}, u32[]{:S(2)}) collective-permute-start(bf16[3,144,256]{2,1,0:T(8,128)(2,1)S(1)} %fusion.45.halo_ref), channel_id=1, source_target_pairs={{0,16},{16,32},{32,48},{48,64},{64,80},{80,96},{96,112},{112,128},... | collective-permute-start | bytes 663560 | tf_op jit(solution)/shard_map/ppermute | solution.py:275
  146.3 19.3 %collective-permute-start.22 = (bf16[512,256]{1,0:T(8,128)(2,1)S(1)}, bf16[512,256]{1,0:T(8,128)(2,1)S(1)}, u32[]{:S(2)}, u32[]{:S(2)}) collective-permute-start(bf16[512,256]{1,0:T(8,128)(2,1)S(1)} %pad_maximum_fusion.8), channel_id=1, source_target_pairs={{0,1},{1,2},{2,3},{3,0},{4,5},{5,6},{6,7},{7,4},{8,9},{9,10},{10,1... | collective-permute-start | bytes 786440 | tf_op jit(solution)/shard_map/ppermute | solution.py:27
  157.3 14.6 %collective-permute-start.23 = (bf16[512,256]{1,0:T(8,128)(2,1)S(1)}, bf16[512,256]{1,0:T(8,128)(2,1)S(1)}, u32[]{:S(2)}, u32[]{:S(2)}) collective-permute-start(bf16[512,256]{1,0:T(8,128)(2,1)S(1)} %pad_maximum_fusion.8), channel_id=1, source_target_pairs={{0,3},{1,0},{2,1},{3,2},{4,7},{5,4},{6,5},{7,6},{8,11},{9,8},{10,9... | collective-permute-start | bytes 786440 | tf_op jit(solution)/shard_map/ppermute | solution.py:27
  165.6 12.5 %collective-permute-start.28 = (bf16[256,256]{1,0:T(8,128)(2,1)S(1)}, bf16[256,256]{1,0:T(8,128)(2,1)S(1)}, u32[]{:S(2)}, u32[]{:S(2)}) collective-permute-start(bf16[256,256]{1,0:T(8,128)(2,1)S(1)} %slice.205), channel_id=1, source_target_pairs={{0,1},{1,2},{2,3},{3,0},{4,5},{5,6},{6,7},{7,4},{8,9},{9,10},{10,1... | collective-permute-start | bytes 393224 | tf_op jit(solution)/shard_map/ppermute | solution.py:27
  171.9 13.5 %collective-permute-start.29 = (bf16[256,256]{1,0:T(8,128)(2,1)S(1)}, bf16[256,256]{1,0:T(8,128)(2,1)S(1)}, u32[]{:S(2)}, u32[]{:S(2)}) collective-permute-start(bf16[256,256]{1,0:T(8,128)(2,1)S(1)} %slice.206), channel_id=1, source_target_pairs={{0,3},{1,0},{2,1},{3,2},{4,7},{5,4},{6,5},{7,6},{8,11},{9,8},{10,9... | collective-permute-start | bytes 393224 | tf_op jit(solution)/shard_map/ppermute | solution.py:27
  174.5 17.3 %collective-permute-start.24 = (bf16[512,256]{1,0:T(8,128)(2,1)S(1)}, bf16[512,256]{1,0:T(8,128)(2,1)S(1)}, u32[]{:S(2)}, u32[]{:S(2)}) collective-permute-start(bf16[512,256]{1,0:T(8,128)(2,1)S(1)} %pad_maximum_fusion.7), channel_id=1, source_target_pairs={{0,1},{1,2},{2,3},{3,0},{4,5},{5,6},{6,7},{7,4},{8,9},{9,10},{10,1... | collective-permute-start | bytes 786440 | tf_op jit(solution)/shard_map/ppermute | solution.py:27
  175.8 17.8 %collective-permute-start.25 = (bf16[512,256]{1,0:T(8,128)(2,1)S(1)}, bf16[512,256]{1,0:T(8,128)(2,1)S(1)}, u32[]{:S(2)}, u32[]{:S(2)}) collective-permute-start(bf16[512,256]{1,0:T(8,128)(2,1)S(1)} %pad_maximum_fusion.7), channel_id=1, source_target_pairs={{0,3},{1,0},{2,1},{3,2},{4,7},{5,4},{6,5},{7,6},{8,11},{9,8},{10,9... | collective-permute-start | bytes 786440 | tf_op jit(solution)/shard_map/ppermute | solution.py:27
  188.3 14.0 %copy-start.11 = (bf16[1024,1024]{1,0:T(8,128)(2,1)S(1)}, bf16[1024,1024]{1,0:T(8,128)(2,1)}, u32[]{:S(2)}) copy-start(bf16[1024,1024]{1,0:T(8,128)(2,1)} %all-gather.5.cloned.1.call-done) | copy-start | bytes 6291460
  188.3 7.5 %collective-permute-start.30 = (bf16[128,1024]{1,0:T(8,128)(2,1)S(1)}, bf16[128,1024]{1,0:T(8,128)(2,1)S(1)}, u32[]{:S(2)}, u32[]{:S(2)}) collective-permute-start(bf16[128,1024]{1,0:T(8,128)(2,1)S(1)} %get-tuple-element.47), channel_id=1, source_target_pairs={{0,4},{4,8},{8,12},{12,0},{1,5},{5,9},{9,13},{13,1},{2,6},{6,10},{... | collective-permute-start | bytes 786440 | tf_op jit(solution)/shard_map/ppermute | solution.py:27
  189.7 6.9 %collective-permute-start.34 = (bf16[128,1024]{1,0:T(8,128)(2,1)S(1)}, bf16[128,1024]{1,0:T(8,128)(2,1)S(1)}, u32[]{:S(2)}, u32[]{:S(2)}) collective-permute-start(bf16[128,1024]{1,0:T(8,128)(2,1)S(1)} %get-tuple-element.46), channel_id=1, source_target_pairs={{0,12},{4,0},{8,4},{12,8},{1,13},{5,1},{9,5},{13,9},{2,14},{6,2},{... | collective-permute-start | bytes 786440 | tf_op jit(solution)/shard_map/ppermute | solution.py:27
  191.8 7.8 %collective-permute-start.26 = (bf16[256,256]{1,0:T(8,128)(2,1)S(1)}, bf16[256,256]{1,0:T(8,128)(2,1)S(1)}, u32[]{:S(2)}, u32[]{:S(2)}) collective-permute-start(bf16[256,256]{1,0:T(8,128)(2,1)S(1)} %slice.202), channel_id=1, source_target_pairs={{0,1},{1,2},{2,3},{3,0},{4,5},{5,6},{6,7},{7,4},{8,9},{9,10},{10,1... | collective-permute-start | bytes 393224 | tf_op jit(solution)/shard_map/ppermute | solution.py:27
  193.6 8.7 %collective-permute-start.27 = (bf16[256,256]{1,0:T(8,128)(2,1)S(1)}, bf16[256,256]{1,0:T(8,128)(2,1)S(1)}, u32[]{:S(2)}, u32[]{:S(2)}) collective-permute-start(bf16[256,256]{1,0:T(8,128)(2,1)S(1)} %slice.203), channel_id=1, source_target_pairs={{0,3},{1,0},{2,1},{3,2},{4,7},{5,4},{6,5},{7,6},{8,11},{9,8},{10,9... | collective-permute-start | bytes 393224 | tf_op jit(solution)/shard_map/ppermute | solution.py:27
  196.9 10.9 %collective-permute-start.31 = (bf16[128,1024]{1,0:T(8,128)(2,1)S(1)}, bf16[128,1024]{1,0:T(8,128)(2,1)S(1)}, u32[]{:S(2)}, u32[]{:S(2)}) collective-permute-start(bf16[128,1024]{1,0:T(8,128)(2,1)S(1)} %get-tuple-element.45), channel_id=1, source_target_pairs={{0,4},{4,8},{8,12},{12,0},{1,5},{5,9},{9,13},{13,1},{2,6},{6,10},{... | collective-permute-start | bytes 786440 | tf_op jit(solution)/shard_map/ppermute | solution.py:27
  197.4 10.4 %collective-permute-start.35 = (bf16[128,1024]{1,0:T(8,128)(2,1)S(1)}, bf16[128,1024]{1,0:T(8,128)(2,1)S(1)}, u32[]{:S(2)}, u32[]{:S(2)}) collective-permute-start(bf16[128,1024]{1,0:T(8,128)(2,1)S(1)} %get-tuple-element.44), channel_id=1, source_target_pairs={{0,12},{4,0},{8,4},{12,8},{1,13},{5,1},{9,5},{13,9},{2,14},{6,2},{... | collective-permute-start | bytes 786440 | tf_op jit(solution)/shard_map/ppermute | solution.py:27
  203.6 10.2 %collective-permute-start.32 = (bf16[128,1024]{1,0:T(8,128)(2,1)S(1)}, bf16[128,1024]{1,0:T(8,128)(2,1)S(1)}, u32[]{:S(2)}, u32[]{:S(2)}) collective-permute-start(bf16[128,1024]{1,0:T(8,128)(2,1)S(1)} %get-tuple-element.43), channel_id=1, source_target_pairs={{0,4},{4,8},{8,12},{12,0},{1,5},{5,9},{9,13},{13,1},{2,6},{6,10},{... | collective-permute-start | bytes 786440 | tf_op jit(solution)/shard_map/ppermute | solution.py:27
  206.2 7.6 %collective-permute-start.33 = (bf16[128,1024]{1,0:T(8,128)(2,1)S(1)}, bf16[128,1024]{1,0:T(8,128)(2,1)S(1)}, u32[]{:S(2)}, u32[]{:S(2)}) collective-permute-start(bf16[128,1024]{1,0:T(8,128)(2,1)S(1)} %get-tuple-element.42), channel_id=1, source_target_pairs={{0,12},{4,0},{8,4},{12,8},{1,13},{5,1},{9,5},{13,9},{2,14},{6,2},{... | collective-permute-start | bytes 786440 | tf_op jit(solution)/shard_map/ppermute | solution.py:27
  (3 other events, 14.4 us)
Sparse Core Ops, SparseCore 0:
  60.7 43.0 all-gather.2
  105.7 39.0 all-gather.4

commit v4 on v3

--- a/solution.py
+++ b/solution.py
@@ -285,7 +285,7 @@
     opposite, above, below = quarter(2), quarter(1), quarter(3)
     first = gather_col(jnp.concatenate([opposite, above[:mid], below[mid:]], axis=0))
     second = jnp.concatenate([above[mid:], below[:mid], quarter(0)], axis=0)
-    second = gather_col(after(second, first[1], first[2]))
+    second = gather_col(second)
 
     def outputs(gathered):
         return lax.dot_general(

time: 226 us -> 226 us (level)
  the two profiles are of different devices: /device:TPU:1 before, /device:TPU:34 now
where the time goes in v4:
time: 226 us; the launch traced here: 222 us
  starting transfers between devices  78.1 us (35%)
  waiting for transfers between devices  77.8 us (34%)
  Pallas kernels  36.1 us (16%)
  between operations  14.2 us (6%)
  matrix products  6.51 us (3%)
  other arithmetic  4.84 us (2%)
  local copies, waits for them, and re-layouts  4.21 us (2%)
    ppermute x34, starting transfers between devices, shift(): return lax.ppermute(x, axis, ring(4, step))  76.1 us
    ppermute x34, waiting for transfers between devices, shift(): return lax.ppermute(x, axis, ring(4, step))  67.7 us
    pallas_call x2, Pallas kernels, project(): pl.pallas_call(functools.partial(project_kernel, quarters), in_specs=[pl....  20.2 us
    pallas_call x2, Pallas kernels, mix(): pl.pallas_call(functools.partial(mix_kernel, first), in_specs=[pl.BlockSp...  15.8 us
    ppermute x1, waiting for transfers between devices, on_device(): w_other = lax.ppermute(w_rows, 'ctx', [(i, i ^ 2) for i in range(16)])  10.1 us
  transfers between devices with their start and end apart: 38, of which 13 were waited for; matrix products, arithmetic and copies ran while one was open for 5% of the time, Pallas kernels for 16%

profile of v4, /device:TPU:34, one launch (start us, length us, event | category | flops | bytes accessed | tf_op | source)
XLA Modules:
  0.0 221.7 jit_solution(4008166085246807359)
XLA Ops:
  6.5 1.1 multiply_convert_fusion
  8.9 3.3 %collective-permute-start = (bf16[352,512]{1,0:T(8,128)(2,1)S(1)}, bf16[352,512]{1,0:T(8,128)(2,1)S(1)}, u32[]{:S(2)}, u32[]{:S(2)}) collective-permute-start(bf16[352,512]{1,0:T(8,128)(2,1)S(1)} %pad_maximum_fusion.5), channel_id=1, source_target_pairs={{0,1},{1,2},{2,3},{3,0},{4,5},{5,6},{6,7},{7,4},{8,9},{9,10},{10,1... | collective-permute-start | bytes 1081352 | tf_op jit(solution)/shard_map/ppermute | solution.py:27
  12.3 2.2 %collective-permute-start.1 = (bf16[352,512]{1,0:T(8,128)(2,1)S(1)}, bf16[352,512]{1,0:T(8,128)(2,1)S(1)}, u32[]{:S(2)}, u32[]{:S(2)}) collective-permute-start(bf16[352,512]{1,0:T(8,128)(2,1)S(1)} %pad_maximum_fusion.6), channel_id=1, source_target_pairs={{0,3},{1,0},{2,1},{3,2},{4,7},{5,4},{6,5},{7,6},{8,11},{9,8},{10,9... | collective-permute-start | bytes 1081352 | tf_op jit(solution)/shard_map/ppermute | solution.py:27
  14.5 5.0 %collective-permute-start.12 = (bf16[48,1024]{1,0:T(8,128)(2,1)S(1)}, bf16[48,1024]{1,0:T(8,128)(2,1)S(1)}, u32[]{:S(2)}, u32[]{:S(2)}) collective-permute-start(bf16[48,1024]{1,0:T(8,128)(2,1)S(1)} %bitcast.54), channel_id=1, source_target_pairs={{0,2},{1,3},{2,0},{3,1},{4,6},{5,7},{6,4},{7,5},{8,10},{9,11},{10,... | collective-permute-start | bytes 294920 | tf_op jit(solution)/shard_map/ppermute | solution.py:27
  19.5 14.7 %collective-permute-done = bf16[352,512]{1,0:T(8,128)(2,1)S(1)} collective-permute-done((bf16[352,512]{1,0:T(8,128)(2,1)S(1)}, bf16[352,512]{1,0:T(8,128)(2,1)S(1)}, u32[]{:S(2)}, u32[]{:S(2)}) %collective-permute-start) | collective-permute-done | bytes 360480 | tf_op jit(solution)/shard_map/ppermute | solution.py:27
  34.3 4.5 %collective-permute-done.12 = bf16[48,1024]{1,0:T(8,128)(2,1)S(1)} collective-permute-done((bf16[48,1024]{1,0:T(8,128)(2,1)S(1)}, bf16[48,1024]{1,0:T(8,128)(2,1)S(1)}, u32[]{:S(2)}, u32[]{:S(2)}) %collective-permute-start.12) | collective-permute-done | bytes 98336 | tf_op jit(solution)/shard_map/ppermute | solution.py:27
  38.8 1.1 constant_dynamic-slice_fusion.5
  40.1 1.7 collective-permute-start.10
  41.7 1.7 collective-permute-start.8
  43.4 1.7 collective-permute-start.2
  45.1 1.3 collective-permute-start.3
  46.4 10.1 %collective-permute-done.13 = bf16[48,4096]{1,0:T(8,128)(2,1)S(1)} collective-permute-done((bf16[48,4096]{1,0:T(8,128)(2,1)S(1)}, bf16[48,4096]{1,0:T(8,128)(2,1)S(1)}, u32[]{:S(2)}, u32[]{:S(2)}) %collective-permute-start.13) | collective-permute-done | bytes 393248 | tf_op jit(solution)/shard_map/ppermute | solution.py:218
  57.5 1.3 collective-permute-done.2
  59.1 1.7 collective-permute-start.6
  60.7 1.7 collective-permute-start.7
  62.4 2.3 %collective-permute-start.4 = (bf16[256,512]{1,0:T(8,128)(2,1)S(1)}, bf16[256,512]{1,0:T(8,128)(2,1)S(1)}, u32[]{:S(2)}, u32[]{:S(2)}) collective-permute-start(bf16[256,512]{1,0:T(8,128)(2,1)S(1)} %slice.184), channel_id=1, source_target_pairs={{0,1},{1,2},{2,3},{3,0},{4,5},{5,6},{6,7},{7,4},{8,9},{9,10},{10,1... | collective-permute-start | bytes 786440 | tf_op jit(solution)/shard_map/ppermute | solution.py:27
  64.8 1.8 collective-permute-start.5
  66.7 9.5 %collective-permute-done.4 = bf16[256,512]{1,0:T(8,128)(2,1)S(1)} collective-permute-done((bf16[256,512]{1,0:T(8,128)(2,1)S(1)}, bf16[256,512]{1,0:T(8,128)(2,1)S(1)}, u32[]{:S(2)}, u32[]{:S(2)}) %collective-permute-start.4) | collective-permute-done | bytes 262176 | tf_op jit(solution)/shard_map/ppermute | solution.py:27
  77.8 1.2 collective-permute-start.14
  78.9 2.3 %collective-permute-start.9 = (bf16[256,1024]{1,0:T(8,128)(2,1)S(1)}, bf16[256,1024]{1,0:T(8,128)(2,1)S(1)}, u32[]{:S(2)}, u32[]{:S(2)}) collective-permute-start(bf16[256,1024]{1,0:T(8,128)(2,1)S(1)} %pad_maximum_fusion.2.refs_2_), channel_id=1, source_target_pairs={{0,12},{4,0},{8,4},{12,8},{1,13},{5,1},{9,5},{13,9},{2,14},{6,2},{... | collective-permute-start | bytes 1572872 | tf_op jit(solution)/shard_map/ppermute | solution.py:27
  81.6 2.8 %collective-permute-start.19 = (f32[144,128]{1,0:T(8,128)S(1)}, f32[144,128]{1,0:T(8,128)S(1)}, u32[]{:S(2)}, u32[]{:S(2)}) collective-permute-start(f32[144,128]{1,0:T(8,128)S(1)} %get-tuple-element.62), channel_id=1, source_target_pairs={{0,1},{1,2},{2,3},{3,0},{4,5},{5,6},{6,7},{7,4},{8,9},{9,10},{10,1... | collective-permute-start | bytes 221192 | tf_op jit(solution)/shard_map/ppermute | solution.py:27
  84.4 1.4 collective-permute-start.20
  85.8 7.3 %collective-permute-done.11.refs_8_ = bf16[256,1024]{1,0:T(8,128)(2,1)S(1)} collective-permute-done((bf16[256,1024]{1,0:T(8,128)(2,1)S(1)}, bf16[256,1024]{1,0:T(8,128)(2,1)S(1)}, u32[]{:S(2)}, u32[]{:S(2)}) %collective-permute-start.11) | collective-permute-done | bytes 524320 | tf_op jit(solution)/shard_map/ppermute | solution.py:27
  93.1 3.8 %collective-permute-start.21 = (f32[144,128]{1,0:T(8,128)S(1)}, f32[144,128]{1,0:T(8,128)S(1)}, u32[]{:S(2)}, u32[]{:S(2)}) collective-permute-start(f32[144,128]{1,0:T(8,128)S(1)} %get-tuple-element.60), channel_id=1, source_target_pairs={{0,2},{1,3},{2,0},{3,1},{4,6},{5,7},{6,4},{7,5},{8,10},{9,11},{10,... | collective-permute-start | bytes 221192 | tf_op jit(solution)/shard_map/ppermute | solution.py:27
  96.9 1.5 fusion.2
  99.1 1.6 collective-permute-start.16
  100.7 1.7 collective-permute-start.17
  102.4 12.5 %project.2.near_ref = bf16[3,768,256]{2,1,0:T(8,128)(2,1)} custom-call(s32[1]{0:T(128)} %bitcast.row_ref, bf16[1024,1024]{1,0:T(8,128)(2,1)} %act_hbm.3, bf16[256,1024]{1,0:T(8,128)(2,1)} %copy-done.3, bf16[256,1024]{1,0:T(8,128)(2,1)} %copy-done.8, bf16[256,1024]{1,0:T(8,128)(2,1)} %copy-done.4, bf16[256,1024]{1,0:T(8,128)(2,1)} %collective-permute-done.8.refs_3_, ...), custom_call_target="tpu_custom_call" | custom-call | flops 12000000000 | bytes 12582912 | tf_op jit(solution)/shard_map/project/pallas_call | solution.py:80
  115.8 7.8 %project.3.far_ref = bf16[3,256,256]{2,1,0:T(8,128)(2,1)} custom-call(s32[1]{0:T(128)} %bitcast.row_ref, bf16[1024,1024]{1,0:T(8,128)(2,1)} %act_hbm.3, bf16[256,1024]{1,0:T(8,128)(2,1)} %collective-permute-done.14.refs_0_, bf16[256,1024]{1,0:T(8,128)(2,1)} %collective-permute-done.15.refs_1_, bf16[256,1024]{1,0:T(8,128)(2,1)} %pad_maximum_fusion.3.refs_2_, ...), custom_call_target="tpu_custom_call" | custom-call | flops 4000000000 | bytes 8388608 | tf_op jit(solution)/shard_map/project/pallas_call | solution.py:80
  124.9 1.9 collective-permute-start.18
  127.3 7.9 %mix.3 = bf16[512,256]{1,0:T(8,128)(2,1)S(1)} custom-call(s32[1]{0:T(128)} %bitcast.row_ref, bf16[3,768,256]{2,1,0:T(8,128)(2,1)S(1)} %copy-done.1, bf16[3,256,256]{2,1,0:T(8,128)(2,1)S(1)} %copy-done.2, bf16[3,144,256]{2,1,0:T(8,128)(2,1)S(1)} %fusion.49.halo_ref, f32[144,256]{1,0:T(8,128)S(1)} %fusion.33.taps_ref), custom_call_target="tpu_custom_call" | custom-call | flops 8999999488 | bytes 2097152 | tf_op jit(solution)/shard_map/mix/pallas_call | solution.py:156
  135.2 7.9 %mix.2 = bf16[512,256]{1,0:T(8,128)(2,1)S(1)} custom-call(s32[1]{0:T(128)} %bitcast.row_ref, bf16[3,768,256]{2,1,0:T(8,128)(2,1)S(1)} %copy-done.1, bf16[3,256,256]{2,1,0:T(8,128)(2,1)S(1)} %copy-done.2, bf16[3,144,256]{2,1,0:T(8,128)(2,1)S(1)} %collective-permute-done.18.halo_ref, f32[144,256]{1,0:T(8,128)S(1)} %fusion.33.taps_ref), custom_call_target="tpu_custom_call" | custom-call | flops 8999999488 | bytes 2097152 | tf_op jit(solution)/shard_map/mix/pallas_call | solution.py:156
  143.3 10.7 %collective-permute-start.26 = (bf16[512,256]{1,0:T(8,128)(2,1)S(1)}, bf16[512,256]{1,0:T(8,128)(2,1)S(1)}, u32[]{:S(2)}, u32[]{:S(2)}) collective-permute-start(bf16[512,256]{1,0:T(8,128)(2,1)S(1)} %pad_maximum_fusion.8), channel_id=1, source_target_pairs={{0,1},{1,2},{2,3},{3,0},{4,5},{5,6},{6,7},{7,4},{8,9},{9,10},{10,1... | collective-permute-start | bytes 786440 | tf_op jit(solution)/shard_map/ppermute | solution.py:27
  154.0 2.4 %collective-permute-start.27 = (bf16[512,256]{1,0:T(8,128)(2,1)S(1)}, bf16[512,256]{1,0:T(8,128)(2,1)S(1)}, u32[]{:S(2)}, u32[]{:S(2)}) collective-permute-start(bf16[512,256]{1,0:T(8,128)(2,1)S(1)} %pad_maximum_fusion.8), channel_id=1, source_target_pairs={{0,3},{1,0},{2,1},{3,2},{4,7},{5,4},{6,5},{7,6},{8,11},{9,8},{10,9... | collective-permute-start | bytes 786440 | tf_op jit(solution)/shard_map/ppermute | solution.py:27
  157.0 3.6 %collective-permute-start.23 = (bf16[512,256]{1,0:T(8,128)(2,1)S(1)}, bf16[512,256]{1,0:T(8,128)(2,1)S(1)}, u32[]{:S(2)}, u32[]{:S(2)}) collective-permute-start(bf16[512,256]{1,0:T(8,128)(2,1)S(1)} %pad_maximum_fusion.7), channel_id=1, source_target_pairs={{0,3},{1,0},{2,1},{3,2},{4,7},{5,4},{6,5},{7,6},{8,11},{9,8},{10,9... | collective-permute-start | bytes 786440 | tf_op jit(solution)/shard_map/ppermute | solution.py:27
  160.6 16.6 %collective-permute-done.26 = bf16[512,256]{1,0:T(8,128)(2,1)S(1)} collective-permute-done((bf16[512,256]{1,0:T(8,128)(2,1)S(1)}, bf16[512,256]{1,0:T(8,128)(2,1)S(1)}, u32[]{:S(2)}, u32[]{:S(2)}) %collective-permute-start.26) | collective-permute-done | bytes 262176 | tf_op jit(solution)/shard_map/ppermute | solution.py:27
  177.8 3.8 %collective-permute-start.29 = (bf16[256,256]{1,0:T(8,128)(2,1)S(1)}, bf16[256,256]{1,0:T(8,128)(2,1)S(1)}, u32[]{:S(2)}, u32[]{:S(2)}) collective-permute-start(bf16[256,256]{1,0:T(8,128)(2,1)S(1)} %slice.206), channel_id=1, source_target_pairs={{0,3},{1,0},{2,1},{3,2},{4,7},{5,4},{6,5},{7,6},{8,11},{9,8},{10,9... | collective-permute-start | bytes 393224 | tf_op jit(solution)/shard_map/ppermute | solution.py:27
  181.5 1.4 collective-permute-done.22
  183.4 3.8 %collective-permute-start.25 = (bf16[256,256]{1,0:T(8,128)(2,1)S(1)}, bf16[256,256]{1,0:T(8,128)(2,1)S(1)}, u32[]{:S(2)}, u32[]{:S(2)}) collective-permute-start(bf16[256,256]{1,0:T(8,128)(2,1)S(1)} %slice.203), channel_id=1, source_target_pairs={{0,3},{1,0},{2,1},{3,2},{4,7},{5,4},{6,5},{7,6},{8,11},{9,8},{10,9... | collective-permute-start | bytes 393224 | tf_op jit(solution)/shard_map/ppermute | solution.py:27
  187.3 2.6 %collective-permute-done.29 = bf16[256,256]{1,0:T(8,128)(2,1)S(1)} collective-permute-done((bf16[256,256]{1,0:T(8,128)(2,1)S(1)}, bf16[256,256]{1,0:T(8,128)(2,1)S(1)}, u32[]{:S(2)}, u32[]{:S(2)}) %collective-permute-start.29) | collective-permute-done | bytes 131104 | tf_op jit(solution)/shard_map/ppermute | solution.py:27
  189.9 2.9 %convolution_convert_fusion = bf16[512,1024]{1,0:T(8,128)(2,1)S(1)} fusion(bf16[1024,1024]{1,0:T(8,128)(2,1)} %all-gather.5.cloned.1.call-done, bf16[256,256]{1,0:T(8,128)(2,1)S(1)} %collective-permute-done.29, bf16[256,256]{1,0:T(8,128)(2,1)S(1)} %collective-permute-done.28, bf16[512,256]{1,0:T(8,128)(2,1)S(1)} %collective-permute-done.27, ...), kind=kOutput, calls=%fused_computation.3 | convolution fusion | flops 1081606144 | bytes 4194304 | tf_op jit(solution)/shard_map/dot_general | solution.py:291
  193.2 3.0 %collective-permute-start.34 = (bf16[128,1024]{1,0:T(8,128)(2,1)S(1)}, bf16[128,1024]{1,0:T(8,128)(2,1)S(1)}, u32[]{:S(2)}, u32[]{:S(2)}) collective-permute-start(bf16[128,1024]{1,0:T(8,128)(2,1)S(1)} %get-tuple-element.44), channel_id=1, source_target_pairs={{0,12},{4,0},{8,4},{12,8},{1,13},{5,1},{9,5},{13,9},{2,14},{6,2},{... | collective-permute-start | bytes 786440 | tf_op jit(solution)/shard_map/ppermute | solution.py:27
  196.1 1.3 convolution_convert_fusion.1
  197.6 3.2 %collective-permute-start.33 = (bf16[128,1024]{1,0:T(8,128)(2,1)S(1)}, bf16[128,1024]{1,0:T(8,128)(2,1)S(1)}, u32[]{:S(2)}, u32[]{:S(2)}) collective-permute-start(bf16[128,1024]{1,0:T(8,128)(2,1)S(1)} %get-tuple-element.40), channel_id=1, source_target_pairs={{0,12},{4,0},{8,4},{12,8},{1,13},{5,1},{9,5},{13,9},{2,14},{6,2},{... | collective-permute-start | bytes 786440 | tf_op jit(solution)/shard_map/ppermute | solution.py:27
  200.8 2.5 %collective-permute-done.30 = bf16[128,1024]{1,0:T(8,128)(2,1)S(1)} collective-permute-done((bf16[128,1024]{1,0:T(8,128)(2,1)S(1)}, bf16[128,1024]{1,0:T(8,128)(2,1)S(1)}, u32[]{:S(2)}, u32[]{:S(2)}) %collective-permute-start.30) | collective-permute-done | bytes 262176 | tf_op jit(solution)/shard_map/ppermute | solution.py:27
  204.2 2.7 %collective-permute-start.35 = (bf16[128,1024]{1,0:T(8,128)(2,1)S(1)}, bf16[128,1024]{1,0:T(8,128)(2,1)S(1)}, u32[]{:S(2)}, u32[]{:S(2)}) collective-permute-start(bf16[128,1024]{1,0:T(8,128)(2,1)S(1)} %get-tuple-element.42), channel_id=1, source_target_pairs={{0,12},{4,0},{8,4},{12,8},{1,13},{5,1},{9,5},{13,9},{2,14},{6,2},{... | collective-permute-start | bytes 786440 | tf_op jit(solution)/shard_map/ppermute | solution.py:27
  206.9 2.0 collective-permute-done.32
  208.9 4.7 %collective-permute-done.31 = bf16[128,1024]{1,0:T(8,128)(2,1)S(1)} collective-permute-done((bf16[128,1024]{1,0:T(8,128)(2,1)S(1)}, bf16[128,1024]{1,0:T(8,128)(2,1)S(1)}, u32[]{:S(2)}, u32[]{:S(2)}) %collective-permute-start.31) | collective-permute-done | bytes 262176 | tf_op jit(solution)/shard_map/ppermute | solution.py:27
  (118 shorter events, 12.1 us)
Async XLA Ops:
  6.5 90.4 %copy-start = (bf16[64,1024]{1,0:T(8,128)(2,1)S(1)}, bf16[64,1024]{1,0:T(8,128)(2,1)}, u32[]{:S(2)}) copy-start(bf16[64,1024]{1,0:T(8,128)(2,1)} %param.17) | copy-start | bytes 393220
  6.5 95.9 %all-gather.3.cloned.1.call-start = ((), (), s32[]{:S(2)}) async-start(), calls=%async_computation | async-start | bytes 7077888 | tf_op jit(solution)/shard_map/all_gather | solution.py:228
  8.9 25.3 %collective-permute-start = (bf16[352,512]{1,0:T(8,128)(2,1)S(1)}, bf16[352,512]{1,0:T(8,128)(2,1)S(1)}, u32[]{:S(2)}, u32[]{:S(2)}) collective-permute-start(bf16[352,512]{1,0:T(8,128)(2,1)S(1)} %pad_maximum_fusion.5), channel_id=1, source_target_pairs={{0,1},{1,2},{2,3},{3,0},{4,5},{5,6},{6,7},{7,4},{8,9},{9,10},{10,1... | collective-permute-start | bytes 1081352 | tf_op jit(solution)/shard_map/ppermute | solution.py:27
  12.3 22.0 %collective-permute-start.1 = (bf16[352,512]{1,0:T(8,128)(2,1)S(1)}, bf16[352,512]{1,0:T(8,128)(2,1)S(1)}, u32[]{:S(2)}, u32[]{:S(2)}) collective-permute-start(bf16[352,512]{1,0:T(8,128)(2,1)S(1)} %pad_maximum_fusion.6), channel_id=1, source_target_pairs={{0,3},{1,0},{2,1},{3,2},{4,7},{5,4},{6,5},{7,6},{8,11},{9,8},{10,9... | collective-permute-start | bytes 1081352 | tf_op jit(solution)/shard_map/ppermute | solution.py:27
  14.5 24.2 %collective-permute-start.12 = (bf16[48,1024]{1,0:T(8,128)(2,1)S(1)}, bf16[48,1024]{1,0:T(8,128)(2,1)S(1)}, u32[]{:S(2)}, u32[]{:S(2)}) collective-permute-start(bf16[48,1024]{1,0:T(8,128)(2,1)S(1)} %bitcast.54), channel_id=1, source_target_pairs={{0,2},{1,3},{2,0},{3,1},{4,6},{5,7},{6,4},{7,5},{8,10},{9,11},{10,... | collective-permute-start | bytes 294920 | tf_op jit(solution)/shard_map/ppermute | solution.py:27
  38.7 17.8 %collective-permute-start.13 = (bf16[48,4096]{1,0:T(8,128)(2,1)S(1)}, bf16[48,4096]{1,0:T(8,128)(2,1)S(1)}, u32[]{:S(2)}, u32[]{:S(2)}) collective-permute-start(bf16[48,4096]{1,0:T(8,128)(2,1)S(1)} %constant_dynamic-update-slice_fusion.2), channel_id=1, source_target_pairs={{0,32},{16,48},{32,0},{48,16},{64,96},{80,112},{96,64},{112,80},{1... | collective-permute-start | bytes 1179656 | tf_op jit(solution)/shard_map/ppermute | solution.py:218
  40.1 17.5 %copy-start.3 = (bf16[256,1024]{1,0:T(8,128)(2,1)}, bf16[256,1024]{1,0:T(8,128)(2,1)S(1)}, u32[]{:S(2)}) copy-start(bf16[256,1024]{1,0:T(8,128)(2,1)S(1)} %pad_maximum_fusion.1.refs_0_) | copy-start | bytes 1572868
  40.1 18.8 %collective-permute-start.10 = (bf16[256,1024]{1,0:T(8,128)(2,1)S(1)}, bf16[256,1024]{1,0:T(8,128)(2,1)}, u32[]{:S(2)}, u32[]{:S(2)}) collective-permute-start(bf16[256,1024]{1,0:T(8,128)(2,1)S(1)} %pad_maximum_fusion.1.refs_0_), channel_id=1, source_target_pairs={{0,4},{4,8},{8,12},{12,0},{1,5},{5,9},{9,13},{13,1},{2,6},{6,10},{... | collective-permute-start | bytes 1572872 | tf_op jit(solution)/shard_map/ppermute | solution.py:27
  41.7 17.1 %collective-permute-start.8 = (bf16[256,1024]{1,0:T(8,128)(2,1)S(1)}, bf16[256,1024]{1,0:T(8,128)(2,1)}, u32[]{:S(2)}, u32[]{:S(2)}) collective-permute-start(bf16[256,1024]{1,0:T(8,128)(2,1)S(1)} %pad_maximum_fusion.1.refs_0_), channel_id=1, source_target_pairs={{0,12},{4,0},{8,4},{12,8},{1,13},{5,1},{9,5},{13,9},{2,14},{6,2},{... | collective-permute-start | bytes 1572872 | tf_op jit(solution)/shard_map/ppermute | solution.py:27
  43.4 15.4 %collective-permute-start.2 = (bf16[256,512]{1,0:T(8,128)(2,1)S(1)}, bf16[256,512]{1,0:T(8,128)(2,1)S(1)}, u32[]{:S(2)}, u32[]{:S(2)}) collective-permute-start(bf16[256,512]{1,0:T(8,128)(2,1)S(1)} %get-tuple-element.54), channel_id=1, source_target_pairs={{0,3},{1,0},{2,1},{3,2},{4,7},{5,4},{6,5},{7,6},{8,11},{9,8},{10,9... | collective-permute-start | bytes 786440 | tf_op jit(solution)/shard_map/ppermute | solution.py:27
  45.1 13.7 %collective-permute-start.3 = (bf16[256,512]{1,0:T(8,128)(2,1)S(1)}, bf16[256,512]{1,0:T(8,128)(2,1)S(1)}, u32[]{:S(2)}, u32[]{:S(2)}) collective-permute-start(bf16[256,512]{1,0:T(8,128)(2,1)S(1)} %get-tuple-element.55), channel_id=1, source_target_pairs={{0,1},{1,2},{2,3},{3,0},{4,5},{5,6},{6,7},{7,4},{8,9},{9,10},{10,1... | collective-permute-start | bytes 786440 | tf_op jit(solution)/shard_map/ppermute | solution.py:27
  56.6 10.0 %copy-start.9 = (f32[3,3,256]{2,1,0:T(4,128)S(1)}, f32[3,3,256]{2,1,0:T(4,128)}, u32[]{:S(2)}) copy-start(f32[3,3,256]{2,1,0:T(4,128)} %param.14) | copy-start | bytes 27652
  56.6 10.1 %copy-start.5 = (f32[128,256]{1,0:T(8,128)S(1)}, f32[128,256]{1,0:T(8,128)}, u32[]{:S(2)}) copy-start(f32[128,256]{1,0:T(8,128)} %param.15) | copy-start | bytes 393220
  56.6 10.1 %copy-start.10 = (f32[256]{0:T(256)S(1)}, f32[256]{0:T(256)}, u32[]{:S(2)}) copy-start(f32[256]{0:T(256)} %param.16) | copy-start | bytes 3076
  58.9 128.4 %all-gather.5.cloned.1.call-start = ((), (), s32[]{:S(2)}) async-start(), calls=%async_computation.1 | async-start | bytes 2228224 | tf_op jit(solution)/shard_map/all_gather | solution.py:271
  59.1 39.4 %copy-start.8 = (bf16[256,1024]{1,0:T(8,128)(2,1)}, bf16[256,1024]{1,0:T(8,128)(2,1)S(1)}, u32[]{:S(2)}) copy-start(bf16[256,1024]{1,0:T(8,128)(2,1)S(1)} %constant_dynamic-update-slice_fusion.refs_1_) | copy-start | bytes 1572868
  59.1 17.8 %collective-permute-start.6 = (bf16[256,1024]{1,0:T(8,128)(2,1)S(1)}, bf16[256,1024]{1,0:T(8,128)(2,1)S(1)}, u32[]{:S(2)}, u32[]{:S(2)}) collective-permute-start(bf16[256,1024]{1,0:T(8,128)(2,1)S(1)} %constant_dynamic-update-slice_fusion.refs_1_), channel_id=1, source_target_pairs={{0,4},{4,8},{8,12},{12,0},{1,5},{5,9},{9,13},{13,1},{2,6},{6,10},{... | collective-permute-start | bytes 1572872 | tf_op jit(solution)/shard_map/ppermute | solution.py:27
  60.7 16.2 %collective-permute-start.7 = (bf16[256,1024]{1,0:T(8,128)(2,1)S(1)}, bf16[256,1024]{1,0:T(8,128)(2,1)}, u32[]{:S(2)}, u32[]{:S(2)}) collective-permute-start(bf16[256,1024]{1,0:T(8,128)(2,1)S(1)} %constant_dynamic-update-slice_fusion.refs_1_), channel_id=1, source_target_pairs={{0,12},{4,0},{8,4},{12,8},{1,13},{5,1},{9,5},{13,9},{2,14},{6,2},{... | collective-permute-start | bytes 1572872 | tf_op jit(solution)/shard_map/ppermute | solution.py:27
  62.4 13.8 %collective-permute-start.4 = (bf16[256,512]{1,0:T(8,128)(2,1)S(1)}, bf16[256,512]{1,0:T(8,128)(2,1)S(1)}, u32[]{:S(2)}, u32[]{:S(2)}) collective-permute-start(bf16[256,512]{1,0:T(8,128)(2,1)S(1)} %slice.184), channel_id=1, source_target_pairs={{0,1},{1,2},{2,3},{3,0},{4,5},{5,6},{6,7},{7,4},{8,9},{9,10},{10,1... | collective-permute-start | bytes 786440 | tf_op jit(solution)/shard_map/ppermute | solution.py:27
  64.8 12.1 %collective-permute-start.5 = (bf16[256,512]{1,0:T(8,128)(2,1)S(1)}, bf16[256,512]{1,0:T(8,128)(2,1)S(1)}, u32[]{:S(2)}, u32[]{:S(2)}) collective-permute-start(bf16[256,512]{1,0:T(8,128)(2,1)S(1)} %slice.187), channel_id=1, source_target_pairs={{0,3},{1,0},{2,1},{3,2},{4,7},{5,4},{6,5},{7,6},{8,11},{9,8},{10,9... | collective-permute-start | bytes 786440 | tf_op jit(solution)/shard_map/ppermute | solution.py:27
  76.9 25.5 %copy-start.4 = (bf16[256,1024]{1,0:T(8,128)(2,1)}, bf16[256,1024]{1,0:T(8,128)(2,1)S(1)}, u32[]{:S(2)}) copy-start(bf16[256,1024]{1,0:T(8,128)(2,1)S(1)} %pad_maximum_fusion.2.refs_2_) | copy-start | bytes 1572868
  77.0 16.1 %collective-permute-start.11 = (bf16[256,1024]{1,0:T(8,128)(2,1)S(1)}, bf16[256,1024]{1,0:T(8,128)(2,1)S(1)}, u32[]{:S(2)}, u32[]{:S(2)}) collective-permute-start(bf16[256,1024]{1,0:T(8,128)(2,1)S(1)} %pad_maximum_fusion.2.refs_2_), channel_id=1, source_target_pairs={{0,4},{4,8},{8,12},{12,0},{1,5},{5,9},{9,13},{13,1},{2,6},{6,10},{... | collective-permute-start | bytes 1572872 | tf_op jit(solution)/shard_map/ppermute | solution.py:27
  77.8 37.2 %collective-permute-start.14 = (bf16[256,1024]{1,0:T(8,128)(2,1)}, bf16[256,1024]{1,0:T(8,128)(2,1)}, u32[]{:S(2)}, u32[]{:S(2)}) collective-permute-start(bf16[256,1024]{1,0:T(8,128)(2,1)} %collective-permute-done.10.refs_6_), channel_id=1, source_target_pairs={{0,4},{4,8},{8,12},{12,0},{1,5},{5,9},{9,13},{13,1},{2,6},{6,10},{... | collective-permute-start | bytes 1572872 | tf_op jit(solution)/shard_map/ppermute | solution.py:27
  78.9 19.6 %collective-permute-start.9 = (bf16[256,1024]{1,0:T(8,128)(2,1)S(1)}, bf16[256,1024]{1,0:T(8,128)(2,1)S(1)}, u32[]{:S(2)}, u32[]{:S(2)}) collective-permute-start(bf16[256,1024]{1,0:T(8,128)(2,1)S(1)} %pad_maximum_fusion.2.refs_2_), channel_id=1, source_target_pairs={{0,12},{4,0},{8,4},{12,8},{1,13},{5,1},{9,5},{13,9},{2,14},{6,2},{... | collective-permute-start | bytes 1572872 | tf_op jit(solution)/shard_map/ppermute | solution.py:27
  81.6 17.5 %collective-permute-start.19 = (f32[144,128]{1,0:T(8,128)S(1)}, f32[144,128]{1,0:T(8,128)S(1)}, u32[]{:S(2)}, u32[]{:S(2)}) collective-permute-start(f32[144,128]{1,0:T(8,128)S(1)} %get-tuple-element.62), channel_id=1, source_target_pairs={{0,1},{1,2},{2,3},{3,0},{4,5},{5,6},{6,7},{7,4},{8,9},{9,10},{10,1... | collective-permute-start | bytes 221192 | tf_op jit(solution)/shard_map/ppermute | solution.py:27
  84.4 16.3 %collective-permute-start.20 = (f32[144,128]{1,0:T(8,128)S(1)}, f32[144,128]{1,0:T(8,128)S(1)}, u32[]{:S(2)}, u32[]{:S(2)}) collective-permute-start(f32[144,128]{1,0:T(8,128)S(1)} %get-tuple-element.61), channel_id=1, source_target_pairs={{0,3},{1,0},{2,1},{3,2},{4,7},{5,4},{6,5},{7,6},{8,11},{9,8},{10,9... | collective-permute-start | bytes 221192 | tf_op jit(solution)/shard_map/ppermute | solution.py:27
  93.1 9.3 %copy-start.6 = (bf16[256,1024]{1,0:T(8,128)(2,1)}, bf16[256,1024]{1,0:T(8,128)(2,1)S(1)}, u32[]{:S(2)}) copy-start(bf16[256,1024]{1,0:T(8,128)(2,1)S(1)} %collective-permute-done.11.refs_8_) | copy-start | bytes 1572868
  93.1 21.8 %collective-permute-start.21 = (f32[144,128]{1,0:T(8,128)S(1)}, f32[144,128]{1,0:T(8,128)S(1)}, u32[]{:S(2)}, u32[]{:S(2)}) collective-permute-start(f32[144,128]{1,0:T(8,128)S(1)} %get-tuple-element.60), channel_id=1, source_target_pairs={{0,2},{1,3},{2,0},{3,1},{4,6},{5,7},{6,4},{7,5},{8,10},{9,11},{10,... | collective-permute-start | bytes 221192 | tf_op jit(solution)/shard_map/ppermute | solution.py:27
  98.5 16.4 %collective-permute-start.15 = (bf16[256,1024]{1,0:T(8,128)(2,1)}, bf16[256,1024]{1,0:T(8,128)(2,1)}, u32[]{:S(2)}, u32[]{:S(2)}) collective-permute-start(bf16[256,1024]{1,0:T(8,128)(2,1)} %collective-permute-done.7.refs_4_), channel_id=1, source_target_pairs={{0,12},{4,0},{8,4},{12,8},{1,13},{5,1},{9,5},{13,9},{2,14},{6,2},{... | collective-permute-start | bytes 1572872 | tf_op jit(solution)/shard_map/ppermute | solution.py:27
  99.1 15.9 %collective-permute-start.16 = (bf16[256,512]{1,0:T(8,128)(2,1)S(1)}, bf16[256,512]{1,0:T(8,128)(2,1)S(1)}, u32[]{:S(2)}, u32[]{:S(2)}) collective-permute-start(bf16[256,512]{1,0:T(8,128)(2,1)S(1)} %slice.192), channel_id=1, source_target_pairs={{0,4},{4,8},{8,12},{12,0},{1,5},{5,9},{9,13},{13,1},{2,6},{6,10},{... | collective-permute-start | bytes 786440 | tf_op jit(solution)/shard_map/ppermute | solution.py:27
  100.7 14.2 %collective-permute-start.17 = (bf16[256,512]{1,0:T(8,128)(2,1)S(1)}, bf16[256,512]{1,0:T(8,128)(2,1)S(1)}, u32[]{:S(2)}, u32[]{:S(2)}) collective-permute-start(bf16[256,512]{1,0:T(8,128)(2,1)S(1)} %slice.193), channel_id=1, source_target_pairs={{0,12},{4,0},{8,4},{12,8},{1,13},{5,1},{9,5},{13,9},{2,14},{6,2},{... | collective-permute-start | bytes 786440 | tf_op jit(solution)/shard_map/ppermute | solution.py:27
  115.8 8.8 %copy-start.1 = (bf16[3,768,256]{2,1,0:T(8,128)(2,1)S(1)}, bf16[3,768,256]{2,1,0:T(8,128)(2,1)}, u32[]{:S(2)}) copy-start(bf16[3,768,256]{2,1,0:T(8,128)(2,1)} %project.2.near_ref) | copy-start | bytes 3538948
  124.9 10.3 %collective-permute-start.18 = (bf16[3,144,256]{2,1,0:T(8,128)(2,1)S(1)}, bf16[3,144,256]{2,1,0:T(8,128)(2,1)S(1)}, u32[]{:S(2)}, u32[]{:S(2)}) collective-permute-start(bf16[3,144,256]{2,1,0:T(8,128)(2,1)S(1)} %fusion.49.halo_ref), channel_id=1, source_target_pairs={{0,16},{16,32},{32,48},{48,64},{64,80},{80,96},{96,112},{112,128},... | collective-permute-start | bytes 663560 | tf_op jit(solution)/shard_map/ppermute | solution.py:275
  143.3 34.0 %collective-permute-start.26 = (bf16[512,256]{1,0:T(8,128)(2,1)S(1)}, bf16[512,256]{1,0:T(8,128)(2,1)S(1)}, u32[]{:S(2)}, u32[]{:S(2)}) collective-permute-start(bf16[512,256]{1,0:T(8,128)(2,1)S(1)} %pad_maximum_fusion.8), channel_id=1, source_target_pairs={{0,1},{1,2},{2,3},{3,0},{4,5},{5,6},{6,7},{7,4},{8,9},{9,10},{10,1... | collective-permute-start | bytes 786440 | tf_op jit(solution)/shard_map/ppermute | solution.py:27
  154.0 23.8 %collective-permute-start.27 = (bf16[512,256]{1,0:T(8,128)(2,1)S(1)}, bf16[512,256]{1,0:T(8,128)(2,1)S(1)}, u32[]{:S(2)}, u32[]{:S(2)}) collective-permute-start(bf16[512,256]{1,0:T(8,128)(2,1)S(1)} %pad_maximum_fusion.8), channel_id=1, source_target_pairs={{0,3},{1,0},{2,1},{3,2},{4,7},{5,4},{6,5},{7,6},{8,11},{9,8},{10,9... | collective-permute-start | bytes 786440 | tf_op jit(solution)/shard_map/ppermute | solution.py:27
  156.4 26.5 %collective-permute-start.22 = (bf16[512,256]{1,0:T(8,128)(2,1)S(1)}, bf16[512,256]{1,0:T(8,128)(2,1)S(1)}, u32[]{:S(2)}, u32[]{:S(2)}) collective-permute-start(bf16[512,256]{1,0:T(8,128)(2,1)S(1)} %pad_maximum_fusion.7), channel_id=1, source_target_pairs={{0,1},{1,2},{2,3},{3,0},{4,5},{5,6},{6,7},{7,4},{8,9},{9,10},{10,1... | collective-permute-start | bytes 786440 | tf_op jit(solution)/shard_map/ppermute | solution.py:27
  157.0 26.4 %collective-permute-start.23 = (bf16[512,256]{1,0:T(8,128)(2,1)S(1)}, bf16[512,256]{1,0:T(8,128)(2,1)S(1)}, u32[]{:S(2)}, u32[]{:S(2)}) collective-permute-start(bf16[512,256]{1,0:T(8,128)(2,1)S(1)} %pad_maximum_fusion.7), channel_id=1, source_target_pairs={{0,3},{1,0},{2,1},{3,2},{4,7},{5,4},{6,5},{7,6},{8,11},{9,8},{10,9... | collective-permute-start | bytes 786440 | tf_op jit(solution)/shard_map/ppermute | solution.py:27
  177.2 10.0 %collective-permute-start.28 = (bf16[256,256]{1,0:T(8,128)(2,1)S(1)}, bf16[256,256]{1,0:T(8,128)(2,1)S(1)}, u32[]{:S(2)}, u32[]{:S(2)}) collective-permute-start(bf16[256,256]{1,0:T(8,128)(2,1)S(1)} %slice.205), channel_id=1, source_target_pairs={{0,1},{1,2},{2,3},{3,0},{4,5},{5,6},{6,7},{7,4},{8,9},{9,10},{10,1... | collective-permute-start | bytes 393224 | tf_op jit(solution)/shard_map/ppermute | solution.py:27
  177.8 12.1 %collective-permute-start.29 = (bf16[256,256]{1,0:T(8,128)(2,1)S(1)}, bf16[256,256]{1,0:T(8,128)(2,1)S(1)}, u32[]{:S(2)}, u32[]{:S(2)}) collective-permute-start(bf16[256,256]{1,0:T(8,128)(2,1)S(1)} %slice.206), channel_id=1, source_target_pairs={{0,3},{1,0},{2,1},{3,2},{4,7},{5,4},{6,5},{7,6},{8,11},{9,8},{10,9... | collective-permute-start | bytes 393224 | tf_op jit(solution)/shard_map/ppermute | solution.py:27
  183.0 13.2 %collective-permute-start.24 = (bf16[256,256]{1,0:T(8,128)(2,1)S(1)}, bf16[256,256]{1,0:T(8,128)(2,1)S(1)}, u32[]{:S(2)}, u32[]{:S(2)}) collective-permute-start(bf16[256,256]{1,0:T(8,128)(2,1)S(1)} %slice.202), channel_id=1, source_target_pairs={{0,1},{1,2},{2,3},{3,0},{4,5},{5,6},{6,7},{7,4},{8,9},{9,10},{10,1... | collective-permute-start | bytes 393224 | tf_op jit(solution)/shard_map/ppermute | solution.py:27
  183.4 12.7 %collective-permute-start.25 = (bf16[256,256]{1,0:T(8,128)(2,1)S(1)}, bf16[256,256]{1,0:T(8,128)(2,1)S(1)}, u32[]{:S(2)}, u32[]{:S(2)}) collective-permute-start(bf16[256,256]{1,0:T(8,128)(2,1)S(1)} %slice.203), channel_id=1, source_target_pairs={{0,3},{1,0},{2,1},{3,2},{4,7},{5,4},{6,5},{7,6},{8,11},{9,8},{10,9... | collective-permute-start | bytes 393224 | tf_op jit(solution)/shard_map/ppermute | solution.py:27
  187.3 8.9 %copy-start.11 = (bf16[1024,1024]{1,0:T(8,128)(2,1)S(1)}, bf16[1024,1024]{1,0:T(8,128)(2,1)}, u32[]{:S(2)}) copy-start(bf16[1024,1024]{1,0:T(8,128)(2,1)} %all-gather.5.cloned.1.call-done) | copy-start | bytes 6291460
  192.8 10.4 %collective-permute-start.30 = (bf16[128,1024]{1,0:T(8,128)(2,1)S(1)}, bf16[128,1024]{1,0:T(8,128)(2,1)S(1)}, u32[]{:S(2)}, u32[]{:S(2)}) collective-permute-start(bf16[128,1024]{1,0:T(8,128)(2,1)S(1)} %get-tuple-element.45), channel_id=1, source_target_pairs={{0,4},{4,8},{8,12},{12,0},{1,5},{5,9},{9,13},{13,1},{2,6},{6,10},{... | collective-permute-start | bytes 786440 | tf_op jit(solution)/shard_map/ppermute | solution.py:27
  193.2 10.1 %collective-permute-start.34 = (bf16[128,1024]{1,0:T(8,128)(2,1)S(1)}, bf16[128,1024]{1,0:T(8,128)(2,1)S(1)}, u32[]{:S(2)}, u32[]{:S(2)}) collective-permute-start(bf16[128,1024]{1,0:T(8,128)(2,1)S(1)} %get-tuple-element.44), channel_id=1, source_target_pairs={{0,12},{4,0},{8,4},{12,8},{1,13},{5,1},{9,5},{13,9},{2,14},{6,2},{... | collective-permute-start | bytes 786440 | tf_op jit(solution)/shard_map/ppermute | solution.py:27
  197.5 11.4 %collective-permute-start.32 = (bf16[128,1024]{1,0:T(8,128)(2,1)S(1)}, bf16[128,1024]{1,0:T(8,128)(2,1)S(1)}, u32[]{:S(2)}, u32[]{:S(2)}) collective-permute-start(bf16[128,1024]{1,0:T(8,128)(2,1)S(1)} %get-tuple-element.41), channel_id=1, source_target_pairs={{0,4},{4,8},{8,12},{12,0},{1,5},{5,9},{9,13},{13,1},{2,6},{6,10},{... | collective-permute-start | bytes 786440 | tf_op jit(solution)/shard_map/ppermute | solution.py:27
  197.6 11.3 %collective-permute-start.33 = (bf16[128,1024]{1,0:T(8,128)(2,1)S(1)}, bf16[128,1024]{1,0:T(8,128)(2,1)S(1)}, u32[]{:S(2)}, u32[]{:S(2)}) collective-permute-start(bf16[128,1024]{1,0:T(8,128)(2,1)S(1)} %get-tuple-element.40), channel_id=1, source_target_pairs={{0,12},{4,0},{8,4},{12,8},{1,13},{5,1},{9,5},{13,9},{2,14},{6,2},{... | collective-permute-start | bytes 786440 | tf_op jit(solution)/shard_map/ppermute | solution.py:27
  203.5 10.1 %collective-permute-start.31 = (bf16[128,1024]{1,0:T(8,128)(2,1)S(1)}, bf16[128,1024]{1,0:T(8,128)(2,1)S(1)}, u32[]{:S(2)}, u32[]{:S(2)}) collective-permute-start(bf16[128,1024]{1,0:T(8,128)(2,1)S(1)} %get-tuple-element.43), channel_id=1, source_target_pairs={{0,4},{4,8},{8,12},{12,0},{1,5},{5,9},{9,13},{13,1},{2,6},{6,10},{... | collective-permute-start | bytes 786440 | tf_op jit(solution)/shard_map/ppermute | solution.py:27
  204.2 9.4 %collective-permute-start.35 = (bf16[128,1024]{1,0:T(8,128)(2,1)S(1)}, bf16[128,1024]{1,0:T(8,128)(2,1)S(1)}, u32[]{:S(2)}, u32[]{:S(2)}) collective-permute-start(bf16[128,1024]{1,0:T(8,128)(2,1)S(1)} %get-tuple-element.42), channel_id=1, source_target_pairs={{0,12},{4,0},{8,4},{12,8},{1,13},{5,1},{9,5},{13,9},{2,14},{6,2},{... | collective-permute-start | bytes 786440 | tf_op jit(solution)/shard_map/ppermute | solution.py:27
  (3 other events, 8.4 us)
Sparse Core Ops, SparseCore 0:
  59.0 42.2 all-gather.2
  103.2 36.7 all-gather.4
